TPU v7x, 32 devices: a whole 2x2x4 slice. The times are simulated.
32 devices in a mesh: sec: 2 (over y), dev: 16 (over z, x, core).
Axes of the slice: x: 2, y: 2, z: 4, core: 2. Of those that a mesh axis runs over, the one named last changes fastest.
Arguments:
- flow_state: float32 [5, 8, 1024, 512], P(None, None, ('sec', 'dev')), may hold values from -6 to 6
- diffusion: float32 [8, 1024, 512], P(None, ('sec', 'dev')), may hold values from 0.02 to 0.1
- wall_stress: float32 [2, 1024, 512], P(None, ('sec', 'dev')), may hold values from -3 to 3
- batch_counts: int32 [32, 48], P(('sec', 'dev')), may hold values from 1 to 4, 120 in all within a row
- batch_routes: int32 [1536, 1], P(('sec', 'dev')), may hold values from 0 to 31; in each aligned block of 48 rows (0 to 47, 48 to 95, ...) at most 2 rows name the same one
- wall_index: int32 [1536, 4], P(('sec', 'dev')), may hold values from 0 to 16383, as said below
- input_weight: bfloat16 [12, 2048], replicated, may hold values from -1.75 to 1.75
- middle_weight: bfloat16 [2048, 2048], P(('sec', 'dev')), may hold values from -0.125 to 0.125
- output_weight: bfloat16 [2, 2048], replicated, may hold values from -0.125 to 0.125
Outputs:
- new_field: float32 [5, 8, 1024, 512], P(None, None, ('sec', 'dev'))
- new_stress: float32 [2, 1024, 512], P(None, ('sec', 'dev'))
- batch_loss: float32 [32], P(('sec', 'dev'))
- grad_w_in: float32 [12, 2048], replicated
- grad_w_mid: float32 [2048, 2048], P(('sec', 'dev'))
Inputs may be any that keep to these rules, and one draw needn't show every extreme that they name: `batch_routes`: within the 48 rows of one device no trainer is named more than 2 times, and every trainer is named by some row. `batch_counts`: each device's row sums to 120. `wall_index`: all entries of the 48 rows of one device are distinct.
All inputs are finite; a program needn't handle non-finite values.
Results may differ from a plain program's by a relative error of at most 0.00091.
Values may be sent and summed in bfloat16 or wider, within the bound.
No kernel may reach another device: no remote copies, remote signals or barrier semaphores. Data moves between devices by JAX's collectives and lax.ppermute only.
A program may use at most 128 MiB of HBM per device.

v0:
```python
import math

import jax
import jax.numpy as jnp
from jax import lax
from jax.sharding import PartitionSpec as P

SLOTS = 2


advect_number = 0.3
wall_gain = 0.5
grad_number = 32.0


def extended(block, sides, width):
    for axis, dim in sides:
        count = lax.axis_size(axis)
        forward = [(i, i + 1) for i in range(count - 1)]
        forward.append((count - 1, 0))
        backward = [(target, source) for source, target in forward]
        low = lax.ppermute(
            lax.slice_in_dim(block, block.shape[dim] - width, None, axis=dim), axis, forward
        )
        high = lax.ppermute(lax.slice_in_dim(block, 0, width, axis=dim), axis, backward)
        block = jnp.concatenate([low, block, high], axis=dim)
    return block


def advance(flow_state, diffusion, below_z, above_z):
    below_x = jnp.concatenate([flow_state[..., :1], flow_state[..., :-1]], axis=3)
    above_x = jnp.concatenate([flow_state[..., 1:], flow_state[..., -1:]], axis=3)
    below_y = jnp.concatenate([flow_state[:, :1], flow_state[:, :-1]], axis=1)
    above_y = jnp.concatenate([flow_state[:, 1:], flow_state[:, -1:]], axis=1)
    spread = below_x + above_x + below_y + above_y + below_z + above_z - 6.0 * flow_state
    return flow_state + advect_number * (below_x - flow_state) + diffusion[None] * spread


def wall_columns(flow_state):
    points = flow_state.shape[2] * flow_state.shape[3]
    inputs = flow_state[0:4, 0:3].reshape(12, points)
    targets = jnp.stack(
        [flow_state[1, 4] - flow_state[1, 3], flow_state[3, 4] - flow_state[3, 3]]
    ).reshape(2, points)
    return jnp.concatenate([inputs, targets], axis=0).astype(jnp.bfloat16)


def apply_wall(advanced, new_stress):
    advanced = advanced.at[1, 0].add(-wall_gain * new_stress[0])
    return advanced.at[3, 0].add(-wall_gain * new_stress[1])


def contract_first(left, right):
    return lax.dot_general(
        left, right, (((0,), (0,)), ((), ())), preferred_element_type=jnp.float32
    )


def contract_last(left, right):
    return lax.dot_general(
        left, right, (((1,), (1,)), ((), ())), preferred_element_type=jnp.float32
    )


def body(
    flow_state,
    diffusion,
    wall_stress,
    batch_counts,
    batch_routes,
    wall_index,
    input_weight,
    middle_weight,
    output_weight,
):
    tile_count, capacity = wall_index.shape
    devices = lax.axis_size(("sec", "dev"))
    channels = 14
    slot_total = devices * SLOTS
    row_total = slot_total * capacity
    points = flow_state.shape[2] * flow_state.shape[3]
    columns = wall_columns(flow_state)
    picked = jnp.take(columns, wall_index.reshape(-1), axis=1).reshape(
        channels, tile_count, capacity
    )
    is_live = (
        jnp.arange(capacity, dtype=jnp.int32)[None, :] < batch_counts.reshape(tile_count)[:, None]
    )
    picked = jnp.where(is_live[None], picked, jnp.zeros((), jnp.bfloat16))
    destination = batch_routes.reshape(tile_count)
    matches = (destination[:, None] == jnp.arange(devices, dtype=jnp.int32)[None, :]).astype(
        jnp.int32
    )
    slot_rank = jnp.sum((jnp.cumsum(matches, axis=0) - matches) * matches, axis=1)
    slot_id = destination * SLOTS + slot_rank
    placing = (slot_id[:, None] == jnp.arange(slot_total, dtype=jnp.int32)[None, :]).astype(
        jnp.bfloat16
    )
    send_rows = jnp.einsum(
        "bs,cbk->sck", placing, picked, preferred_element_type=jnp.float32
    ).astype(jnp.bfloat16)
    send_rows = send_rows.reshape(devices, SLOTS, channels, capacity)
    send_live = jnp.einsum(
        "bs,bk->sk", placing, is_live.astype(jnp.bfloat16), preferred_element_type=jnp.float32
    ).astype(jnp.bfloat16)
    send_live = send_live.reshape(devices, SLOTS, capacity)
    got_rows, got_live = (
        lax.all_to_all(send_rows, ("sec", "dev"), split_axis=0, concat_axis=0, tiled=True),
        lax.all_to_all(send_live, ("sec", "dev"), split_axis=0, concat_axis=0, tiled=True),
    )
    sample_rows = jnp.transpose(got_rows, (0, 1, 3, 2)).reshape(row_total, channels)
    features = sample_rows[:, :12]
    targets = sample_rows[:, 12:].astype(jnp.float32)
    live_rows = got_live.reshape(row_total).astype(jnp.float32)
    pre_first = jnp.dot(features, input_weight, preferred_element_type=jnp.float32)
    first_tanh = jnp.tanh(pre_first)
    first_act = first_tanh.astype(jnp.bfloat16)
    part = first_act
    pre_second = jnp.dot(
        part,
        lax.all_gather(middle_weight, ("sec", "dev"), axis=0, tiled=True),
        preferred_element_type=jnp.float32,
    )
    second_tanh = jnp.tanh(pre_second)
    second_act = second_tanh.astype(jnp.bfloat16)
    prediction = contract_last(second_act, output_weight)
    errors = (prediction - targets) * live_rows[:, None]
    sent_back = jnp.transpose(
        prediction.astype(jnp.bfloat16).reshape(devices, SLOTS, capacity, 2), (0, 1, 3, 2)
    )
    answers = lax.all_to_all(sent_back, ("sec", "dev"), split_axis=0, concat_axis=0, tiled=True)
    answers = answers.reshape(slot_total, 2, capacity)
    live_total = jnp.sum(live_rows)
    batch_loss = (0.5 * jnp.sum(errors * errors) / live_total).reshape(1)
    live_dev = 5 * tile_count * capacity // 8
    scale = grad_number / math.sqrt(live_dev * devices)
    back_out = (errors * scale).astype(jnp.bfloat16)
    back_second = (
        jnp.dot(back_out, output_weight, preferred_element_type=jnp.float32)
        * (1.0 - second_tanh * second_tanh)
    ).astype(jnp.bfloat16)
    back_hidden = contract_last(
        back_second, lax.all_gather(middle_weight, ("sec", "dev"), axis=0, tiled=True)
    )
    back_first = (back_hidden * (1.0 - first_tanh * first_tanh)).astype(jnp.bfloat16)
    part = first_act
    grad_w_mid = lax.psum_scatter(
        contract_first(part, back_second), ("sec", "dev"), scatter_dimension=0, tiled=True
    )
    grad_w_in = lax.psum(contract_first(features, back_first), ("sec", "dev"))
    per_tile = jnp.einsum("bs,sck->cbk", placing, answers, preferred_element_type=jnp.float32)
    target_index = jnp.where(is_live, wall_index, points).reshape(-1)
    new_stress = (
        wall_stress.reshape(2, points)
        .at[:, target_index]
        .set(per_tile.reshape(2, -1), mode="drop")
        .reshape(wall_stress.shape)
    )
    padded = extended(flow_state.astype(jnp.bfloat16), ((("sec", "dev"), 2),), 1).astype(
        flow_state.dtype
    )
    advanced = advance(flow_state, diffusion, padded[:, :, :-2], padded[:, :, 2:])
    new_field = apply_wall(advanced, new_stress)
    return (new_field, new_stress, batch_loss, grad_w_in, grad_w_mid)


def solution(mesh):
    in_specs = (
        P(None, None, ("sec", "dev"), None),
        P(None, ("sec", "dev"), None),
        P(None, ("sec", "dev"), None),
        P(("sec", "dev"), None),
        P(("sec", "dev"), None),
        P(("sec", "dev"), None),
        P(),
        P(("sec", "dev"), None),
        P(),
    )
    out_specs = (
        P(None, None, ("sec", "dev"), None),
        P(None, ("sec", "dev"), None),
        P(("sec", "dev")),
        P(),
        P(("sec", "dev"), None),
    )
    return jax.shard_map(body, mesh=mesh, in_specs=in_specs, out_specs=out_specs, check_vma=False)
```

profile of v0, /device:TPU:11, one launch (start us, length us, event | category | flops | bytes accessed | tf_op | source)
XLA Modules:
  0.0 423.7 jit_solution(3434637611886213195)
XLA Ops:
  7.2 0.0 all-gather.2.cloned.1.call-start
  7.2 0.7 all-gather.2.cloned.1.call-update
  7.9 0.8 fusion.25
  8.7 0.1 reduce_window_sum.11
  8.8 0.8 select_reduce_fusion
  9.6 0.7 fusion.36
  10.3 0.8 convolution_convert_fusion.1
  11.2 0.7 copy.49
  11.9 6.3 %all-to-all-start.2 = ((bf16[32,2,4]{2,1,0:T(2,128)(2,1)}), bf16[32,2,4]{2,1,0:T(2,128)(2,1)S(1)}, u32[]{:S(2)}, u32[]{:S(2)}) async-start(bf16[32,2,4]{2,1,0:T(2,128)(2,1)} %bitcast.18), calls=%async_computation.2 | async-start | bytes 32768 | tf_op jit(solution)/shard_map/all_to_all | solution.py:109
  18.2 0.8 copy.37
  18.9 0.1 reshape.293
  19.0 2.0 convert_element_type.52
  21.1 0.1 copy.54
  21.2 0.1 copy.55
  21.2 1.0 copy-done.3
  22.3 0.3 copy.53
  22.6 0.2 pad_maximum_fusion.1
  22.9 3.4 copy.38
  26.2 3.4 gather_fusion
  29.7 0.1 copy.39
  29.8 0.2 convolution_convert_fusion
  30.0 0.1 copy.40
  30.1 0.7 copy.41
  30.8 5.8 %all-to-all-start = ((bf16[32,2,14,4]{2,1,3,0:T(2,128)(2,1)}), bf16[32,2,14,4]{2,1,3,0:T(2,128)(2,1)S(1)}, u32[]{:S(2)}, u32[]{:S(2)}) async-start(bf16[32,2,14,4]{2,1,3,0:T(2,128)(2,1)} %copy.41), calls=%async_computation | async-start | bytes 131072 | tf_op jit(solution)/shard_map/all_to_all | solution.py:108
  36.7 0.0 all-reduce.2.cloned.1.call-start
  36.7 0.1 reshape.302
  36.8 5.0 %all-to-all-done = bf16[32,2,14,4]{2,1,3,0:T(2,128)(2,1)S(1)} async-done(((bf16[32,2,14,4]{2,1,3,0:T(2,128)(2,1)}), bf16[32,2,14,4]{2,1,3,0:T(2,128)(2,1)S(1)}, u32[]{:S(2)}, u32[]{:S(2)}) %all-to-all-start) | async-done | bytes 7200 | tf_op jit(solution)/shard_map/all_to_all | solution.py:108
  41.8 0.1 slice.163
  41.9 0.1 copy.52
  42.0 1.8 convolution_tanh_fusion.1
  43.8 45.8 %all-gather.2.cloned.1.call-done = bf16[2048,2048]{1,0:T(8,128)(2,1)} async-done(((bf16[64,2048]{1,0:T(8,128)(2,1)}), bf16[2048,2048]{1,0:T(8,128)(2,1)}) %all-gather.2.cloned.1.call-update) | async-done | bytes 8388624 | tf_op jit(solution)/shard_map/all_gather | solution.py:121
  89.5 6.4 %convolution_tanh_fusion = f32[256,2048]{1,0:T(8,128)S(1)} fusion(bf16[2048,2048]{1,0:T(8,128)(2,1)} %all-gather.2.cloned.1.call-done, f32[256,2048]{1,0:T(8,128)} %convolution_tanh_fusion.1), kind=kOutput, calls=%fused_computation.8 | convolution fusion | flops 2148007936 | bytes 12582912 | tf_op jit(solution)/shard_map/dot_general | solution.py:119
  95.9 1.0 multiply_reduce_fusion
  96.9 1.5 fusion.8
  98.4 7.4 %fusion.9 = f32[12,2048]{1,0:T(8,128)} fusion(bf16[256,2048]{1,0:T(8,128)(2,1)} %fusion.8, bf16[2048,2048]{1,0:T(8,128)(2,1)} %all-gather.2.cloned.1.call-done, f32[256,2048]{1,0:T(8,128)} %convolution_tanh_fusion.1, bf16[256,14]{1,0:T(8,128)(2,1)S(1)} %bitcast.59), kind=kOutput, calls=%fused_computation.22 | convolution fusion | flops 2162163712 | bytes 11639808 | tf_op jit(solution)/shard_map/dot_general | solution.py:54
  105.8 0.0 reduce-scatter.2.cloned.1.call-start
  105.9 10.0 %fusion.13 = f32[2048,2048]{1,0:T(8,128)} fusion(bf16[256,2048]{1,0:T(8,128)(2,1)} %fusion.8, f32[256,2048]{1,0:T(8,128)} %convolution_tanh_fusion.1), kind=kOutput, calls=%fused_computation.30 | convolution fusion | flops 2148007936 | bytes 19922944 | tf_op jit(solution)/shard_map/dot_general | solution.py:54
  115.9 1.3 fusion.45
  117.1 0.9 collective-permute-start
  118.0 0.1 copy.36
  118.1 0.1 reshape.291
  118.3 4.6 %copy.35 = f32[2,32,512]{0,2,1:T(8,128)} copy(f32[2,32,512]{2,1,0:T(8,128)S(1)} %copy-done.5) | data formatting | bytes 262144 | tf_op args[2]
  122.9 0.9 fusion.44
  123.8 1.1 fusion.41
  124.9 2.8 fusion.43
  127.7 3.5 fusion.42
  131.2 0.6 convert_reduce_fusion
  131.8 3.4 maximum_convert_fusion
  135.2 0.1 reshape.296
  135.3 0.6 copy.43
  136.0 7.1 %all-to-all-start.1 = ((bf16[32,2,2,4]{3,1,2,0:T(2,128)(2,1)}), bf16[32,2,2,4]{3,1,2,0:T(2,128)(2,1)S(1)}, u32[]{:S(2)}, u32[]{:S(2)}) async-start(bf16[32,2,2,4]{3,1,2,0:T(2,128)(2,1)} %copy.43), calls=%async_computation.1 | async-start | bytes 65536 | tf_op jit(solution)/shard_map/all_to_all | solution.py:131
  143.1 9.2 %fusion.4 = f32[5,8,32,512]{3,2,1,0:T(8,128)} fusion(f32[5,8,34,512]{3,2,1,0:T(8,128)} %maximum_convert_fusion, f32[5,8,32,1]{3,2,1,0:T(8,128)} %get-tuple-element.49, f32[5,8,32,511]{3,2,1,0:T(8,128)} %get-tuple-element.51, f32[5,7,32,512]{3,2,1,0:T(8,128)} %get-tuple-element.53, f32[5,1,32,512]{3,2,1,0:T(8,128)} %get-tuple-element.55, ...), kind=kLoop, calls=%fused_computation.13 | loop fusion | flops 10485760 | bytes 21495808 | tf_op jit(solution)/shard_map/add | solution.py:36
  153.7 0.2 convolution_bitcast_fusion
  153.9 0.1 copy.46
  154.0 0.1 reshape.312
  154.1 0.1 copy.47
  154.2 7.6 %scatter_fusion = f32[2,16384]{0,1:T(8,128)} fusion(f32[2,16384]{0,1:T(8,128)} %bitcast.52, s32[192]{0:T(256)S(1)} %bitcast.68, f32[192,2]{1,0:T(8,128)S(1)} %copy.47), kind=kCustom, calls=%fused_computation.1 | custom fusion | bytes 5376 | tf_op jit(solution)/shard_map/scatter | solution.py:156
  161.8 5.9 %copy.50 = f32[2,32,512]{2,1,0:T(8,128)} copy(f32[2,32,512]{0,2,1:T(8,128)} %bitcast.53) | data formatting | bytes 262144
  167.7 12.3 %fusion = (f32[16384]{0:T(1024)S(1)}, f32[16384]{0:T(1024)S(1)}) fusion(f32[2,16384]{0,1:T(8,128)} %scatter_fusion), kind=kLoop, calls=%fused_computation.3 | loop fusion | flops 32768 | bytes 262144 | tf_op jit(solution)/shard_map/mul | solution.py:50
  180.0 1.5 fusion.17
  181.5 1.5 fusion.16
  183.0 43.9 %all-reduce.2.cloned.1.call-done = f32[12,2048]{1,0:T(8,128)} async-done(((f32[12,2048]{1,0:T(8,128)}), f32[12,2048]{1,0:T(8,128)}) %all-reduce.2.cloned.1.call-update) | async-done | bytes 98320 | tf_op jit(solution)/shard_map/psum | solution.py:150
  226.9 187.5 %reduce-scatter.2.cloned.1.call-done = f32[64,2048]{1,0:T(8,128)} async-done(((f32[2048,2048]{1,0:T(8,128)}), f32[64,2048]{1,0:T(8,128)}) %reduce-scatter.2.cloned.1.call-update) | async-done | bytes 524304 | tf_op jit(solution)/shard_map/reduce_scatter | solution.py:147
  414.4 1.6 copy.60
  (36 shorter events, 0.3 us)
Async XLA Ops:
  7.2 34.9 %copy-start = (bf16[12,2048]{1,0:T(8,128)(2,1)S(1)}, bf16[12,2048]{1,0:T(8,128)(2,1)}, u32[]{:S(2)}) copy-start(bf16[12,2048]{1,0:T(8,128)(2,1)} %param.19) | copy-start | bytes 147460
  7.2 13.9 %copy-start.2 = (f32[5,8,32,512]{3,2,1,0:T(8,128)S(1)}, f32[5,8,32,512]{3,2,1,0:T(8,128)}, u32[]{:S(2)}) copy-start(f32[5,8,32,512]{3,2,1,0:T(8,128)} %param.13) | copy-start | bytes 7864324
  7.2 82.3 %all-gather.2.cloned.1.call-start = ((), (), s32[]{:S(2)}) async-start(), calls=%async_computation.4 | async-start | bytes 8650752 | tf_op jit(solution)/shard_map/all_gather | solution.py:121
  11.9 19.0 %all-to-all-start.2 = ((bf16[32,2,4]{2,1,0:T(2,128)(2,1)}), bf16[32,2,4]{2,1,0:T(2,128)(2,1)S(1)}, u32[]{:S(2)}, u32[]{:S(2)}) async-start(bf16[32,2,4]{2,1,0:T(2,128)(2,1)} %bitcast.18), calls=%async_computation.2 | async-start | bytes 32768 | tf_op jit(solution)/shard_map/all_to_all | solution.py:109
  21.1 1.2 copy-start.3
  22.8 6.9 %copy-start.7 = (s32[48,4]{0,1:T(4,128)S(1)}, s32[48,4]{0,1:T(4,128)}, u32[]{:S(2)}) copy-start(s32[48,4]{0,1:T(4,128)} %param.18) | copy-start | bytes 2308
  22.8 6.9 %copy-start.8 = (s32[1,48]{1,0:T(1,128)S(1)}, s32[1,48]{1,0:T(1,128)}, u32[]{:S(2)}) copy-start(s32[1,48]{1,0:T(1,128)} %param.16) | copy-start | bytes 580
  30.8 11.0 %all-to-all-start = ((bf16[32,2,14,4]{2,1,3,0:T(2,128)(2,1)}), bf16[32,2,14,4]{2,1,3,0:T(2,128)(2,1)S(1)}, u32[]{:S(2)}, u32[]{:S(2)}) async-start(bf16[32,2,14,4]{2,1,3,0:T(2,128)(2,1)} %copy.41), calls=%async_computation | async-start | bytes 131072 | tf_op jit(solution)/shard_map/all_to_all | solution.py:108
  36.7 190.2 %all-reduce.2.cloned.1.call-start = ((), (), s32[]{:S(2)}) async-start(), calls=%async_computation.5 | async-start | bytes 262144 | tf_op jit(solution)/shard_map/psum | solution.py:150
  43.8 52.1 %copy-start.6 = (bf16[2,2048]{1,0:T(2,128)(2,1)S(1)}, bf16[2,2048]{1,0:T(2,128)(2,1)}, u32[]{:S(2)}) copy-start(bf16[2,2048]{1,0:T(2,128)(2,1)} %param.21) | copy-start | bytes 24580
  105.8 308.6 %reduce-scatter.2.cloned.1.call-start = ((), (), s32[]{:S(2)}) async-start(), calls=%async_computation.6 | async-start | bytes 17301504 | tf_op jit(solution)/shard_map/reduce_scatter | solution.py:147
  115.8 2.4 copy-start.5
  117.1 14.7 %collective-permute-start = (bf16[5,8,1,512]{3,2,1,0:T(2,128)(2,1)S(1)}, bf16[5,8,1,512]{3,2,1,0:T(2,128)(2,1)}, u32[]{:S(2)}, u32[]{:S(2)}) collective-permute-start(bf16[5,8,1,512]{3,2,1,0:T(2,128)(2,1)S(1)} %get-tuple-element.56), channel_id=1, source_target_pairs={{0,1},{1,2},{2,3},{3,4},{4,5},{5,6},{6,7},{7,8},{8,9},{9,10},{10,1... | collective-permute-start | bytes 122888 | tf_op jit(solution)/shard_map/ppermute | solution.py:22
  118.0 13.8 %collective-permute-start.1 = (bf16[5,8,1,512]{3,2,1,0:T(2,128)(2,1)S(1)}, bf16[5,8,1,512]{3,2,1,0:T(2,128)(2,1)}, u32[]{:S(2)}, u32[]{:S(2)}) collective-permute-start(bf16[5,8,1,512]{3,2,1,0:T(2,128)(2,1)S(1)} %get-tuple-element.57), channel_id=1, source_target_pairs={{1,0},{2,1},{3,2},{4,3},{5,4},{6,5},{7,6},{8,7},{9,8},{10,9},{11,1... | collective-permute-start | bytes 122888 | tf_op jit(solution)/shard_map/ppermute | solution.py:25
  127.7 4.1 copy-start.4
  136.0 17.7 %all-to-all-start.1 = ((bf16[32,2,2,4]{3,1,2,0:T(2,128)(2,1)}), bf16[32,2,2,4]{3,1,2,0:T(2,128)(2,1)S(1)}, u32[]{:S(2)}, u32[]{:S(2)}) async-start(bf16[32,2,2,4]{3,1,2,0:T(2,128)(2,1)} %copy.43), calls=%async_computation.1 | async-start | bytes 65536 | tf_op jit(solution)/shard_map/all_to_all | solution.py:131
  167.7 248.3 %copy-start.1 = (bf16[12,2048]{1,0:T(8,128)(2,1)S(1)}, bf16[12,2048]{1,0:T(8,128)(2,1)}, u32[]{:S(2)}) copy-start(bf16[12,2048]{1,0:T(8,128)(2,1)} %param.19) | copy-start | bytes 147460
Sparse Core Ops, SparseCore 0:
  10.8 78.6 all-gather.1
  105.9 120.9 all-reduce.1
  229.8 184.6 reduce-scatter.1
where the time goes:
time: 427 us; the launch traced here: 424 us
  waiting for transfers between devices  283 us (66%)
  local copies, waits for them, and re-layouts  41.7 us (10%)
  other arithmetic  33.2 us (8%)
  matrix products  29.2 us (7%)
  starting transfers between devices  20.3 us (5%)
  between operations  16.5 us (4%)
    reduce_scatter x1, waiting for transfers between devices, body(): lax.psum_scatter(contract_first(part, back_second), ('sec', 'dev'), scatt...  188 us
    all_gather x1, waiting for transfers between devices, body(): lax.all_gather(middle_weight, ('sec', 'dev'), axis=0, tiled=True)  45.8 us
    psum x1, waiting for transfers between devices, body(): grad_w_in = lax.psum(contract_first(features, back_first), ('sec', 'dev'))  43.9 us
    dot_general x2, matrix products, contract_first(): lax.dot_general(left, right, (((0,), (0,)), ((), ())), preferred_element_...  17.4 us
    unnamed x27, local copies, waits for them, and re-layouts  14.4 us
    mul x1, other arithmetic, apply_wall(): return advanced.at[3, 0].add(-wall_gain * new_stress[1])  12.3 us
    add x1, other arithmetic, advance(): flow_state + advect_number * (below_x - flow_state)  9.22 us
  transfers between devices with their start and end apart: 8, of which 4 were waited for; matrix products, arithmetic and copies ran while one was open for 20% of the time, Pallas kernels for 0%

commit v1 on v0

v1 whole, which is shorter than its diff:
```python
import functools
import math

import jax
import jax.numpy as jnp
from jax import lax
from jax.experimental import pallas as pl
from jax.experimental.pallas import tpu as pltpu
from jax.sharding import Mesh, PartitionSpec as P

CORES = 2
LANE = 128

advect_number = 0.3
wall_gain = 0.5
grad_number = 32.0

FEATURES = 12
CHANNELS = 14
ROWS = 16

CHIPS = ("sec", "chip")
EVERY = ("sec", "chip", "core")

NN = (((1,), (0,)), ((), ()))
NT = (((1,), (1,)), ((), ()))
TN = (((0,), (0,)), ((), ()))


def mm(left, right, dims=NN):
    return lax.dot_general(left, right, dims, preferred_element_type=jnp.float32)


def round_up(value, step):
    return -(-value // step) * step


def iota(shape, axis):
    return lax.broadcasted_iota(jnp.int32, shape, axis)


def params(mib, **more):
    return pltpu.CompilerParams(vmem_limit_bytes=mib << 20, **more)


def pick_kernel(counts_ref, routes_ref, index_ref, flow_ref, rows_ref, info_ref, *, nx, capacity):
    tiles = counts_ref.shape[1]
    nz = flow_ref.shape[2]
    lanes = rows_ref.shape[1]
    shift = nx.bit_length() - 1
    counts = counts_ref[...].astype(jnp.float32)
    row, col = iota((tiles, tiles), 0), iota((tiles, tiles), 1)
    wide = jnp.broadcast_to(counts, (tiles, tiles))
    before = jnp.sum(jnp.where(col < row, wide, 0.0), axis=1, keepdims=True)
    own = jnp.sum(jnp.where(col == row, wide, 0.0), axis=1, keepdims=True)
    place = iota((tiles, lanes), 1).astype(jnp.float32)
    index = index_ref[...].astype(jnp.float32)
    routes = routes_ref[...].astype(jnp.float32)
    point = jnp.full((1, lanes), -1.0, jnp.float32)
    route = jnp.full((1, lanes), -1.0, jnp.float32)
    for k in range(capacity):
        here = (place == before + k) & (own > k)
        point = point + jnp.sum(
            jnp.where(here, index[:, k : k + 1] + 1.0, 0.0), axis=0, keepdims=True
        )
        route = route + jnp.sum(jnp.where(here, routes + 1.0, 0.0), axis=0, keepdims=True)
    point = point.astype(jnp.int32)
    info_ref[...] = jnp.concatenate(
        [point, route.astype(jnp.int32), jnp.full((6, lanes), -1, jnp.int32)], axis=0
    )
    at_z = lax.shift_right_arithmetic(point, shift)
    at_x = jnp.where(point < 0, -1, point & (nx - 1))
    hot_x = jnp.where(iota((nx, lanes), 0) == at_x, 1.0, 0.0).astype(jnp.bfloat16)
    hot_z = iota((nz, lanes), 0) == at_z

    def select(plane):
        near = mm(plane.astype(jnp.bfloat16), hot_x)
        return jnp.sum(jnp.where(hot_z, near, 0.0), axis=0, keepdims=True)

    out = [select(flow_ref[v, l]) for v in range(4) for l in range(3)]
    out += [select(flow_ref[v, 4] - flow_ref[v, 3]) for v in (1, 3)]
    out.append(jnp.zeros((ROWS - CHANNELS, lanes), jnp.float32))
    rows_ref[...] = jnp.concatenate(out, axis=0).astype(jnp.bfloat16)


def pick_samples(counts, routes, index, flow, lanes):
    tiles, capacity = index.shape
    nz, nx = flow.shape[2:]
    assert nx & (nx - 1) == 0
    whole = lambda shape: pl.BlockSpec(shape, lambda i: (0,) * len(shape))
    return pl.pallas_call(
        functools.partial(pick_kernel, nx=nx, capacity=capacity),
        grid=(1,),
        in_specs=[
            whole((1, tiles)),
            whole((tiles, 1)),
            whole((tiles, capacity)),
            whole((4, 5, nz, nx)),
        ],
        out_specs=[whole((ROWS, lanes)), whole((8, lanes))],
        out_shape=[
            jax.ShapeDtypeStruct((ROWS, lanes), jnp.bfloat16),
            jax.ShapeDtypeStruct((8, lanes), jnp.int32),
        ],
        compiler_params=params(32),
        name="pick",
    )(counts, routes, index, flow)


def assemble(core_ref, mine_ref, other_ref, weight_ref):
    core = core_ref[0]
    chips, rows, _ = mine_ref.shape
    for j in range(chips):
        at = pl.multiple_of((2 * j + core) * rows, rows)
        weight_ref[pl.ds(at, rows), :] = mine_ref[j]
        at = pl.multiple_of((2 * j + 1 - core) * rows, rows)
        weight_ref[pl.ds(at, rows), :] = other_ref[j]


def features_of(rows_ref):
    parts = [rows_ref[i] for i in range(rows_ref.shape[0])]
    across = parts[0] if len(parts) == 1 else jnp.concatenate(parts, axis=1)
    across = across.astype(jnp.float32)
    features = jnp.where(iota(across.shape, 0) < FEATURES, across, 0.0)
    return across, features


def forward_kernel(core_ref, rows_ref, mine_ref, other_ref, win_ref, wout_ref, second_ref, pred_ref, weight_ref, *, step):
    @pl.when(pl.program_id(0) == 0)
    def _():
        assemble(core_ref, mine_ref, other_ref, weight_ref)

    hidden = weight_ref.shape[0]
    _, features = features_of(rows_ref)
    tall = features.T.astype(jnp.bfloat16)
    total = None
    for at in range(0, hidden, step):
        first = jnp.tanh(mm(tall, win_ref[:, at : at + step])).astype(jnp.bfloat16)
        term = mm(first, weight_ref[at : at + step, :])
        total = term if total is None else total + term
    second = jnp.tanh(total).T
    second_ref[...] = second
    pred_ref[...] = mm(wout_ref[...], second.astype(jnp.bfloat16))


def forward(core, rows, mine, other, win, wout, group):
    chips, rows_dev, width = mine.shape
    lanes = rows.shape[2]
    hidden = win.shape[1]
    tile = group * lanes
    return pl.pallas_call(
        functools.partial(forward_kernel, step=min(hidden, 512)),
        grid=(chips // group,),
        in_specs=[
            pl.BlockSpec(memory_space=pltpu.SMEM),
            pl.BlockSpec((group, ROWS, lanes), lambda i: (i, 0, 0)),
            pl.BlockSpec(mine.shape, lambda i: (0, 0, 0)),
            pl.BlockSpec(other.shape, lambda i: (0, 0, 0)),
            pl.BlockSpec(win.shape, lambda i: (0, 0)),
            pl.BlockSpec(wout.shape, lambda i: (0, 0)),
        ],
        out_specs=[
            pl.BlockSpec((width, tile), lambda i: (0, i)),
            pl.BlockSpec((wout.shape[0], tile), lambda i: (0, i)),
        ],
        out_shape=[
            jax.ShapeDtypeStruct((width, chips * lanes), jnp.float32),
            jax.ShapeDtypeStruct((wout.shape[0], chips * lanes), jnp.float32),
        ],
        scratch_shapes=[pltpu.VMEM((hidden, width), jnp.bfloat16)],
        compiler_params=params(48),
        name="forward",
    )(core, rows, mine, other, win, wout)


def backward_kernel(
    core_ref, rows_ref, mine_ref, other_ref, win_ref, wout_ref, second_ref, pred_ref,
    keep_ref, send_ref, gin_ref, weight_ref, grad_ref, *, step, live, lanes, scale,
):
    i = pl.program_id(0)

    @pl.when(i == 0)
    def _():
        assemble(core_ref, mine_ref, other_ref, weight_ref)
        grad_ref[...] = jnp.zeros_like(grad_ref)
        gin_ref[...] = jnp.zeros_like(gin_ref)

    hidden = weight_ref.shape[0]
    across, features = features_of(rows_ref)
    tile = across.shape[1]
    counted = (iota((1, tile), 1) & (lanes - 1)) < live
    errors = jnp.where(counted, pred_ref[...] - across[FEATURES:CHANNELS], 0.0)
    back_out = (errors * scale).astype(jnp.bfloat16)
    second = second_ref[...]
    back = mm(wout_ref[...], back_out, TN) * (1.0 - second * second)
    across_back = back.astype(jnp.bfloat16)
    tall_back = back.T.astype(jnp.bfloat16)
    wide = features.astype(jnp.bfloat16)
    tall = features.T.astype(jnp.bfloat16)
    for at in range(0, hidden, step):
        act = jnp.tanh(mm(tall, win_ref[:, at : at + step]))
        grad_ref[:, at : at + step] += mm(across_back, act.astype(jnp.bfloat16))
        back_hidden = mm(tall_back, weight_ref[at : at + step, :], NT)
        back_first = (back_hidden * (1.0 - act * act)).astype(jnp.bfloat16)
        gin_ref[:, at : at + step] += mm(wide, back_first)

    @pl.when(i == pl.num_programs(0) - 1)
    def _():
        core = core_ref[0]
        chips, rows, _ = keep_ref.shape
        for j in range(chips):
            pair = grad_ref[:, 2 * j * rows : 2 * (j + 1) * rows].T
            low, high = pair[:rows], pair[rows:]
            keep_ref[j] = jnp.where(core == 0, low, high)
            send_ref[j] = jnp.where(core == 0, high, low)


def backward(core, rows, mine, other, win, wout, second, pred, group, live, scale):
    chips, rows_dev, width = mine.shape
    lanes = rows.shape[2]
    hidden = win.shape[1]
    tile = group * lanes
    assert lanes & (lanes - 1) == 0
    out3 = pl.BlockSpec(mine.shape, lambda i: (0, 0, 0))
    return pl.pallas_call(
        functools.partial(
            backward_kernel, step=min(hidden, 512), live=live, lanes=lanes, scale=scale
        ),
        grid=(chips // group,),
        in_specs=[
            pl.BlockSpec(memory_space=pltpu.SMEM),
            pl.BlockSpec((group, ROWS, lanes), lambda i: (i, 0, 0)),
            pl.BlockSpec(mine.shape, lambda i: (0, 0, 0)),
            pl.BlockSpec(other.shape, lambda i: (0, 0, 0)),
            pl.BlockSpec(win.shape, lambda i: (0, 0)),
            pl.BlockSpec(wout.shape, lambda i: (0, 0)),
            pl.BlockSpec((width, tile), lambda i: (0, i)),
            pl.BlockSpec((wout.shape[0], tile), lambda i: (0, i)),
        ],
        out_specs=[out3, out3, pl.BlockSpec((ROWS, hidden), lambda i: (0, 0))],
        out_shape=[
            jax.ShapeDtypeStruct(mine.shape, jnp.float32),
            jax.ShapeDtypeStruct(mine.shape, jnp.float32),
            jax.ShapeDtypeStruct((ROWS, hidden), jnp.float32),
        ],
        scratch_shapes=[
            pltpu.VMEM((hidden, width), jnp.bfloat16),
            pltpu.VMEM((width, hidden), jnp.float32),
        ],
        compiler_params=params(56),
        name="backward",
    )(core, rows, mine, other, win, wout, second, pred)


def slab_kernel(flow_ref, diff_ref, below_ref, above_ref, out_ref):
    layers, nz, nx = flow_ref.shape[1:]
    at_z, at_x = iota((nz, nx), 0), iota((nz, nx), 1)
    first_z, last_z = at_z == 0, at_z == nz - 1
    first_x, last_x = at_x == 0, at_x == nx - 1
    below_edge = below_ref[0].astype(jnp.float32)
    above_edge = above_ref[0].astype(jnp.float32)
    for l in range(layers):
        mid = flow_ref[0, l]
        below_x = jnp.where(first_x, mid, pltpu.roll(mid, 1, 1))
        above_x = jnp.where(last_x, mid, pltpu.roll(mid, nx - 1, 1))
        below_z = jnp.where(first_z, below_edge[l : l + 1], pltpu.roll(mid, 1, 0))
        above_z = jnp.where(last_z, above_edge[l : l + 1], pltpu.roll(mid, nz - 1, 0))
        below_y = flow_ref[0, max(l - 1, 0)]
        above_y = flow_ref[0, min(l + 1, layers - 1)]
        spread = below_x + above_x + below_y + above_y + below_z + above_z - 6.0 * mid
        out_ref[0, l] = mid + advect_number * (below_x - mid) + diff_ref[l] * spread


def slab(flow, diff, below, above):
    vars_, layers, nz, nx = flow.shape
    block = pl.BlockSpec((1, layers, nz, nx), lambda v: (v, 0, 0, 0))
    edge = pl.BlockSpec((1, layers, nx), lambda v: (v, 0, 0))
    return pl.pallas_call(
        slab_kernel,
        grid=(vars_,),
        in_specs=[block, pl.BlockSpec((layers, nz, nx), lambda v: (0, 0, 0)), edge, edge],
        out_specs=block,
        out_shape=jax.ShapeDtypeStruct(flow.shape, flow.dtype),
        compiler_params=params(32),
        name="slab",
    )(flow, diff, below, above)


def wall_kernel(info_ref, pred_ref, stress_ref, field_ref, stress_out, field_out):
    nz, nx = stress_ref.shape[1:]
    lanes = info_ref.shape[1]
    shift = nx.bit_length() - 1
    point = info_ref[0:1, :]
    at_z = lax.shift_right_arithmetic(point, shift)
    at_x = jnp.where(point < 0, -1, point & (nx - 1))
    hot_x = jnp.where(iota((nx, lanes), 0) == at_x, 1.0, 0.0).astype(jnp.bfloat16)
    hot_z = jnp.where(iota((nz, lanes), 0) == at_z, 1.0, 0.0)
    mask = jnp.broadcast_to(point >= 0, hot_z.shape)
    hit = mm(hot_z.astype(jnp.bfloat16), hot_x, NT)
    sent = jnp.where(pl.program_id(0) == 0, pred_ref[0:1, :], pred_ref[1:2, :])
    put = jnp.where(mask, hot_z * sent, 0.0).astype(jnp.bfloat16)
    fresh = jnp.where(hit > 0.5, mm(put, hot_x, NT), stress_ref[0])
    stress_out[0] = fresh
    field_out[0, 0] = field_ref[0, 0] - wall_gain * fresh


def wall(info, pred, stress, field):
    nz, nx = stress.shape[1:]
    lanes = info.shape[1]
    plane = pl.BlockSpec((1, nz, nx), lambda i: (i, 0, 0))
    layer = pl.BlockSpec((1, 1, nz, nx), lambda i: (2 * i + 1, 0, 0, 0))
    return pl.pallas_call(
        wall_kernel,
        grid=(2,),
        in_specs=[
            pl.BlockSpec((8, lanes), lambda i: (0, 0)),
            pl.BlockSpec((2, lanes), lambda i: (0, 0)),
            plane,
            layer,
        ],
        out_specs=[plane, layer],
        out_shape=[
            jax.ShapeDtypeStruct(stress.shape, stress.dtype),
            jax.ShapeDtypeStruct(field.shape, field.dtype),
        ],
        input_output_aliases={3: 1},
        compiler_params=params(16),
        name="wall",
    )(info, pred, stress, field)


def swap_cores(block):
    return lax.ppermute(block, "core", [(0, 1), (1, 0)])


def flip(block, mask, chips):
    return lax.ppermute(block, CHIPS, [(i, i ^ mask) for i in range(chips)])


def sum_chips(block, chips):
    mask = 1
    while mask < chips:
        if 2 * mask < chips:
            one, two, three = (flip(block, k * mask, chips) for k in (1, 2, 3))
            block = (block + one) + (two + three)
        else:
            block = block + flip(block, mask, chips)
        mask *= 4
    return block


def exchange(blocks):
    return lax.all_to_all(blocks, CHIPS, split_axis=0, concat_axis=0, tiled=True)


def body(
    flow_state,
    diffusion,
    wall_stress,
    batch_counts,
    batch_routes,
    wall_index,
    input_weight,
    middle_weight,
    output_weight,
):
    tile_count, capacity = wall_index.shape
    chips = lax.axis_size(CHIPS)
    devices = chips * CORES
    assert chips & (chips - 1) == 0
    chip, core = lax.axis_index(CHIPS), lax.axis_index("core")
    rows_dev, hidden = middle_weight.shape
    width = hidden // chips
    live_dev = 5 * tile_count * capacity // 8
    lanes = LANE
    while lanes < live_dev:
        lanes *= 2
    group = max(1, 512 // lanes)
    scale = grad_number / math.sqrt(live_dev * devices)

    order = [(i, (i + 1) % devices) for i in range(devices)]
    back_order = [(b, a) for a, b in order]
    edges = flow_state.astype(jnp.bfloat16)
    below = lax.ppermute(edges[:, :, -1], EVERY, order)
    above = lax.ppermute(edges[:, :, 0], EVERY, back_order)

    own_rows, info = pick_samples(batch_counts, batch_routes, wall_index, flow_state, lanes)
    blocks = jnp.transpose(middle_weight.reshape(rows_dev, chips, width), (1, 0, 2))
    if lanes == width:
        shared = jnp.broadcast_to(own_rows[None], (chips, ROWS, lanes))
        got = exchange(jnp.concatenate([blocks, shared], axis=1))
        mine, rows = got[:, :rows_dev], got[:, rows_dev:]
    else:
        mine = exchange(blocks)
        rows = exchange(jnp.broadcast_to(own_rows[None], (chips, ROWS, lanes)))
    other = swap_cores(mine)

    win = jnp.pad(input_weight, ((0, ROWS - FEATURES), (0, 0)))
    wout = lax.dynamic_slice_in_dim(output_weight, chip * width, width, axis=1)
    core_word = core.astype(jnp.int32).reshape(1)
    second, part = forward(core_word, rows, mine, other, win, wout, group)
    pred = sum_chips(part, chips)

    keep, send, grad_in = backward(
        core_word, rows, mine, other, win, wout, second, pred, group, live_dev, scale
    )
    grad = exchange(keep + swap_cores(send))
    grad_w_mid = jnp.transpose(grad, (1, 0, 2)).reshape(rows_dev, hidden)

    own_pred = lax.dynamic_slice_in_dim(pred, chip * lanes, lanes, axis=1)
    errors = own_pred - own_rows[FEATURES:CHANNELS].astype(jnp.float32)
    squares = 0.5 * jnp.sum(errors * errors, axis=0)
    match = info[1][:, None] == jnp.arange(devices, dtype=jnp.int32)[None, :]
    loss = jnp.sum(jnp.where(match, squares[:, None], 0.0), axis=0)
    count = jnp.sum(match.astype(jnp.float32), axis=0)
    tail = jnp.pad(jnp.stack([loss, count]), ((0, ROWS - CHANNELS), (0, hidden - devices)))
    packed = jnp.concatenate([grad_in[:FEATURES], tail], axis=0)
    packed = packed + swap_cores(packed)
    packed = sum_chips(packed, chips)
    grad_w_in = packed[:FEATURES]
    mine_at = chip * CORES + core
    sums = lax.dynamic_slice(packed, (FEATURES, mine_at), (2, 1))
    batch_loss = sums[0] / sums[1]

    field = slab(flow_state, diffusion, below, above)
    new_stress, new_field = wall(info, own_pred, wall_stress, field)
    return (new_field, new_stress, batch_loss, grad_w_in, grad_w_mid)


def solution(mesh):
    sec, dev = mesh.shape["sec"], mesh.shape["dev"]
    inner = Mesh(mesh.devices.reshape(sec, dev // CORES, CORES), EVERY)
    in_specs = (
        P(None, None, EVERY, None),
        P(None, EVERY, None),
        P(None, EVERY, None),
        P(EVERY, None),
        P(EVERY, None),
        P(EVERY, None),
        P(),
        P(EVERY, None),
        P(),
    )
    out_specs = (
        P(None, None, EVERY, None),
        P(None, EVERY, None),
        P(EVERY),
        P(),
        P(EVERY, None),
    )
    return jax.shard_map(body, mesh=inner, in_specs=in_specs, out_specs=out_specs, check_vma=False)
```

time: 427 us -> 114 us (0.27)
  waiting for transfers between devices: 283 us -> 21 us
  matrix products: 29.2 us -> 0 us
  other arithmetic: 33.2 us -> 6.54 us
  local copies, waits for them, and re-layouts: 41.7 us -> 15.1 us
  Pallas kernels: 0 us -> 26.1 us
  blocking collectives: 0 us -> 14.5 us
  between operations: 16.5 us -> 3.31 us
  starting transfers between devices: 20.3 us -> 26.8 us
    reduce_scatter x1 -> x0, waiting for transfers between devices: 188 us -> none  [body(): lax.psum_scatter(contract_first(part, back_second), ('sec', 'dev'), scatt...]
    all_gather x1 -> x0, waiting for transfers between devices: 45.8 us -> none  [body(): lax.all_gather(middle_weight, ('sec', 'dev'), axis=0, tiled=True)]
    psum x1 -> x0, waiting for transfers between devices: 43.9 us -> none  [body(): grad_w_in = lax.psum(contract_first(features, back_first), ('sec', 'dev'))]
    dot_general x9 -> x0, matrix products: 29.2 us -> none  [the longest x2 17.4 us: contract_first(): lax.dot_general(left, right, (((0,), (0,)), ((), ())), preferred_element_...]
    pallas_call x0 -> x5, Pallas kernels: none -> 26.1 us  [the longest x1 13.1 us: backward(): pl.pallas_call(functools.partial(backward_kernel, step=min(hidden, 512),...]
    ppermute x2 -> x17, starting transfers between devices: 0.91 us -> 22 us  [the longest x12 12.5 us: flip(): return lax.ppermute(block, CHIPS, [(i, i ^ mask) for i in range(chips)])]
    ppermute x2 -> x17, waiting for transfers between devices: 0.01 us -> 21 us  [the longest x1 14.8 us: body(): above = lax.ppermute(edges[:, :, 0], EVERY, back_order)]
    all_to_all x0 -> x1, blocking collectives: none -> 14.5 us  [exchange(): lax.all_to_all(blocks, CHIPS, split_axis=0, concat_axis=0, tiled=True)]
  transfers between devices with their start and end apart: 8 -> 18, of which waited for: 4 -> 7; matrix products, arithmetic and copies ran while one was open for 20% -> 11% of each run, Pallas kernels for 0% -> 5%
where the time goes in v1:
time: 114 us; the launch traced here: 113 us
  starting transfers between devices  26.8 us (24%)
  Pallas kernels  26.1 us (23%)
  waiting for transfers between devices  21 us (18%)
  local copies, waits for them, and re-layouts  15.1 us (13%)
  blocking collectives  14.5 us (13%)
  other arithmetic  6.54 us (6%)
  between operations  3.31 us (3%)
    ppermute x1, waiting for transfers between devices, body(): above = lax.ppermute(edges[:, :, 0], EVERY, back_order)  14.8 us
    all_to_all x1, blocking collectives, exchange(): lax.all_to_all(blocks, CHIPS, split_axis=0, concat_axis=0, tiled=True)  14.5 us
    pallas_call x1, Pallas kernels, backward(): pl.pallas_call(functools.partial(backward_kernel, step=min(hidden, 512),...  13.1 us
    ppermute x12, starting transfers between devices, flip(): return lax.ppermute(block, CHIPS, [(i, i ^ mask) for i in range(chips)])  12.5 us
    unnamed x33, local copies, waits for them, and re-layouts  7.8 us
    pallas_call x1, Pallas kernels, forward(): pl.pallas_call(functools.partial(forward_kernel, step=min(hidden, 512)),...  6.86 us
    ppermute x3, starting transfers between devices, swap_cores(): return lax.ppermute(block, 'core', [(0, 1), (1, 0)])  5.89 us
    ppermute x12, waiting for transfers between devices, flip(): return lax.ppermute(block, CHIPS, [(i, i ^ mask) for i in range(chips)])  5.25 us
  transfers between devices with their start and end apart: 18, of which 7 were waited for; matrix products, arithmetic and copies ran while one was open for 11% of the time, Pallas kernels for 5%

profile of v1, /device:TPU:11, one launch (start us, length us, event | category | flops | bytes accessed | tf_op | source)
XLA Modules:
  0.0 113.3 jit_solution(2041761858829682493)
XLA Ops:
  0.6 0.0 copy-start
  0.6 0.8 copy.23.routes_ref
  1.4 0.8 copy.24.index_ref
  2.2 0.1 bitcast_bitcast_fusion
  2.3 0.0 copy-start.1
  2.3 1.7 %copy-done.1 = f32[5,8,32,512]{3,2,1,0:T(8,128)S(1)} copy-done((f32[5,8,32,512]{3,2,1,0:T(8,128)S(1)}, f32[5,8,32,512]{3,2,1,0:T(8,128)}, u32[]{:S(2)}) %copy-start.1) | copy-done | bytes 2621464
  4.0 0.7 copy-done.11
  4.7 0.5 pick.1
  5.2 0.0 copy-start.2
  5.3 14.5 %all_to_all.10 = bf16[16,80,128]{2,1,0:T(8,128)(2,1)} all-to-all(bf16[16,80,128]{2,1,0:T(8,128)(2,1)S(1)} %pad_maximum_fusion), channel_id=1, replica_groups=mesh['sec'=2,'chip'=8,'core'=2] {'sec','chip'}, dimensions={0} | all-to-all | bytes 655360 | tf_op jit(solution)/shard_map/all_to_all | solution.py:353
  19.8 1.0 slice.41.mine_ref
  20.8 2.7 %collective-permute-start = (bf16[16,64,128]{2,1,0:T(8,128)(2,1)S(1)}, bf16[16,64,128]{2,1,0:T(8,128)(2,1)S(1)}, u32[]{:S(2)}, u32[]{:S(2)}) collective-permute-start(bf16[16,64,128]{2,1,0:T(8,128)(2,1)S(1)} %slice.41.mine_ref), channel_id=1, source_target_pairs={{0,1},{1,0},{2,3},{3,2},{4,5},{5,4},{6,7},{7,6},{8,9},{9,8},{10,11... | collective-permute-start | bytes 786440 | tf_op jit(solution)/shard_map/ppermute | solution.py:333
  23.5 0.8 pad.8.win_ref
  24.4 0.7 constant_dynamic-slice_fusion.2.wout_ref
  25.0 0.8 slice.40.rows_ref
  25.9 0.0 collective-permute-done.other_ref
  25.9 6.9 %forward.1 = (f32[128,2048]{1,0:T(8,128)S(1)}, f32[2,2048]{1,0:T(2,128)S(1)}) custom-call(s32[1]{0:T(128)} %bitcast.core_ref, bf16[16,16,128]{2,1,0:T(8,128)(2,1)S(1)} %slice.40.rows_ref, bf16[16,64,128]{2,1,0:T(8,128)(2,1)S(1)} %slice.41.mine_ref, bf16[16,64,128]{2,1,0:T(8,128)(2,1)S(1)} %collective-permute-done.other_ref, ...), custom_call_target="tpu_custom_call" | custom-call | tf_op jit(solution)/shard_map/forward/pallas_call | solution.py:151
  32.8 1.0 copy-done.4
  33.7 1.9 %collective-permute-start.3 = (f32[2,2048]{1,0:T(2,128)S(1)}, f32[2,2048]{1,0:T(2,128)S(1)}, u32[]{:S(2)}, u32[]{:S(2)}) collective-permute-start(f32[2,2048]{1,0:T(2,128)S(1)} %get-tuple-element.16), channel_id=1, source_target_pairs={{0,6},{2,4},{4,2},{6,0},{8,14},{10,12},{12,10},{14,8},{16,22},{18,... | collective-permute-start | bytes 49160 | tf_op jit(solution)/shard_map/ppermute | solution.py:337
  35.6 0.5 collective-permute-start.2
  36.1 0.3 collective-permute-start.1
  36.4 0.8 collective-permute-done.3
  37.2 1.0 collective-permute-done.2
  38.2 0.5 collective-permute-done.1
  38.7 1.5 %collective-permute-start.6 = (f32[2,2048]{1,0:T(2,128)S(1)}, f32[2,2048]{1,0:T(2,128)S(1)}, u32[]{:S(2)}, u32[]{:S(2)}) collective-permute-start(f32[2,2048]{1,0:T(2,128)S(1)} %add_add_fusion.3), channel_id=1, source_target_pairs={{0,24},{2,26},{4,28},{6,30},{8,16},{10,18},{12,20},{14,22},{16,8},... | collective-permute-start | bytes 49160 | tf_op jit(solution)/shard_map/ppermute | solution.py:337
  40.2 1.2 %collective-permute-start.5 = (f32[2,2048]{1,0:T(2,128)S(1)}, f32[2,2048]{1,0:T(2,128)S(1)}, u32[]{:S(2)}, u32[]{:S(2)}) collective-permute-start(f32[2,2048]{1,0:T(2,128)S(1)} %add_add_fusion.3), channel_id=1, source_target_pairs={{0,16},{2,18},{4,20},{6,22},{8,24},{10,26},{12,28},{14,30},{16,0},... | collective-permute-start | bytes 49160 | tf_op jit(solution)/shard_map/ppermute | solution.py:337
  41.4 1.0 collective-permute-start.4
  42.3 0.9 collective-permute-done.6
  43.2 0.0 collective-permute-done.5
  43.2 2.0 %collective-permute-done.4 = f32[2,2048]{1,0:T(2,128)S(1)} collective-permute-done((f32[2,2048]{1,0:T(2,128)S(1)}, f32[2,2048]{1,0:T(2,128)S(1)}, u32[]{:S(2)}, u32[]{:S(2)}) %collective-permute-start.4) | collective-permute-done | bytes 16416 | tf_op jit(solution)/shard_map/ppermute | solution.py:337
  45.3 0.1 select_reduce_fusion
  45.5 0.4 copy-done.14
  45.9 13.1 %backward.1 = (f32[16,64,128]{2,1,0:T(8,128)}, f32[16,64,128]{2,1,0:T(8,128)}, f32[16,2048]{1,0:T(8,128)}) custom-call(s32[1]{0:T(128)} %bitcast.core_ref, bf16[16,16,128]{2,1,0:T(8,128)(2,1)} %copy-done.7, bf16[16,64,128]{2,1,0:T(8,128)(2,1)} %copy-done.3, bf16[16,64,128]{2,1,0:T(8,128)(2,1)} %copy-done.5, bf16[16,2048]{1,0:T(8,128)(2,1)} %copy-done.6, ...), custom_call_target="tpu_custom_call" | custom-call | tf_op jit(solution)/shard_map/backward/pallas_call | solution.py:225
  59.0 1.0 pad_maximum_fusion.1
  60.0 3.1 %collective-permute-start.9 = (f32[16,2048]{1,0:T(8,128)S(1)}, f32[16,2048]{1,0:T(8,128)S(1)}, u32[]{:S(2)}, u32[]{:S(2)}) collective-permute-start(f32[16,2048]{1,0:T(8,128)S(1)} %pad_maximum_fusion.1), channel_id=1, source_target_pairs={{0,1},{1,0},{2,3},{3,2},{4,5},{5,4},{6,7},{7,6},{8,9},{9,8},{10,11... | collective-permute-start | bytes 393224 | tf_op jit(solution)/shard_map/ppermute | solution.py:333
  63.1 0.1 collective-permute-start.16
  63.2 0.9 collective-permute-done.9
  64.1 1.6 %fusion.1 = f32[16,2048]{1,0:T(8,128)} fusion(f32[16,2048]{1,0:T(8,128)S(1)} %collective-permute-done.9, f32[4,2048]{1,0:T(4,128)S(1)} %select_maximum_fusion, f32[12,2048]{1,0:T(8,128)} %bitcast.26), kind=kLoop, calls=%fused_computation.24 | loop fusion | flops 65536 | bytes 393216 | tf_op jit(solution)/shard_map/add | solution.py:418
  65.7 0.1 collective-permute-start.12
  65.7 1.4 %collective-permute-start.11 = (f32[16,2048]{1,0:T(8,128)}, f32[16,2048]{1,0:T(8,128)}, u32[]{:S(2)}, u32[]{:S(2)}) collective-permute-start(f32[16,2048]{1,0:T(8,128)} %fusion.1), channel_id=1, source_target_pairs={{0,4},{2,6},{4,0},{6,2},{8,12},{10,14},{12,8},{14,10},{16,20},{18,... | collective-permute-start | bytes 393224 | tf_op jit(solution)/shard_map/ppermute | solution.py:337
  67.1 1.2 %collective-permute-start.10 = (f32[16,2048]{1,0:T(8,128)}, f32[16,2048]{1,0:T(8,128)}, u32[]{:S(2)}, u32[]{:S(2)}) collective-permute-start(f32[16,2048]{1,0:T(8,128)} %fusion.1), channel_id=1, source_target_pairs={{0,2},{2,0},{4,6},{6,4},{8,10},{10,8},{12,14},{14,12},{16,18},{18,... | collective-permute-start | bytes 393224 | tf_op jit(solution)/shard_map/ppermute | solution.py:337
  68.3 2.5 %copy.33 = bf16[5,8,32,512]{3,1,0,2:T(8,128)(2,1)} copy(f32[5,8,32,512]{3,2,1,0:T(8,128)S(1)} %copy-done.2) | data formatting | bytes 3932160 | tf_op args[0]
  70.8 0.9 add.76
  71.6 4.8 %all-to-all-start.1 = ((f32[16,64,128]{2,1,0:T(8,128)}), f32[16,64,128]{2,1,0:T(8,128)}, u32[]{:S(2)}, u32[]{:S(2)}) async-start(f32[16,64,128]{2,1,0:T(8,128)} %add.76), calls=%async_computation.1 | async-start | bytes 1048576 | tf_op jit(solution)/shard_map/all_to_all | solution.py:353
  76.4 0.0 collective-permute-done.11
  76.4 0.0 collective-permute-done.10
  76.4 1.8 %add_add_fusion.1 = f32[16,2048]{1,0:T(8,128)} fusion(f32[16,2048]{1,0:T(8,128)} %collective-permute-done.11, f32[16,2048]{1,0:T(8,128)} %collective-permute-done.12, f32[16,2048]{1,0:T(8,128)} %fusion.1, f32[16,2048]{1,0:T(8,128)} %collective-permute-done.10), kind=kLoop, calls=%fused_computation.6 | loop fusion | flops 98304 | bytes 655360 | tf_op jit(solution)/shard_map/add | solution.py:345
  78.2 3.0 %collective-permute-start.15 = (f32[16,2048]{1,0:T(8,128)}, f32[16,2048]{1,0:T(8,128)}, u32[]{:S(2)}, u32[]{:S(2)}) collective-permute-start(f32[16,2048]{1,0:T(8,128)} %add_add_fusion.1), channel_id=1, source_target_pairs={{0,24},{2,26},{4,28},{6,30},{8,16},{10,18},{12,20},{14,22},{16,8},... | collective-permute-start | bytes 393224 | tf_op jit(solution)/shard_map/ppermute | solution.py:337
  81.2 0.3 collective-permute-start.14
  81.5 0.3 collective-permute-start.13
  81.8 1.4 %slice_bitcast_fusion = (bf16[5,8,512]{2,1,0:T(8,128)(2,1)}, bf16[5,8,512]{2,1,0:T(8,128)(2,1)S(1)}) fusion(bf16[5,8,32,512]{3,1,0,2:T(8,128)(2,1)} %copy.33), kind=kLoop, calls=%fused_computation.7 | loop fusion | bytes 163840 | tf_op jit(solution)/shard_map/squeeze | solution.py:385
  83.2 2.6 %collective-permute-start.8 = (bf16[5,8,512]{2,1,0:T(8,128)(2,1)}, bf16[5,8,512]{2,1,0:T(8,128)(2,1)S(1)}, u32[]{:S(2)}, u32[]{:S(2)}) collective-permute-start(bf16[5,8,512]{2,1,0:T(8,128)(2,1)} %get-tuple-element.27), channel_id=1, source_target_pairs={{1,0},{2,1},{3,2},{4,3},{5,4},{6,5},{7,6},{8,7},{9,8},{10,9},{11,1... | collective-permute-start | bytes 122888 | tf_op jit(solution)/shard_map/ppermute | solution.py:385
  85.8 1.1 collective-permute-start.7
  86.9 14.8 %collective-permute-done.8.above_ref = bf16[5,8,512]{2,1,0:T(8,128)(2,1)S(1)} collective-permute-done((bf16[5,8,512]{2,1,0:T(8,128)(2,1)}, bf16[5,8,512]{2,1,0:T(8,128)(2,1)S(1)}, u32[]{:S(2)}, u32[]{:S(2)}) %collective-permute-start.8) | collective-permute-done | bytes 40992 | tf_op jit(solution)/shard_map/ppermute | solution.py:385
  101.7 0.0 collective-permute-done.7.below_ref
  101.7 3.6 %slab.1.field_ref = f32[5,8,32,512]{3,2,1,0:T(8,128)} custom-call(f32[5,8,32,512]{3,2,1,0:T(8,128)S(1)} %copy-done.2, f32[8,32,512]{2,1,0:T(8,128)S(1)} %copy-done.8, bf16[5,8,512]{2,1,0:T(8,128)(2,1)S(1)} %collective-permute-done.7.below_ref, bf16[5,8,512]{2,1,0:T(8,128)(2,1)S(1)} %collective-permute-done.8.above_ref), custom_call_target="tpu_custom_call" | custom-call | tf_op jit(solution)/shard_map/slab/pallas_call | solution.py:278
  105.3 1.9 %wall.1 = (f32[2,32,512]{2,1,0:T(8,128)}, f32[5,8,32,512]{3,2,1,0:T(8,128)}) custom-call(s32[8,128]{1,0:T(8,128)S(1)} %get-tuple-element.14.info_ref, f32[2,128]{1,0:T(2,128)S(1)} %get-tuple-element.26.pred_ref, f32[2,32,512]{2,1,0:T(8,128)S(1)} %copy-done.9, f32[5,8,32,512]{3,2,1,0:T(8,128)} %slab.1.field_ref), custom_call_target="tpu_custom_call", output_to_operand_aliasing={{1}: (3, {})} | custom-call | tf_op jit(solution)/shard_map/wall/pallas_call | solution.py:312
  107.2 0.0 collective-permute-done.13
  107.2 1.1 add_add_fusion
  108.4 0.0 copy-start.13
  108.4 0.1 constant_dynamic-slice_fusion
  108.4 0.5 fusion
  110.3 0.0 all-to-all-done.1
  110.3 1.9 %copy_bitcast_fusion = f32[64,2048]{1,0:T(8,128)} fusion(f32[16,64,128]{2,1,0:T(8,128)} %all-to-all-done.1), kind=kLoop, calls=%fused_computation.1 | loop fusion | bytes 1048576 | tf_op jit(solution)/shard_map/reshape | solution.py:408
  (34 shorter events, 0.2 us)
Async XLA Ops:
  0.6 1.6 %copy-start = (bf16[64,2048]{1,0:T(8,128)(2,1)S(1)}, bf16[64,2048]{1,0:T(8,128)(2,1)}, u32[]{:S(2)}) copy-start(bf16[64,2048]{1,0:T(8,128)(2,1)} %param.16) | copy-start | bytes 786436
  2.3 1.7 %copy-start.1 = (f32[5,8,32,512]{3,2,1,0:T(8,128)S(1)}, f32[5,8,32,512]{3,2,1,0:T(8,128)}, u32[]{:S(2)}) copy-start(f32[5,8,32,512]{3,2,1,0:T(8,128)} %flow_ref.3) | copy-start | bytes 7864324
  4.0 0.7 copy-start.11
  5.2 63.1 %copy-start.2 = (f32[5,8,32,512]{3,2,1,0:T(8,128)S(1)}, f32[5,8,32,512]{3,2,1,0:T(8,128)}, u32[]{:S(2)}) copy-start(f32[5,8,32,512]{3,2,1,0:T(8,128)} %flow_ref.3) | copy-start | bytes 7864324
  20.8 24.7 %copy-start.3 = (bf16[16,64,128]{2,1,0:T(8,128)(2,1)}, bf16[16,64,128]{2,1,0:T(8,128)(2,1)S(1)}, u32[]{:S(2)}) copy-start(bf16[16,64,128]{2,1,0:T(8,128)(2,1)S(1)} %slice.41.mine_ref) | copy-start | bytes 786436
  20.8 5.1 %collective-permute-start = (bf16[16,64,128]{2,1,0:T(8,128)(2,1)S(1)}, bf16[16,64,128]{2,1,0:T(8,128)(2,1)S(1)}, u32[]{:S(2)}, u32[]{:S(2)}) collective-permute-start(bf16[16,64,128]{2,1,0:T(8,128)(2,1)S(1)} %slice.41.mine_ref), channel_id=1, source_target_pairs={{0,1},{1,0},{2,3},{3,2},{4,5},{5,4},{6,7},{7,6},{8,9},{9,8},{10,11... | collective-permute-start | bytes 786440 | tf_op jit(solution)/shard_map/ppermute | solution.py:333
  24.4 21.1 %copy-start.6 = (bf16[16,2048]{1,0:T(8,128)(2,1)}, bf16[16,2048]{1,0:T(8,128)(2,1)S(1)}, u32[]{:S(2)}) copy-start(bf16[16,2048]{1,0:T(8,128)(2,1)S(1)} %pad.8.win_ref) | copy-start | bytes 196612
  25.0 20.4 %copy-start.10 = (bf16[2,128]{1,0:T(2,128)(2,1)}, bf16[2,128]{1,0:T(2,128)(2,1)S(1)}, u32[]{:S(2)}) copy-start(bf16[2,128]{1,0:T(2,128)(2,1)S(1)} %constant_dynamic-slice_fusion.2.wout_ref) | copy-start | bytes 1540
  25.9 19.6 %copy-start.7 = (bf16[16,16,128]{2,1,0:T(8,128)(2,1)}, bf16[16,16,128]{2,1,0:T(8,128)(2,1)S(1)}, u32[]{:S(2)}) copy-start(bf16[16,16,128]{2,1,0:T(8,128)(2,1)S(1)} %slice.40.rows_ref) | copy-start | bytes 196612
  25.9 19.6 %copy-start.5 = (bf16[16,64,128]{2,1,0:T(8,128)(2,1)}, bf16[16,64,128]{2,1,0:T(8,128)(2,1)S(1)}, u32[]{:S(2)}) copy-start(bf16[16,64,128]{2,1,0:T(8,128)(2,1)S(1)} %collective-permute-done.other_ref) | copy-start | bytes 786436
  32.8 1.0 copy-start.4
  33.7 3.5 %collective-permute-start.3 = (f32[2,2048]{1,0:T(2,128)S(1)}, f32[2,2048]{1,0:T(2,128)S(1)}, u32[]{:S(2)}, u32[]{:S(2)}) collective-permute-start(f32[2,2048]{1,0:T(2,128)S(1)} %get-tuple-element.16), channel_id=1, source_target_pairs={{0,6},{2,4},{4,2},{6,0},{8,14},{10,12},{12,10},{14,8},{16,22},{18,... | collective-permute-start | bytes 49160 | tf_op jit(solution)/shard_map/ppermute | solution.py:337
  35.6 2.6 %collective-permute-start.2 = (f32[2,2048]{1,0:T(2,128)S(1)}, f32[2,2048]{1,0:T(2,128)S(1)}, u32[]{:S(2)}, u32[]{:S(2)}) collective-permute-start(f32[2,2048]{1,0:T(2,128)S(1)} %get-tuple-element.16), channel_id=1, source_target_pairs={{0,4},{2,6},{4,0},{6,2},{8,12},{10,14},{12,8},{14,10},{16,20},{18,... | collective-permute-start | bytes 49160 | tf_op jit(solution)/shard_map/ppermute | solution.py:337
  36.1 2.6 %collective-permute-start.1 = (f32[2,2048]{1,0:T(2,128)S(1)}, f32[2,2048]{1,0:T(2,128)S(1)}, u32[]{:S(2)}, u32[]{:S(2)}) collective-permute-start(f32[2,2048]{1,0:T(2,128)S(1)} %get-tuple-element.16), channel_id=1, source_target_pairs={{0,2},{2,0},{4,6},{6,4},{8,10},{10,8},{12,14},{14,12},{16,18},{18,... | collective-permute-start | bytes 49160 | tf_op jit(solution)/shard_map/ppermute | solution.py:337
  38.7 4.5 %collective-permute-start.6 = (f32[2,2048]{1,0:T(2,128)S(1)}, f32[2,2048]{1,0:T(2,128)S(1)}, u32[]{:S(2)}, u32[]{:S(2)}) collective-permute-start(f32[2,2048]{1,0:T(2,128)S(1)} %add_add_fusion.3), channel_id=1, source_target_pairs={{0,24},{2,26},{4,28},{6,30},{8,16},{10,18},{12,20},{14,22},{16,8},... | collective-permute-start | bytes 49160 | tf_op jit(solution)/shard_map/ppermute | solution.py:337
  40.2 3.1 %collective-permute-start.5 = (f32[2,2048]{1,0:T(2,128)S(1)}, f32[2,2048]{1,0:T(2,128)S(1)}, u32[]{:S(2)}, u32[]{:S(2)}) collective-permute-start(f32[2,2048]{1,0:T(2,128)S(1)} %add_add_fusion.3), channel_id=1, source_target_pairs={{0,16},{2,18},{4,20},{6,22},{8,24},{10,26},{12,28},{14,30},{16,0},... | collective-permute-start | bytes 49160 | tf_op jit(solution)/shard_map/ppermute | solution.py:337
  41.4 3.9 %collective-permute-start.4 = (f32[2,2048]{1,0:T(2,128)S(1)}, f32[2,2048]{1,0:T(2,128)S(1)}, u32[]{:S(2)}, u32[]{:S(2)}) collective-permute-start(f32[2,2048]{1,0:T(2,128)S(1)} %add_add_fusion.3), channel_id=1, source_target_pairs={{0,8},{2,10},{4,12},{6,14},{8,0},{10,2},{12,4},{14,6},{16,24},{18,... | collective-permute-start | bytes 49160 | tf_op jit(solution)/shard_map/ppermute | solution.py:337
  45.3 0.6 copy-start.14
  59.0 11.8 %copy-start.12 = (f32[16,64,128]{2,1,0:T(8,128)S(1)}, f32[16,64,128]{2,1,0:T(8,128)}, u32[]{:S(2)}) copy-start(f32[16,64,128]{2,1,0:T(8,128)} %get-tuple-element.21) | copy-start | bytes 1572868
  60.0 4.1 %collective-permute-start.9 = (f32[16,2048]{1,0:T(8,128)S(1)}, f32[16,2048]{1,0:T(8,128)S(1)}, u32[]{:S(2)}, u32[]{:S(2)}) collective-permute-start(f32[16,2048]{1,0:T(8,128)S(1)} %pad_maximum_fusion.1), channel_id=1, source_target_pairs={{0,1},{1,0},{2,3},{3,2},{4,5},{5,4},{6,7},{7,6},{8,9},{9,8},{10,11... | collective-permute-start | bytes 393224 | tf_op jit(solution)/shard_map/ppermute | solution.py:333
  63.1 7.7 %collective-permute-start.16 = (f32[16,64,128]{2,1,0:T(8,128)}, f32[16,64,128]{2,1,0:T(8,128)S(1)}, u32[]{:S(2)}, u32[]{:S(2)}) collective-permute-start(f32[16,64,128]{2,1,0:T(8,128)} %get-tuple-element.22), channel_id=1, source_target_pairs={{0,1},{1,0},{2,3},{3,2},{4,5},{5,4},{6,7},{7,6},{8,9},{9,8},{10,11... | collective-permute-start | bytes 1572872 | tf_op jit(solution)/shard_map/ppermute | solution.py:333
  65.7 10.8 %collective-permute-start.12 = (f32[16,2048]{1,0:T(8,128)}, f32[16,2048]{1,0:T(8,128)}, u32[]{:S(2)}, u32[]{:S(2)}) collective-permute-start(f32[16,2048]{1,0:T(8,128)} %fusion.1), channel_id=1, source_target_pairs={{0,6},{2,4},{4,2},{6,0},{8,14},{10,12},{12,10},{14,8},{16,22},{18,... | collective-permute-start | bytes 393224 | tf_op jit(solution)/shard_map/ppermute | solution.py:337
  65.7 10.7 %collective-permute-start.11 = (f32[16,2048]{1,0:T(8,128)}, f32[16,2048]{1,0:T(8,128)}, u32[]{:S(2)}, u32[]{:S(2)}) collective-permute-start(f32[16,2048]{1,0:T(8,128)} %fusion.1), channel_id=1, source_target_pairs={{0,4},{2,6},{4,0},{6,2},{8,12},{10,14},{12,8},{14,10},{16,20},{18,... | collective-permute-start | bytes 393224 | tf_op jit(solution)/shard_map/ppermute | solution.py:337
  67.1 9.3 %collective-permute-start.10 = (f32[16,2048]{1,0:T(8,128)}, f32[16,2048]{1,0:T(8,128)}, u32[]{:S(2)}, u32[]{:S(2)}) collective-permute-start(f32[16,2048]{1,0:T(8,128)} %fusion.1), channel_id=1, source_target_pairs={{0,2},{2,0},{4,6},{6,4},{8,10},{10,8},{12,14},{14,12},{16,18},{18,... | collective-permute-start | bytes 393224 | tf_op jit(solution)/shard_map/ppermute | solution.py:337
  70.8 30.9 %copy-start.8 = (f32[8,32,512]{2,1,0:T(8,128)S(1)}, f32[8,32,512]{2,1,0:T(8,128)}, u32[]{:S(2)}) copy-start(f32[8,32,512]{2,1,0:T(8,128)} %diff_ref.1) | copy-start | bytes 1572868
  71.6 38.7 %all-to-all-start.1 = ((f32[16,64,128]{2,1,0:T(8,128)}), f32[16,64,128]{2,1,0:T(8,128)}, u32[]{:S(2)}, u32[]{:S(2)}) async-start(f32[16,64,128]{2,1,0:T(8,128)} %add.76), calls=%async_computation.1 | async-start | bytes 1048576 | tf_op jit(solution)/shard_map/all_to_all | solution.py:353
  78.2 29.0 %collective-permute-start.15 = (f32[16,2048]{1,0:T(8,128)}, f32[16,2048]{1,0:T(8,128)}, u32[]{:S(2)}, u32[]{:S(2)}) collective-permute-start(f32[16,2048]{1,0:T(8,128)} %add_add_fusion.1), channel_id=1, source_target_pairs={{0,24},{2,26},{4,28},{6,30},{8,16},{10,18},{12,20},{14,22},{16,8},... | collective-permute-start | bytes 393224 | tf_op jit(solution)/shard_map/ppermute | solution.py:337
  81.2 26.0 %collective-permute-start.14 = (f32[16,2048]{1,0:T(8,128)}, f32[16,2048]{1,0:T(8,128)}, u32[]{:S(2)}, u32[]{:S(2)}) collective-permute-start(f32[16,2048]{1,0:T(8,128)} %add_add_fusion.1), channel_id=1, source_target_pairs={{0,16},{2,18},{4,20},{6,22},{8,24},{10,26},{12,28},{14,30},{16,0},... | collective-permute-start | bytes 393224 | tf_op jit(solution)/shard_map/ppermute | solution.py:337
  81.5 25.7 %collective-permute-start.13 = (f32[16,2048]{1,0:T(8,128)}, f32[16,2048]{1,0:T(8,128)}, u32[]{:S(2)}, u32[]{:S(2)}) collective-permute-start(f32[16,2048]{1,0:T(8,128)} %add_add_fusion.1), channel_id=1, source_target_pairs={{0,8},{2,10},{4,12},{6,14},{8,0},{10,2},{12,4},{14,6},{16,24},{18,... | collective-permute-start | bytes 393224 | tf_op jit(solution)/shard_map/ppermute | solution.py:337
  83.2 18.5 %collective-permute-start.8 = (bf16[5,8,512]{2,1,0:T(8,128)(2,1)}, bf16[5,8,512]{2,1,0:T(8,128)(2,1)S(1)}, u32[]{:S(2)}, u32[]{:S(2)}) collective-permute-start(bf16[5,8,512]{2,1,0:T(8,128)(2,1)} %get-tuple-element.27), channel_id=1, source_target_pairs={{1,0},{2,1},{3,2},{4,3},{5,4},{6,5},{7,6},{8,7},{9,8},{10,9},{11,1... | collective-permute-start | bytes 122888 | tf_op jit(solution)/shard_map/ppermute | solution.py:385
  85.8 15.9 %collective-permute-start.7 = (bf16[5,8,512]{2,1,0:T(8,128)(2,1)S(1)}, bf16[5,8,512]{2,1,0:T(8,128)(2,1)S(1)}, u32[]{:S(2)}, u32[]{:S(2)}) collective-permute-start(bf16[5,8,512]{2,1,0:T(8,128)(2,1)S(1)} %get-tuple-element.28), channel_id=1, source_target_pairs={{0,1},{1,2},{2,3},{3,4},{4,5},{5,6},{6,7},{7,8},{8,9},{9,10},{10,1... | collective-permute-start | bytes 122888 | tf_op jit(solution)/shard_map/ppermute | solution.py:384
  86.9 18.4 %copy-start.9 = (f32[2,32,512]{2,1,0:T(8,128)S(1)}, f32[2,32,512]{2,1,0:T(8,128)}, u32[]{:S(2)}) copy-start(f32[2,32,512]{2,1,0:T(8,128)} %stress_ref.1) | copy-start | bytes 393220
  108.4 3.8 %copy-start.13 = (f32[16,2048]{1,0:T(8,128)}, f32[16,2048]{1,0:T(8,128)S(1)}, u32[]{:S(2)}) copy-start(f32[16,2048]{1,0:T(8,128)S(1)} %add_add_fusion) | copy-start | bytes 393220

commit v2 on v1

v2 whole, which is shorter than its diff:
```python
import functools
import math

import jax
import jax.numpy as jnp
from jax import lax
from jax.experimental import pallas as pl
from jax.experimental.pallas import tpu as pltpu
from jax.sharding import Mesh, PartitionSpec as P


CORES = 2
LANE = 128
TILE = 2048
STEP = 256
KEEP_BYTES = 16 << 20

advect_number = 0.3
wall_gain = 0.5
grad_number = 32.0

FEATURES = 12
CHANNELS = 14
ROWS = 16

CHIPS = ("sec", "chip")
EVERY = ("sec", "chip", "core")

NN = (((1,), (0,)), ((), ()))
NT = (((1,), (1,)), ((), ()))
TN = (((0,), (0,)), ((), ()))


def mm(left, right, dims=NN):
    return lax.dot_general(left, right, dims, preferred_element_type=jnp.float32)


def round_up(value, step):
    return -(-value // step) * step


def iota(shape, axis):
    return lax.broadcasted_iota(jnp.int32, shape, axis)


def params(mib, **more):
    return pltpu.CompilerParams(vmem_limit_bytes=mib << 20, **more)


def pick_kernel(
    counts_ref, routes_ref, index_ref, flow_ref, low_ref, high_ref, weight_ref,
    rows_ref, info_ref, first_ref, last_ref, *block_ref, nx,
):
    first_ref[...] = low_ref[:, :, 0].astype(jnp.bfloat16)
    last_ref[...] = high_ref[:, :, high_ref.shape[2] - 1].astype(jnp.bfloat16)
    tiles = counts_ref.shape[1]
    nz = flow_ref.shape[2]
    lanes = rows_ref.shape[2]
    shift = nx.bit_length() - 1
    counts = counts_ref[...].astype(jnp.float32)
    row, col = iota((tiles, tiles), 0), iota((tiles, tiles), 1)
    tall = jnp.sum(jnp.where(col == row, counts, 0.0), axis=1, keepdims=True)
    before = jnp.sum(jnp.where(row < col, tall, 0.0), axis=0, keepdims=True)
    place = iota((lanes, tiles), 0).astype(jnp.float32)
    index = index_ref[...].astype(jnp.float32) + 1.0
    routes = routes_ref[...].astype(jnp.float32) + 1.0
    point = jnp.full((lanes, 1), -1.0, jnp.float32)
    route = jnp.full((lanes, 1), -1.0, jnp.float32)
    for k in range(index_ref.shape[0]):
        here = (place == before + k) & (counts > k)
        point += jnp.sum(jnp.where(here, index[k : k + 1], 0.0), axis=1, keepdims=True)
        route += jnp.sum(jnp.where(here, routes, 0.0), axis=1, keepdims=True)
    side = iota((lanes, LANE), 1)
    both = jnp.where(side == 0, point, jnp.where(side == 1, route, -1.0))
    info = both.T[:8].astype(jnp.int32)
    info_ref[...] = info
    point = info[0:1]
    at_z = lax.shift_right_arithmetic(point, shift)
    at_x = jnp.where(point < 0, -1, point & (nx - 1))
    hot_x = jnp.where(iota((nx, lanes), 0) == at_x, 1.0, 0.0).astype(jnp.bfloat16)
    hot_z = iota((nz, lanes), 0) == at_z

    planes = [flow_ref[v, l] for v in range(4) for l in range(3)]
    planes += [flow_ref[v, 4] - flow_ref[v, 3] for v in (1, 3)]
    stack = jnp.concatenate([plane.astype(jnp.bfloat16) for plane in planes], axis=0)
    near = mm(stack, hot_x).reshape(CHANNELS, nz, lanes)
    found = jnp.sum(jnp.where(hot_z[None], near, 0.0), axis=1)
    spare = jnp.zeros((ROWS - CHANNELS, lanes), jnp.float32)
    packed = jnp.concatenate([found, spare], axis=0).astype(jnp.bfloat16)
    rows_ref[0] = packed
    if block_ref:
        chips, tall, width = block_ref[0].shape
        for j in range(chips):
            block_ref[0][j, : tall - ROWS] = weight_ref[:, j * width : (j + 1) * width]
            block_ref[0][j, tall - ROWS :] = packed


def whole(shape):
    return pl.BlockSpec(shape, lambda i: (0,) * len(shape))


def pick_samples(counts, routes, index, flow, weight, lanes, joint):
    capacity, tiles = index.shape
    nv, nl, nz, nx = flow.shape
    assert nx & (nx - 1) == 0 and nz % 8 == 0
    plane = jax.ShapeDtypeStruct((nv, nl, nx), jnp.bfloat16)
    outs = [
        jax.ShapeDtypeStruct((1, ROWS, lanes), jnp.bfloat16),
        jax.ShapeDtypeStruct((8, lanes), jnp.int32),
        plane,
        plane,
    ]
    if joint is not None:
        outs.append(jax.ShapeDtypeStruct(joint, jnp.bfloat16))
    return pl.pallas_call(
        functools.partial(pick_kernel, nx=nx),
        grid=(1,),
        in_specs=[
            whole((1, tiles)),
            whole((1, tiles)),
            whole((capacity, tiles)),
            whole((4, 5, nz, nx)),
            whole((nv, nl, 8, nx)),
            pl.BlockSpec((nv, nl, 8, nx), lambda i: (0, 0, nz // 8 - 1, 0)),
            whole(weight.shape),
        ],
        out_specs=[whole(out.shape) for out in outs],
        out_shape=outs,
        compiler_params=params(16),
        name="pick",
    )(counts, routes, index, flow, flow, flow, weight)


def widen_kernel(weight_ref, out_ref):
    out_ref[...] = jnp.zeros_like(out_ref)
    out_ref[:FEATURES] = weight_ref[...]


def widen(weight):
    shape = (ROWS, weight.shape[1])
    return pl.pallas_call(
        widen_kernel,
        grid=(1,),
        in_specs=[whole(weight.shape)],
        out_specs=whole(shape),
        out_shape=jax.ShapeDtypeStruct(shape, weight.dtype),
        compiler_params=params(4),
        name="widen",
    )(weight)


def features_of(rows_ref):
    blocks = [rows_ref[g] for g in range(rows_ref.shape[0])]
    across = blocks[0] if len(blocks) == 1 else jnp.concatenate(blocks, axis=1)
    across = across.astype(jnp.float32)
    return across, jnp.where(iota(across.shape, 0) < FEATURES, across, 0.0)


def forward_kernel(
    place_ref, got_ref, mine_ref, other_ref, win_ref, wout_ref,
    second_ref, pred_ref, rows_ref, weight_ref, *first_ref, step,
):
    @pl.when(pl.program_id(0) == 0)
    def _():
        core = place_ref[0]
        chips, rows, _ = mine_ref.shape
        for j in range(chips):
            at = pl.multiple_of((CORES * j + core) * rows, rows)
            weight_ref[pl.ds(at, rows), :] = mine_ref[j]
            at = pl.multiple_of((CORES * j + 1 - core) * rows, rows)
            weight_ref[pl.ds(at, rows), :] = other_ref[j]

    hidden = weight_ref.shape[0]
    rows_ref[...] = got_ref[...]
    _, features = features_of(got_ref)
    tall = features.T.astype(jnp.bfloat16)
    total = None
    for at in range(0, hidden, step):
        first = jnp.tanh(mm(tall, win_ref[:, at : at + step])).astype(jnp.bfloat16)
        if first_ref:
            first_ref[0][:, at : at + step] = first
        term = mm(first, weight_ref[at : at + step, :])
        total = term if total is None else total + term
    second = jnp.tanh(total).T
    second_ref[...] = second
    pred_ref[...] = mm(wout_ref[...], second.astype(jnp.bfloat16))


def forward(place, got, skip, mine, other, win, wout, rows_dev, group, keep):
    chips, _, width = mine.shape
    lanes = got.shape[2]
    hidden = win.shape[1]
    tile, samples = group * lanes, chips * lanes
    out_specs = [
        pl.BlockSpec((width, tile), lambda i: (0, i)),
        pl.BlockSpec((wout.shape[0], tile), lambda i: (0, i)),
        pl.BlockSpec((group, ROWS, lanes), lambda i: (i, 0, 0)),
        whole((hidden, width)),
    ]
    out_shape = [
        jax.ShapeDtypeStruct((width, samples), jnp.float32),
        jax.ShapeDtypeStruct((wout.shape[0], samples), jnp.float32),
        jax.ShapeDtypeStruct((chips, ROWS, lanes), got.dtype),
        jax.ShapeDtypeStruct((hidden, width), jnp.bfloat16),
    ]
    if keep:
        out_specs.append(pl.BlockSpec((tile, hidden), lambda i: (i, 0)))
        out_shape.append(jax.ShapeDtypeStruct((samples, hidden), jnp.bfloat16))
    return pl.pallas_call(
        functools.partial(forward_kernel, step=min(hidden, STEP)),
        grid=(chips // group,),
        in_specs=[
            pl.BlockSpec(memory_space=pltpu.SMEM),
            pl.BlockSpec((group, ROWS, lanes), lambda i: (i, skip, 0)),
            whole((chips, rows_dev, width)),
            whole((chips, rows_dev, width)),
            whole(win.shape),
            whole(wout.shape),
        ],
        out_specs=out_specs,
        out_shape=out_shape,
        compiler_params=params(28),
        name="forward",
    )(place, got, mine, other, win, wout)


def back_second(across, pred_ref, second_ref, wout_ref, lanes, live, scale):
    counted = (iota((1, across.shape[1]), 1) & (lanes - 1)) < live
    errors = jnp.where(counted, pred_ref[...] - across[FEATURES:CHANNELS], 0.0)
    back_out = (errors * scale).astype(jnp.bfloat16)
    second = second_ref[...]
    return mm(wout_ref[...], back_out, TN) * (1.0 - second * second)


def middle_kernel(
    place_ref, rows_ref, win_ref, wout_ref, second_ref, pred_ref, *refs, step, live, scale, kept
):
    first_ref = refs[0] if kept else None
    keep_ref, send_ref, grad_ref = refs[kept:]
    i = pl.program_id(0)

    @pl.when(i == 0)
    def _():
        grad_ref[...] = jnp.zeros_like(grad_ref)

    hidden = win_ref.shape[1]
    lanes = rows_ref.shape[2]
    across, features = features_of(rows_ref)
    back = back_second(across, pred_ref, second_ref, wout_ref, lanes, live, scale)
    across_back = back.astype(jnp.bfloat16)
    tall = features.T.astype(jnp.bfloat16)
    for at in range(0, hidden, step):
        if kept:
            first = first_ref[:, at : at + step]
        else:
            first = jnp.tanh(mm(tall, win_ref[:, at : at + step])).astype(jnp.bfloat16)
        grad_ref[:, at : at + step] += mm(across_back, first)

    @pl.when(i == pl.num_programs(0) - 1)
    def _():
        core = place_ref[0]
        chips, rows, _ = keep_ref.shape
        for j in range(chips):
            pair = grad_ref[:, CORES * j * rows : CORES * (j + 1) * rows].T
            low, high = pair[:rows], pair[rows:]
            keep_ref[j] = jnp.where(core == 0, low, high)
            send_ref[j] = jnp.where(core == 0, high, low)


def middle_gradient(place, rows, win, wout, second, pred, first, rows_dev, group, live, scale):
    chips, _, lanes = rows.shape
    hidden = win.shape[1]
    width = wout.shape[1]
    tile = group * lanes
    assert lanes & (lanes - 1) == 0
    kept = len(first)
    blocks = jax.ShapeDtypeStruct((chips, rows_dev, width), jnp.float32)
    return pl.pallas_call(
        functools.partial(
            middle_kernel, step=min(hidden, STEP), live=live, scale=scale, kept=kept
        ),
        grid=(chips // group,),
        in_specs=[
            pl.BlockSpec(memory_space=pltpu.SMEM),
            pl.BlockSpec((group, ROWS, lanes), lambda i: (i, 0, 0)),
            whole(win.shape),
            whole(wout.shape),
            pl.BlockSpec((width, tile), lambda i: (0, i)),
            pl.BlockSpec((wout.shape[0], tile), lambda i: (0, i)),
        ]
        + [pl.BlockSpec((tile, hidden), lambda i: (i, 0))] * kept,
        out_specs=[whole(blocks.shape), whole(blocks.shape)],
        out_shape=[blocks, blocks],
        scratch_shapes=[pltpu.VMEM((width, hidden), jnp.float32)],
        compiler_params=params(16),
        name="middle",
    )(place, rows, win, wout, second, pred, *first)


def input_kernel(
    place_ref, rows_ref, win_ref, wout_ref, weight_ref, second_ref, pred_ref, all_ref, own_ref,
    info_ref, stay_ref, send_ref, gin_ref, *, step, live, scale, devices,
):
    @pl.when(pl.program_id(0) == 0)
    def _():
        gin_ref[...] = jnp.zeros_like(gin_ref)
        lanes = info_ref.shape[1]
        at = pl.multiple_of(place_ref[1] * lanes, lanes)
        errors = all_ref[:, pl.ds(at, lanes)] - own_ref[0, FEATURES:CHANNELS].astype(jnp.float32)
        squares = 0.5 * jnp.sum(errors * errors, axis=0, keepdims=True)
        route = info_ref[1:2].astype(jnp.float32)
        side = iota((8, lanes), 0)
        both = jnp.where(side == 0, route, squares).T
        across = round_up(devices, LANE)
        match = both[:, 0:1] == iota((lanes, across), 1).astype(jnp.float32)
        loss = jnp.sum(jnp.where(match, both[:, 1:2], 0.0), axis=0, keepdims=True)
        count = jnp.sum(jnp.where(match, 1.0, 0.0), axis=0, keepdims=True)
        gin_ref[FEATURES:CHANNELS, :across] = jnp.concatenate([loss, count], axis=0)

    hidden = win_ref.shape[1]
    across, features = features_of(rows_ref)
    wide = features.astype(jnp.bfloat16)
    tall = features.T.astype(jnp.bfloat16)
    back = back_second(
        across, pred_ref, second_ref, wout_ref, rows_ref.shape[2], live, scale
    )
    tall_back = back.T.astype(jnp.bfloat16)
    for at in range(0, hidden, step):
        act = jnp.tanh(mm(tall, win_ref[:, at : at + step]))
        back_hidden = mm(tall_back, weight_ref[at : at + step, :], NT)
        back_first = (back_hidden * (1.0 - act * act)).astype(jnp.bfloat16)
        gin_ref[:, at : at + step] += mm(wide, back_first)

    @pl.when(pl.program_id(0) == pl.num_programs(0) - 1)
    def _():
        low, high = gin_ref[:, : hidden // CORES], gin_ref[:, hidden // CORES :]
        first = place_ref[0] == 0
        stay_ref[...] = jnp.where(first, low, high)
        send_ref[...] = jnp.where(first, high, low)


def input_gradient(
    place, rows, win, wout, weight, second, pred, own, info, group, live, scale, devices
):
    chips, _, lanes = rows.shape
    hidden, width = weight.shape
    tile = group * lanes
    half = jax.ShapeDtypeStruct((ROWS, hidden // CORES), jnp.float32)
    return pl.pallas_call(
        functools.partial(
            input_kernel, step=min(hidden, STEP), live=live, scale=scale, devices=devices
        ),
        grid=(chips // group,),
        in_specs=[
            pl.BlockSpec(memory_space=pltpu.SMEM),
            pl.BlockSpec((group, ROWS, lanes), lambda i: (i, 0, 0)),
            whole(win.shape),
            whole(wout.shape),
            whole(weight.shape),
            pl.BlockSpec((width, tile), lambda i: (0, i)),
            pl.BlockSpec((pred.shape[0], tile), lambda i: (0, i)),
            whole(pred.shape),
            whole(own.shape),
            whole(info.shape),
        ],
        out_specs=[whole(half.shape), whole(half.shape)],
        out_shape=[half, half],
        scratch_shapes=[pltpu.VMEM((ROWS, hidden), jnp.float32)],
        compiler_params=params(16),
        name="input",
    )(place, rows, win, wout, weight, second, pred, pred, own, info)


def join_kernel(place_ref, half_ref, rest_ref, gin_ref, loss_ref):
    first = place_ref[0] == 0
    half, rest = half_ref[...], rest_ref[...]
    low, high = jnp.where(first, half, rest), jnp.where(first, rest, half)
    across = low.shape[1]
    gin_ref[:, :across] = low[:FEATURES]
    gin_ref[:, across:] = high[:FEATURES]
    mine = iota((1, across), 1) == place_ref[1] * CORES + place_ref[0]
    loss = jnp.sum(jnp.where(mine, low[FEATURES : FEATURES + 1], 0.0), axis=1, keepdims=True)
    count = jnp.sum(jnp.where(mine, low[FEATURES + 1 : CHANNELS], 0.0), axis=1, keepdims=True)
    loss_ref[...] = loss / count


def join_halves(place, half, rest):
    across = half.shape[1] * CORES
    return pl.pallas_call(
        join_kernel,
        grid=(1,),
        in_specs=[pl.BlockSpec(memory_space=pltpu.SMEM), whole(half.shape), whole(rest.shape)],
        out_specs=[whole((FEATURES, across)), whole((1, 1))],
        out_shape=[
            jax.ShapeDtypeStruct((FEATURES, across), jnp.float32),
            jax.ShapeDtypeStruct((1, 1), jnp.float32),
        ],
        compiler_params=params(8),
        name="join",
    )(place, half, rest)


def lay_kernel(blocks_ref, out_ref):
    chips, _, width = blocks_ref.shape
    for j in range(chips):
        out_ref[:, j * width : (j + 1) * width] = blocks_ref[j]


def lay_rows(blocks):
    chips, rows, width = blocks.shape
    return pl.pallas_call(
        lay_kernel,
        grid=(1,),
        in_specs=[whole(blocks.shape)],
        out_specs=whole((rows, chips * width)),
        out_shape=jax.ShapeDtypeStruct((rows, chips * width), blocks.dtype),
        compiler_params=params(8),
        name="lay",
    )(blocks)


def slab_kernel(flow_ref, diff_ref, below_ref, above_ref, out_ref):
    layers, nz, nx = flow_ref.shape[1:]
    at_z, at_x = iota((nz, nx), 0), iota((nz, nx), 1)
    first_z, last_z = at_z == 0, at_z == nz - 1
    first_x, last_x = at_x == 0, at_x == nx - 1
    below_edge = below_ref[0].astype(jnp.float32)
    above_edge = above_ref[0].astype(jnp.float32)
    for l in range(layers):
        mid = flow_ref[0, l]
        below_x = jnp.where(first_x, mid, pltpu.roll(mid, 1, 1))
        above_x = jnp.where(last_x, mid, pltpu.roll(mid, nx - 1, 1))
        below_z = jnp.where(first_z, below_edge[l : l + 1], pltpu.roll(mid, 1, 0))
        above_z = jnp.where(last_z, above_edge[l : l + 1], pltpu.roll(mid, nz - 1, 0))
        below_y = flow_ref[0, max(l - 1, 0)]
        above_y = flow_ref[0, min(l + 1, layers - 1)]
        spread = below_x + above_x + below_y + above_y + below_z + above_z - 6.0 * mid
        out_ref[0, l] = mid + advect_number * (below_x - mid) + diff_ref[l] * spread


def slab(flow, diff, below, above):
    vars_, layers, nz, nx = flow.shape
    block = pl.BlockSpec((1, layers, nz, nx), lambda v: (v, 0, 0, 0))
    edge = pl.BlockSpec((1, layers, nx), lambda v: (v, 0, 0))
    return pl.pallas_call(
        slab_kernel,
        grid=(vars_,),
        in_specs=[block, pl.BlockSpec((layers, nz, nx), lambda v: (0, 0, 0)), edge, edge],
        out_specs=block,
        out_shape=jax.ShapeDtypeStruct(flow.shape, flow.dtype),
        compiler_params=params(16),
        name="slab",
    )(flow, diff, below, above)


def wall_kernel(place_ref, info_ref, pred_ref, stress_ref, field_ref, stress_out, field_out):
    nz, nx = stress_ref.shape[1:]
    lanes = info_ref.shape[1]
    shift = nx.bit_length() - 1
    point = info_ref[0:1, :]
    at_z = lax.shift_right_arithmetic(point, shift)
    at_x = jnp.where(point < 0, -1, point & (nx - 1))
    hot_x = jnp.where(iota((nx, lanes), 0) == at_x, 1.0, 0.0).astype(jnp.bfloat16)
    hot_z = jnp.where(iota((nz, lanes), 0) == at_z, 1.0, 0.0)
    mask = jnp.broadcast_to(point >= 0, hot_z.shape)
    hit = mm(hot_z.astype(jnp.bfloat16), hot_x, NT)
    at = pl.multiple_of(place_ref[1] * lanes, lanes)
    own = pred_ref[:, pl.ds(at, lanes)]
    sent = jnp.where(pl.program_id(0) == 0, own[0:1], own[1:2])
    put = jnp.where(mask, hot_z * sent, 0.0).astype(jnp.bfloat16)
    fresh = jnp.where(hit > 0.5, mm(put, hot_x, NT), stress_ref[0])
    stress_out[0] = fresh
    field_out[0, 0] = field_ref[0, 0] - wall_gain * fresh


def wall(place, info, pred, stress, field):
    nz, nx = stress.shape[1:]
    plane = pl.BlockSpec((1, nz, nx), lambda i: (i, 0, 0))
    layer = pl.BlockSpec((1, 1, nz, nx), lambda i: (2 * i + 1, 0, 0, 0))
    return pl.pallas_call(
        wall_kernel,
        grid=(2,),
        in_specs=[
            pl.BlockSpec(memory_space=pltpu.SMEM),
            whole(info.shape),
            whole(pred.shape),
            plane,
            layer,
        ],
        out_specs=[plane, layer],
        out_shape=[
            jax.ShapeDtypeStruct(stress.shape, stress.dtype),
            jax.ShapeDtypeStruct(field.shape, field.dtype),
        ],
        input_output_aliases={4: 1},
        compiler_params=params(16),
        name="wall",
    )(place, info, pred, stress, field)


def swap_cores(block):
    return lax.ppermute(block, "core", [(0, 1), (1, 0)])


def flip(block, mask, chips):
    return lax.ppermute(block, CHIPS, [(i, i ^ mask) for i in range(chips)])


def sum_chips(block, chips, most):
    mask = 1
    while mask < chips:
        fan = min(most, chips // mask)
        others = [flip(block, k * mask, chips) for k in range(1, fan)]
        if fan == 4:
            block = (block + others[0]) + (others[1] + others[2])
        else:
            block = block + others[0]
        mask *= fan
    return block


def exchange(blocks):
    return lax.all_to_all(blocks, CHIPS, split_axis=0, concat_axis=0, tiled=True)


def step(
    flow_state,
    diffusion,
    wall_stress,
    batch_counts,
    batch_routes,
    wall_index,
    input_weight,
    middle_weight,
    output_weight,
):
    tile_count, capacity = wall_index.shape
    chips = lax.axis_size(CHIPS)
    devices = chips * CORES
    assert chips & (chips - 1) == 0
    chip, core = lax.axis_index(CHIPS), lax.axis_index("core")
    rows_dev, hidden = middle_weight.shape
    width = hidden // chips
    live_dev = 5 * tile_count * capacity // 8
    lanes = LANE
    while lanes < live_dev:
        lanes *= 2
    group = max(1, min(chips, TILE // lanes))
    scale = grad_number / math.sqrt(live_dev * devices)

    order = [(i, (i + 1) % devices) for i in range(devices)]
    back_order = [(b, a) for a, b in order]
    place = jnp.stack([core, chip]).astype(jnp.int32)
    joint = lanes == width and rows_dev % ROWS == 0
    far = lambda array: pltpu.with_memory_space_constraint(array, pltpu.HBM)
    own, info, first_z, last_z, *blocks = pick_samples(
        far(batch_counts),
        far(batch_routes.reshape(1, tile_count)),
        far(wall_index.T),
        far(flow_state),
        far(middle_weight),
        lanes,
        (chips, rows_dev + ROWS, width) if joint else None,
    )
    below = lax.ppermute(last_z, EVERY, order)
    above = lax.ppermute(first_z, EVERY, back_order)
    if joint:
        mine = exchange(blocks[0])
        got, skip = mine, rows_dev // ROWS
    else:
        mine = exchange(
            jnp.transpose(middle_weight.reshape(rows_dev, chips, width), (1, 0, 2))
        )
        got, skip = None, 0
    if not joint:
        got = exchange(jnp.broadcast_to(own, (chips, ROWS, lanes)))
    other = swap_cores(mine)

    win = widen(input_weight)
    wout = lax.dynamic_slice_in_dim(output_weight, chip * width, width, axis=1)
    keep = chips * lanes * hidden * 2 <= KEEP_BYTES
    second, part, rows, weight, *first = forward(
        place, got, skip, mine, other, win, wout, rows_dev, group, keep
    )
    pred = sum_chips(part, chips, 4)

    stay, send = middle_gradient(
        place, rows, win, wout, second, pred, first, rows_dev, group, live_dev, scale
    )
    summed = stay + swap_cores(send)
    grad = exchange(summed)
    grad_w_mid = lay_rows(grad)

    stay, send = input_gradient(
        place, rows, win, wout, weight, second, pred, own, info, group, live_dev, scale, devices
    )
    half = stay + swap_cores(send)
    half = sum_chips(half, chips, 2)
    rest = swap_cores(half)
    grad_w_in, loss = join_halves(place, half, rest)
    batch_loss = loss.reshape(1)

    field = slab(flow_state, diffusion, below, above)
    new_stress, new_field = wall(place, info, pred, wall_stress, field)
    return (new_field, new_stress, batch_loss, grad_w_in, grad_w_mid)


def solution(mesh):
    sec, dev = mesh.shape["sec"], mesh.shape["dev"]
    inner = Mesh(mesh.devices.reshape(sec, dev // CORES, CORES), EVERY)
    in_specs = (
        P(None, None, EVERY, None),
        P(None, EVERY, None),
        P(None, EVERY, None),
        P(EVERY, None),
        P(EVERY, None),
        P(EVERY, None),
        P(),
        P(EVERY, None),
        P(),
    )
    out_specs = (
        P(None, None, EVERY, None),
        P(None, EVERY, None),
        P(EVERY),
        P(),
        P(EVERY, None),
    )
    return jax.shard_map(step, mesh=inner, in_specs=in_specs, out_specs=out_specs, check_vma=False)
```

time: 114 us -> 99.6 us (0.87)
  the two profiles are of different devices: /device:TPU:11 before, /device:TPU:27 now
where the time goes in v2:
time: 99.6 us; the launch traced here: 99.2 us
  waiting for transfers between devices  28.3 us (28%)
  starting transfers between devices  26.7 us (27%)
  Pallas kernels  25.4 us (26%)
  blocking collectives  14.7 us (15%)
  local copies, waits for them, and re-layouts  2.3 us (2%)
  other arithmetic  1.03 us (1%)
    ppermute x10, waiting for transfers between devices, flip(): return lax.ppermute(block, CHIPS, [(i, i ^ mask) for i in range(chips)])  17.7 us
    all_to_all x1, blocking collectives, exchange(): lax.all_to_all(blocks, CHIPS, split_axis=0, concat_axis=0, tiled=True)  14.7 us
    ppermute x4, starting transfers between devices, swap_cores(): return lax.ppermute(block, 'core', [(0, 1), (1, 0)])  10.9 us
    ppermute x10, starting transfers between devices, flip(): return lax.ppermute(block, CHIPS, [(i, i ^ mask) for i in range(chips)])  8.63 us
    pallas_call x1, Pallas kernels, input_gradient(): pl.pallas_call(functools.partial(input_kernel, step=min(hidden, STEP), li...  6.91 us
    all_to_all x1, starting transfers between devices, exchange(): lax.all_to_all(blocks, CHIPS, split_axis=0, concat_axis=0, tiled=True)  6.04 us
    pallas_call x1, Pallas kernels, forward(): pl.pallas_call(functools.partial(forward_kernel, step=min(hidden, STEP)),...  5.94 us
    ppermute x1, waiting for transfers between devices, step(): above = lax.ppermute(first_z, EVERY, back_order)  5.92 us
  transfers between devices with their start and end apart: 17, of which 13 were waited for; matrix products, arithmetic and copies ran while one was open for 0% of the time, Pallas kernels for 14%

profile of v2, /device:TPU:27, one launch (start us, length us, event | category | flops | bytes accessed | tf_op | source)
XLA Modules:
  0.0 99.2 jit_solution(2697247736474751866)
XLA Ops:
  0.6 0.0 copy-start
  0.6 0.0 copy-start.8
  0.7 2.6 %pick.1 = (bf16[1,16,128]{2,1,0:T(8,128)(2,1)S(1)}, s32[8,128]{1,0:T(8,128)S(1)}, bf16[5,8,512]{2,1,0:T(8,128)(2,1)S(1)}, bf16[5,8,512]{2,1,0:T(8,128)(2,1)S(1)}, bf16[16,80,128]{2,1,0:T(8,128)(2,1)S(1)}) custom-call(s32[1,48]{1,0:T(1,128)} %counts_ref.1, s32[1,48]{1,0:T(1,128)} %bitcast.6, s32[4,48]{1,0:T(4,128)} %bitcast.5, f32[5,8,32,512]{3,2,1,0:T(8,128)} %flow_ref.3, ...), custom_call_target="tpu_custom_call" | custom-call | tf_op jit(solution)/shard_map/pick/pallas_call | solution.py:115
  3.3 14.7 %all_to_all.10.got_ref.mine_ref = bf16[16,80,128]{2,1,0:T(8,128)(2,1)S(1)} all-to-all(bf16[16,80,128]{2,1,0:T(8,128)(2,1)S(1)} %get-tuple-element.24), channel_id=1, replica_groups=mesh['sec'=2,'chip'=8,'core'=2] {'sec','chip'}, dimensions={0} | all-to-all | bytes 655360 | tf_op jit(solution)/shard_map/all_to_all | solution.py:523
  18.0 1.3 %collective-permute-start = (bf16[16,80,128]{2,1,0:T(8,128)(2,1)S(1)}, bf16[16,80,128]{2,1,0:T(8,128)(2,1)S(1)}, u32[]{:S(2)}, u32[]{:S(2)}) collective-permute-start(bf16[16,80,128]{2,1,0:T(8,128)(2,1)S(1)} %all_to_all.10.got_ref.mine_ref), channel_id=1, source_target_pairs={{0,1},{1,0},{2,3},{3,2},{4,5},{5,4},{6,7},{7,6},{8,9},{9,8},{10,11... | collective-permute-start | bytes 983048 | tf_op jit(solution)/shard_map/ppermute | solution.py:502
  19.3 0.0 copy-done.8
  19.3 0.0 copy-done
  19.4 0.1 pad_add_fusion.place_ref
  19.4 1.1 %collective-permute-done.other_ref = bf16[16,80,128]{2,1,0:T(8,128)(2,1)S(1)} collective-permute-done((bf16[16,80,128]{2,1,0:T(8,128)(2,1)S(1)}, bf16[16,80,128]{2,1,0:T(8,128)(2,1)S(1)}, u32[]{:S(2)}, u32[]{:S(2)}) %collective-permute-start) | collective-permute-done | bytes 327712 | tf_op jit(solution)/shard_map/ppermute | solution.py:502
  20.6 5.9 %forward.1 = (f32[128,2048]{1,0:T(8,128)S(1)}, f32[2,2048]{1,0:T(2,128)S(1)}, bf16[16,16,128]{2,1,0:T(8,128)(2,1)S(1)}, bf16[2048,128]{1,0:T(8,128)(2,1)S(1)}, bf16[2048,2048]{1,0:T(8,128)(2,1)S(1)}) custom-call(s32[2]{0:T(128)S(1)} %pad_add_fusion.place_ref, bf16[16,80,128]{2,1,0:T(8,128)(2,1)S(1)} %all_to_all.10.got_ref.mine_ref, ...), custom_call_target="tpu_custom_call" | custom-call | tf_op jit(solution)/shard_map/forward/pallas_call | solution.py:209
  26.5 0.0 copy-start.2
  26.5 0.0 copy-start.5
  26.5 1.2 %collective-permute-start.1 = (f32[2,2048]{1,0:T(2,128)S(1)}, f32[2,2048]{1,0:T(2,128)S(1)}, u32[]{:S(2)}, u32[]{:S(2)}) collective-permute-start(f32[2,2048]{1,0:T(2,128)S(1)} %get-tuple-element.25), channel_id=1, source_target_pairs={{0,2},{2,0},{4,6},{6,4},{8,10},{10,8},{12,14},{14,12},{16,18},{18,... | collective-permute-start | bytes 49160 | tf_op jit(solution)/shard_map/ppermute | solution.py:506
  27.7 0.1 collective-permute-start.2
  27.8 1.4 %collective-permute-start.3 = (f32[2,2048]{1,0:T(2,128)S(1)}, f32[2,2048]{1,0:T(2,128)S(1)}, u32[]{:S(2)}, u32[]{:S(2)}) collective-permute-start(f32[2,2048]{1,0:T(2,128)S(1)} %get-tuple-element.25), channel_id=1, source_target_pairs={{0,6},{2,4},{4,2},{6,0},{8,14},{10,12},{12,10},{14,8},{16,22},{18,... | collective-permute-start | bytes 49160 | tf_op jit(solution)/shard_map/ppermute | solution.py:506
  29.2 0.0 collective-permute-done.1
  29.2 1.1 %collective-permute-done.2 = f32[2,2048]{1,0:T(2,128)S(1)} collective-permute-done((f32[2,2048]{1,0:T(2,128)S(1)}, f32[2,2048]{1,0:T(2,128)S(1)}, u32[]{:S(2)}, u32[]{:S(2)}) %collective-permute-start.2) | collective-permute-done | bytes 16416 | tf_op jit(solution)/shard_map/ppermute | solution.py:506
  30.3 1.0 collective-permute-done.3
  31.3 1.9 %collective-permute-start.4 = (f32[2,2048]{1,0:T(2,128)S(1)}, f32[2,2048]{1,0:T(2,128)S(1)}, u32[]{:S(2)}, u32[]{:S(2)}) collective-permute-start(f32[2,2048]{1,0:T(2,128)S(1)} %add_add_fusion.1), channel_id=1, source_target_pairs={{0,8},{2,10},{4,12},{6,14},{8,0},{10,2},{12,4},{14,6},{16,24},{18,... | collective-permute-start | bytes 49160 | tf_op jit(solution)/shard_map/ppermute | solution.py:506
  33.2 0.7 collective-permute-start.5
  34.0 1.0 collective-permute-start.6
  34.9 0.0 collective-permute-done.4
  34.9 0.9 collective-permute-done.5
  35.8 2.5 %collective-permute-done.6 = f32[2,2048]{1,0:T(2,128)S(1)} collective-permute-done((f32[2,2048]{1,0:T(2,128)S(1)}, f32[2,2048]{1,0:T(2,128)S(1)}, u32[]{:S(2)}, u32[]{:S(2)}) %collective-permute-start.6) | collective-permute-done | bytes 16416 | tf_op jit(solution)/shard_map/ppermute | solution.py:506
  38.4 2.2 %middle.1 = (f32[16,64,128]{2,1,0:T(8,128)S(1)}, f32[16,64,128]{2,1,0:T(8,128)S(1)}) custom-call(s32[2]{0:T(128)S(1)} %pad_add_fusion.place_ref, bf16[16,16,128]{2,1,0:T(8,128)(2,1)S(1)} %get-tuple-element.30.rows_ref, bf16[16,2048]{1,0:T(8,128)(2,1)S(1)} %widen.1.win_ref, bf16[2,128]{1,0:T(2,128)(2,1)S(1)} %constant_dynamic-slice_fusion.wout_ref, ...), custom_call_target="tpu_custom_call" | custom-call | tf_op jit(solution)/shard_map/middle/pallas_call | solution.py:278
  40.6 0.0 copy-done.2
  40.6 0.0 copy-done.5
  40.6 3.9 %collective-permute-start.15 = (f32[16,64,128]{2,1,0:T(8,128)S(1)}, f32[16,64,128]{2,1,0:T(8,128)S(1)}, u32[]{:S(2)}, u32[]{:S(2)}) collective-permute-start(f32[16,64,128]{2,1,0:T(8,128)S(1)} %get-tuple-element.40), channel_id=1, source_target_pairs={{0,1},{1,0},{2,3},{3,2},{4,5},{5,4},{6,7},{7,6},{8,9},{9,8},{10,11... | collective-permute-start | bytes 1572872 | tf_op jit(solution)/shard_map/ppermute | solution.py:502
  44.4 1.5 %collective-permute-done.15 = f32[16,64,128]{2,1,0:T(8,128)S(1)} collective-permute-done((f32[16,64,128]{2,1,0:T(8,128)S(1)}, f32[16,64,128]{2,1,0:T(8,128)S(1)}, u32[]{:S(2)}, u32[]{:S(2)}) %collective-permute-start.15) | collective-permute-done | bytes 524320 | tf_op jit(solution)/shard_map/ppermute | solution.py:502
  46.0 0.0 copy-start.1
  46.0 0.9 add.55
  46.8 6.0 %all-to-all-start.1 = ((f32[16,64,128]{2,1,0:T(8,128)}), f32[16,64,128]{2,1,0:T(8,128)S(1)}, u32[]{:S(2)}, u32[]{:S(2)}) async-start(f32[16,64,128]{2,1,0:T(8,128)} %add.55), calls=%async_computation.1 | async-start | bytes 1048576 | tf_op jit(solution)/shard_map/all_to_all | solution.py:523
  52.9 0.0 copy-start.3
  52.9 1.2 %copy-done.3 = f32[128,2048]{1,0:T(8,128)S(1)} copy-done((f32[128,2048]{1,0:T(8,128)S(1)}, f32[128,2048]{1,0:T(8,128)}, u32[]{:S(2)}) %copy-start.3) | copy-done | bytes 1048600
  54.1 0.0 copy-start.6
  54.1 1.0 %copy-done.6 = bf16[2048,128]{1,0:T(8,128)(2,1)S(1)} copy-done((bf16[2048,128]{1,0:T(8,128)(2,1)S(1)}, bf16[2048,128]{1,0:T(8,128)(2,1)}, u32[]{:S(2)}) %copy-start.6) | copy-done | bytes 524312
  55.2 0.0 copy-start.4
  55.2 6.9 %input.1 = (f32[16,1024]{1,0:T(8,128)S(1)}, f32[16,1024]{1,0:T(8,128)S(1)}) custom-call(s32[2]{0:T(128)S(1)} %pad_add_fusion.place_ref, bf16[16,16,128]{2,1,0:T(8,128)(2,1)S(1)} %get-tuple-element.30.rows_ref, bf16[16,2048]{1,0:T(8,128)(2,1)S(1)} %widen.1.win_ref, bf16[2,128]{1,0:T(2,128)(2,1)S(1)} %constant_dynamic-slice_fusion.wout_ref, ...), custom_call_target="tpu_custom_call" | custom-call | tf_op jit(solution)/shard_map/input/pallas_call | solution.py:349
  62.1 0.9 collective-permute-start.9
  63.0 0.9 collective-permute-done.9
  63.9 0.3 collective-permute-start.10
  64.3 2.8 %collective-permute-done.10 = f32[16,1024]{1,0:T(8,128)S(1)} collective-permute-done((f32[16,1024]{1,0:T(8,128)S(1)}, f32[16,1024]{1,0:T(8,128)S(1)}, u32[]{:S(2)}, u32[]{:S(2)}) %collective-permute-start.10) | collective-permute-done | bytes 65568 | tf_op jit(solution)/shard_map/ppermute | solution.py:506
  67.1 0.3 collective-permute-start.11
  67.5 2.8 %collective-permute-done.11 = f32[16,1024]{1,0:T(8,128)S(1)} collective-permute-done((f32[16,1024]{1,0:T(8,128)S(1)}, f32[16,1024]{1,0:T(8,128)S(1)}, u32[]{:S(2)}, u32[]{:S(2)}) %collective-permute-start.11) | collective-permute-done | bytes 65568 | tf_op jit(solution)/shard_map/ppermute | solution.py:506
  70.3 0.4 collective-permute-start.12
  70.7 4.4 %collective-permute-done.12 = f32[16,1024]{1,0:T(8,128)S(1)} collective-permute-done((f32[16,1024]{1,0:T(8,128)S(1)}, f32[16,1024]{1,0:T(8,128)S(1)}, u32[]{:S(2)}, u32[]{:S(2)}) %collective-permute-start.12) | collective-permute-done | bytes 65568 | tf_op jit(solution)/shard_map/ppermute | solution.py:506
  75.1 1.2 %collective-permute-start.13 = (f32[16,1024]{1,0:T(8,128)S(1)}, f32[16,1024]{1,0:T(8,128)S(1)}, u32[]{:S(2)}, u32[]{:S(2)}) collective-permute-start(f32[16,1024]{1,0:T(8,128)S(1)} %add.53), channel_id=1, source_target_pairs={{0,16},{2,18},{4,20},{6,22},{8,24},{10,26},{12,28},{14,30},{16,0},... | collective-permute-start | bytes 196616 | tf_op jit(solution)/shard_map/ppermute | solution.py:506
  76.3 2.2 %collective-permute-done.13 = f32[16,1024]{1,0:T(8,128)S(1)} collective-permute-done((f32[16,1024]{1,0:T(8,128)S(1)}, f32[16,1024]{1,0:T(8,128)S(1)}, u32[]{:S(2)}, u32[]{:S(2)}) %collective-permute-start.13) | collective-permute-done | bytes 65568 | tf_op jit(solution)/shard_map/ppermute | solution.py:506
  78.5 4.8 %collective-permute-start.14 = (f32[16,1024]{1,0:T(8,128)S(1)}, f32[16,1024]{1,0:T(8,128)S(1)}, u32[]{:S(2)}, u32[]{:S(2)}) collective-permute-start(f32[16,1024]{1,0:T(8,128)S(1)} %add.54.half_ref), channel_id=1, source_target_pairs={{0,1},{1,0},{2,3},{3,2},{4,5},{5,4},{6,7},{7,6},{8,9},{9,8},{10,11... | collective-permute-start | bytes 196616 | tf_op jit(solution)/shard_map/ppermute | solution.py:502
  83.3 1.0 %collective-permute-start.7 = (bf16[5,8,512]{2,1,0:T(8,128)(2,1)S(1)}, bf16[5,8,512]{2,1,0:T(8,128)(2,1)S(1)}, u32[]{:S(2)}, u32[]{:S(2)}) collective-permute-start(bf16[5,8,512]{2,1,0:T(8,128)(2,1)S(1)} %get-tuple-element.26), channel_id=1, source_target_pairs={{0,1},{1,2},{2,3},{3,4},{4,5},{5,6},{6,7},{7,8},{8,9},{9,10},{10,1... | collective-permute-start | bytes 122888 | tf_op jit(solution)/shard_map/ppermute | solution.py:565
  84.4 0.0 copy-start.7
  84.4 0.0 collective-permute-start.8
  84.4 1.1 %collective-permute-done.7.below_ref = bf16[5,8,512]{2,1,0:T(8,128)(2,1)S(1)} collective-permute-done((bf16[5,8,512]{2,1,0:T(8,128)(2,1)S(1)}, bf16[5,8,512]{2,1,0:T(8,128)(2,1)S(1)}, u32[]{:S(2)}, u32[]{:S(2)}) %collective-permute-start.7) | collective-permute-done | bytes 40992 | tf_op jit(solution)/shard_map/ppermute | solution.py:565
  85.5 5.9 %collective-permute-done.8.above_ref = bf16[5,8,512]{2,1,0:T(8,128)(2,1)S(1)} collective-permute-done((bf16[5,8,512]{2,1,0:T(8,128)(2,1)S(1)}, bf16[5,8,512]{2,1,0:T(8,128)(2,1)S(1)}, u32[]{:S(2)}, u32[]{:S(2)}) %collective-permute-start.8) | collective-permute-done | bytes 40992 | tf_op jit(solution)/shard_map/ppermute | solution.py:566
  91.4 0.0 copy-done.1
  91.4 0.0 copy-done.4
  91.4 3.8 %slab.1.field_ref = f32[5,8,32,512]{3,2,1,0:T(8,128)} custom-call(f32[5,8,32,512]{3,2,1,0:T(8,128)S(1)} %copy-done.1, f32[8,32,512]{2,1,0:T(8,128)S(1)} %copy-done.4, bf16[5,8,512]{2,1,0:T(8,128)(2,1)S(1)} %collective-permute-done.7.below_ref, bf16[5,8,512]{2,1,0:T(8,128)(2,1)S(1)} %collective-permute-done.8.above_ref), custom_call_target="tpu_custom_call" | custom-call | tf_op jit(solution)/shard_map/slab/pallas_call | solution.py:445
  95.2 0.0 copy-done.7
  95.2 2.0 %wall.1 = (f32[2,32,512]{2,1,0:T(8,128)}, f32[5,8,32,512]{3,2,1,0:T(8,128)}) custom-call(s32[2]{0:T(128)S(1)} %pad_add_fusion.place_ref, s32[8,128]{1,0:T(8,128)S(1)} %get-tuple-element.23.info_ref, f32[2,2048]{1,0:T(2,128)S(1)} %add_add_fusion.pred_ref.all_ref, f32[2,32,512]{2,1,0:T(8,128)S(1)} %copy-done.7, ...), custom_call_target="tpu_custom_call", output_to_operand_aliasing={{1}: (4, {})} | custom-call | tf_op jit(solution)/shard_map/wall/pallas_call | solution.py:480
  97.1 0.0 collective-permute-done.14.rest_ref
  97.1 1.2 %join.1 = (f32[12,2048]{1,0:T(8,128)}, f32[1,1]{1,0:T(1,128)}) custom-call(s32[2]{0:T(128)S(1)} %pad_add_fusion.place_ref, f32[16,1024]{1,0:T(8,128)S(1)} %add.54.half_ref, f32[16,1024]{1,0:T(8,128)S(1)} %collective-permute-done.14.rest_ref), custom_call_target="tpu_custom_call" | custom-call | tf_op jit(solution)/shard_map/join/pallas_call | solution.py:389
  98.3 0.0 all-to-all-done.1.blocks_ref
  98.3 0.8 lay.1
  (9 shorter events, 0.1 us)
Async XLA Ops:
  0.6 18.7 %copy-start = (bf16[2,2048]{1,0:T(2,128)(2,1)S(1)}, bf16[2,2048]{1,0:T(2,128)(2,1)}, u32[]{:S(2)}) copy-start(bf16[2,2048]{1,0:T(2,128)(2,1)} %param.17) | copy-start | bytes 24580
  0.6 18.7 %copy-start.8 = (bf16[12,2048]{1,0:T(8,128)(2,1)S(1)}, bf16[12,2048]{1,0:T(8,128)(2,1)}, u32[]{:S(2)}) copy-start(bf16[12,2048]{1,0:T(8,128)(2,1)} %weight_ref.3) | copy-start | bytes 147460
  18.0 2.6 %collective-permute-start = (bf16[16,80,128]{2,1,0:T(8,128)(2,1)S(1)}, bf16[16,80,128]{2,1,0:T(8,128)(2,1)S(1)}, u32[]{:S(2)}, u32[]{:S(2)}) collective-permute-start(bf16[16,80,128]{2,1,0:T(8,128)(2,1)S(1)} %all_to_all.10.got_ref.mine_ref), channel_id=1, source_target_pairs={{0,1},{1,0},{2,3},{3,2},{4,5},{5,4},{6,7},{7,6},{8,9},{9,8},{10,11... | collective-permute-start | bytes 983048 | tf_op jit(solution)/shard_map/ppermute | solution.py:502
  26.5 14.0 %copy-start.2 = (f32[128,2048]{1,0:T(8,128)}, f32[128,2048]{1,0:T(8,128)S(1)}, u32[]{:S(2)}) copy-start(f32[128,2048]{1,0:T(8,128)S(1)} %get-tuple-element.32.second_ref) | copy-start | bytes 3145732
  26.5 14.0 %copy-start.5 = (bf16[2048,128]{1,0:T(8,128)(2,1)}, bf16[2048,128]{1,0:T(8,128)(2,1)S(1)}, u32[]{:S(2)}) copy-start(bf16[2048,128]{1,0:T(8,128)(2,1)S(1)} %get-tuple-element.31.weight_ref) | copy-start | bytes 1572868
  26.5 2.7 %collective-permute-start.1 = (f32[2,2048]{1,0:T(2,128)S(1)}, f32[2,2048]{1,0:T(2,128)S(1)}, u32[]{:S(2)}, u32[]{:S(2)}) collective-permute-start(f32[2,2048]{1,0:T(2,128)S(1)} %get-tuple-element.25), channel_id=1, source_target_pairs={{0,2},{2,0},{4,6},{6,4},{8,10},{10,8},{12,14},{14,12},{16,18},{18,... | collective-permute-start | bytes 49160 | tf_op jit(solution)/shard_map/ppermute | solution.py:506
  27.7 2.6 %collective-permute-start.2 = (f32[2,2048]{1,0:T(2,128)S(1)}, f32[2,2048]{1,0:T(2,128)S(1)}, u32[]{:S(2)}, u32[]{:S(2)}) collective-permute-start(f32[2,2048]{1,0:T(2,128)S(1)} %get-tuple-element.25), channel_id=1, source_target_pairs={{0,4},{2,6},{4,0},{6,2},{8,12},{10,14},{12,8},{14,10},{16,20},{18,... | collective-permute-start | bytes 49160 | tf_op jit(solution)/shard_map/ppermute | solution.py:506
  27.8 3.5 %collective-permute-start.3 = (f32[2,2048]{1,0:T(2,128)S(1)}, f32[2,2048]{1,0:T(2,128)S(1)}, u32[]{:S(2)}, u32[]{:S(2)}) collective-permute-start(f32[2,2048]{1,0:T(2,128)S(1)} %get-tuple-element.25), channel_id=1, source_target_pairs={{0,6},{2,4},{4,2},{6,0},{8,14},{10,12},{12,10},{14,8},{16,22},{18,... | collective-permute-start | bytes 49160 | tf_op jit(solution)/shard_map/ppermute | solution.py:506
  31.3 3.6 %collective-permute-start.4 = (f32[2,2048]{1,0:T(2,128)S(1)}, f32[2,2048]{1,0:T(2,128)S(1)}, u32[]{:S(2)}, u32[]{:S(2)}) collective-permute-start(f32[2,2048]{1,0:T(2,128)S(1)} %add_add_fusion.1), channel_id=1, source_target_pairs={{0,8},{2,10},{4,12},{6,14},{8,0},{10,2},{12,4},{14,6},{16,24},{18,... | collective-permute-start | bytes 49160 | tf_op jit(solution)/shard_map/ppermute | solution.py:506
  33.2 2.6 %collective-permute-start.5 = (f32[2,2048]{1,0:T(2,128)S(1)}, f32[2,2048]{1,0:T(2,128)S(1)}, u32[]{:S(2)}, u32[]{:S(2)}) collective-permute-start(f32[2,2048]{1,0:T(2,128)S(1)} %add_add_fusion.1), channel_id=1, source_target_pairs={{0,16},{2,18},{4,20},{6,22},{8,24},{10,26},{12,28},{14,30},{16,0},... | collective-permute-start | bytes 49160 | tf_op jit(solution)/shard_map/ppermute | solution.py:506
  34.0 4.4 %collective-permute-start.6 = (f32[2,2048]{1,0:T(2,128)S(1)}, f32[2,2048]{1,0:T(2,128)S(1)}, u32[]{:S(2)}, u32[]{:S(2)}) collective-permute-start(f32[2,2048]{1,0:T(2,128)S(1)} %add_add_fusion.1), channel_id=1, source_target_pairs={{0,24},{2,26},{4,28},{6,30},{8,16},{10,18},{12,20},{14,22},{16,8},... | collective-permute-start | bytes 49160 | tf_op jit(solution)/shard_map/ppermute | solution.py:506
  40.6 5.4 %collective-permute-start.15 = (f32[16,64,128]{2,1,0:T(8,128)S(1)}, f32[16,64,128]{2,1,0:T(8,128)S(1)}, u32[]{:S(2)}, u32[]{:S(2)}) collective-permute-start(f32[16,64,128]{2,1,0:T(8,128)S(1)} %get-tuple-element.40), channel_id=1, source_target_pairs={{0,1},{1,0},{2,3},{3,2},{4,5},{5,4},{6,7},{7,6},{8,9},{9,8},{10,11... | collective-permute-start | bytes 1572872 | tf_op jit(solution)/shard_map/ppermute | solution.py:502
  46.0 45.4 %copy-start.1 = (f32[5,8,32,512]{3,2,1,0:T(8,128)S(1)}, f32[5,8,32,512]{3,2,1,0:T(8,128)}, u32[]{:S(2)}) copy-start(f32[5,8,32,512]{3,2,1,0:T(8,128)} %flow_ref.3) | copy-start | bytes 7864324
  46.8 51.5 %all-to-all-start.1 = ((f32[16,64,128]{2,1,0:T(8,128)}), f32[16,64,128]{2,1,0:T(8,128)S(1)}, u32[]{:S(2)}, u32[]{:S(2)}) async-start(f32[16,64,128]{2,1,0:T(8,128)} %add.55), calls=%async_computation.1 | async-start | bytes 1048576 | tf_op jit(solution)/shard_map/all_to_all | solution.py:523
  52.9 1.2 %copy-start.3 = (f32[128,2048]{1,0:T(8,128)S(1)}, f32[128,2048]{1,0:T(8,128)}, u32[]{:S(2)}) copy-start(f32[128,2048]{1,0:T(8,128)} %copy-done.2) | copy-start | bytes 3145732
  54.1 1.0 %copy-start.6 = (bf16[2048,128]{1,0:T(8,128)(2,1)S(1)}, bf16[2048,128]{1,0:T(8,128)(2,1)}, u32[]{:S(2)}) copy-start(bf16[2048,128]{1,0:T(8,128)(2,1)} %copy-done.5) | copy-start | bytes 1572868
  55.2 36.2 %copy-start.4 = (f32[8,32,512]{2,1,0:T(8,128)S(1)}, f32[8,32,512]{2,1,0:T(8,128)}, u32[]{:S(2)}) copy-start(f32[8,32,512]{2,1,0:T(8,128)} %diff_ref.1) | copy-start | bytes 1572868
  62.1 1.8 %collective-permute-start.9 = (f32[16,1024]{1,0:T(8,128)S(1)}, f32[16,1024]{1,0:T(8,128)S(1)}, u32[]{:S(2)}, u32[]{:S(2)}) collective-permute-start(f32[16,1024]{1,0:T(8,128)S(1)} %get-tuple-element.35), channel_id=1, source_target_pairs={{0,1},{1,0},{2,3},{3,2},{4,5},{5,4},{6,7},{7,6},{8,9},{9,8},{10,11... | collective-permute-start | bytes 196616 | tf_op jit(solution)/shard_map/ppermute | solution.py:502
  63.9 3.2 %collective-permute-start.10 = (f32[16,1024]{1,0:T(8,128)S(1)}, f32[16,1024]{1,0:T(8,128)S(1)}, u32[]{:S(2)}, u32[]{:S(2)}) collective-permute-start(f32[16,1024]{1,0:T(8,128)S(1)} %add.50), channel_id=1, source_target_pairs={{0,2},{2,0},{4,6},{6,4},{8,10},{10,8},{12,14},{14,12},{16,18},{18,... | collective-permute-start | bytes 196616 | tf_op jit(solution)/shard_map/ppermute | solution.py:506
  67.1 3.2 %collective-permute-start.11 = (f32[16,1024]{1,0:T(8,128)S(1)}, f32[16,1024]{1,0:T(8,128)S(1)}, u32[]{:S(2)}, u32[]{:S(2)}) collective-permute-start(f32[16,1024]{1,0:T(8,128)S(1)} %add.51), channel_id=1, source_target_pairs={{0,4},{2,6},{4,0},{6,2},{8,12},{10,14},{12,8},{14,10},{16,20},{18,... | collective-permute-start | bytes 196616 | tf_op jit(solution)/shard_map/ppermute | solution.py:506
  70.3 4.8 %collective-permute-start.12 = (f32[16,1024]{1,0:T(8,128)S(1)}, f32[16,1024]{1,0:T(8,128)S(1)}, u32[]{:S(2)}, u32[]{:S(2)}) collective-permute-start(f32[16,1024]{1,0:T(8,128)S(1)} %add.52), channel_id=1, source_target_pairs={{0,8},{2,10},{4,12},{6,14},{8,0},{10,2},{12,4},{14,6},{16,24},{18,... | collective-permute-start | bytes 196616 | tf_op jit(solution)/shard_map/ppermute | solution.py:506
  75.1 3.4 %collective-permute-start.13 = (f32[16,1024]{1,0:T(8,128)S(1)}, f32[16,1024]{1,0:T(8,128)S(1)}, u32[]{:S(2)}, u32[]{:S(2)}) collective-permute-start(f32[16,1024]{1,0:T(8,128)S(1)} %add.53), channel_id=1, source_target_pairs={{0,16},{2,18},{4,20},{6,22},{8,24},{10,26},{12,28},{14,30},{16,0},... | collective-permute-start | bytes 196616 | tf_op jit(solution)/shard_map/ppermute | solution.py:506
  78.5 18.6 %collective-permute-start.14 = (f32[16,1024]{1,0:T(8,128)S(1)}, f32[16,1024]{1,0:T(8,128)S(1)}, u32[]{:S(2)}, u32[]{:S(2)}) collective-permute-start(f32[16,1024]{1,0:T(8,128)S(1)} %add.54.half_ref), channel_id=1, source_target_pairs={{0,1},{1,0},{2,3},{3,2},{4,5},{5,4},{6,7},{7,6},{8,9},{9,8},{10,11... | collective-permute-start | bytes 196616 | tf_op jit(solution)/shard_map/ppermute | solution.py:502
  83.3 2.1 %collective-permute-start.7 = (bf16[5,8,512]{2,1,0:T(8,128)(2,1)S(1)}, bf16[5,8,512]{2,1,0:T(8,128)(2,1)S(1)}, u32[]{:S(2)}, u32[]{:S(2)}) collective-permute-start(bf16[5,8,512]{2,1,0:T(8,128)(2,1)S(1)} %get-tuple-element.26), channel_id=1, source_target_pairs={{0,1},{1,2},{2,3},{3,4},{4,5},{5,6},{6,7},{7,8},{8,9},{9,10},{10,1... | collective-permute-start | bytes 122888 | tf_op jit(solution)/shard_map/ppermute | solution.py:565
  84.4 10.8 %copy-start.7 = (f32[2,32,512]{2,1,0:T(8,128)S(1)}, f32[2,32,512]{2,1,0:T(8,128)}, u32[]{:S(2)}) copy-start(f32[2,32,512]{2,1,0:T(8,128)} %stress_ref.1) | copy-start | bytes 393220
  84.4 7.0 %collective-permute-start.8 = (bf16[5,8,512]{2,1,0:T(8,128)(2,1)S(1)}, bf16[5,8,512]{2,1,0:T(8,128)(2,1)S(1)}, u32[]{:S(2)}, u32[]{:S(2)}) collective-permute-start(bf16[5,8,512]{2,1,0:T(8,128)(2,1)S(1)} %get-tuple-element.27), channel_id=1, source_target_pairs={{1,0},{2,1},{3,2},{4,3},{5,4},{6,5},{7,6},{8,7},{9,8},{10,9},{11,1... | collective-permute-start | bytes 122888 | tf_op jit(solution)/shard_map/ppermute | solution.py:566

commit v3 on v2

--- a/solution.py
+++ b/solution.py
@@ -22,6 +22,7 @@
 FEATURES = 12
 CHANNELS = 14
 ROWS = 16
+TAIL = ROWS - FEATURES
 
 CHIPS = ("sec", "chip")
 EVERY = ("sec", "chip", "core")
@@ -35,10 +36,6 @@
     return lax.dot_general(left, right, dims, preferred_element_type=jnp.float32)
 
 
-def round_up(value, step):
-    return -(-value // step) * step
-
-
 def iota(shape, axis):
     return lax.broadcasted_iota(jnp.int32, shape, axis)
 
@@ -48,11 +45,8 @@
 
 
 def pick_kernel(
-    counts_ref, routes_ref, index_ref, flow_ref, low_ref, high_ref, weight_ref,
-    rows_ref, info_ref, first_ref, last_ref, *block_ref, nx,
+    counts_ref, routes_ref, index_ref, flow_ref, weight_ref, rows_ref, info_ref, *block_ref, nx
 ):
-    first_ref[...] = low_ref[:, :, 0].astype(jnp.bfloat16)
-    last_ref[...] = high_ref[:, :, high_ref.shape[2] - 1].astype(jnp.bfloat16)
     tiles = counts_ref.shape[1]
     nz = flow_ref.shape[2]
     lanes = rows_ref.shape[2]
@@ -101,14 +95,11 @@
 
 def pick_samples(counts, routes, index, flow, weight, lanes, joint):
     capacity, tiles = index.shape
-    nv, nl, nz, nx = flow.shape
-    assert nx & (nx - 1) == 0 and nz % 8 == 0
-    plane = jax.ShapeDtypeStruct((nv, nl, nx), jnp.bfloat16)
+    nz, nx = flow.shape[2:]
+    assert nx & (nx - 1) == 0
     outs = [
         jax.ShapeDtypeStruct((1, ROWS, lanes), jnp.bfloat16),
         jax.ShapeDtypeStruct((8, lanes), jnp.int32),
-        plane,
-        plane,
     ]
     if joint is not None:
         outs.append(jax.ShapeDtypeStruct(joint, jnp.bfloat16))
@@ -120,15 +111,35 @@
             whole((1, tiles)),
             whole((capacity, tiles)),
             whole((4, 5, nz, nx)),
+            whole(weight.shape),
+        ],
+        out_specs=[whole(out.shape) for out in outs],
+        out_shape=outs,
+        compiler_params=params(10),
+        name="pick",
+    )(counts, routes, index, flow, weight)
+
+
+def edge_kernel(low_ref, high_ref, first_ref, last_ref):
+    first_ref[...] = low_ref[:, :, 0].astype(jnp.bfloat16)
+    last_ref[...] = high_ref[:, :, high_ref.shape[2] - 1].astype(jnp.bfloat16)
+
+
+def edge_planes(flow):
+    nv, nl, nz, nx = flow.shape
+    plane = jax.ShapeDtypeStruct((nv, nl, nx), jnp.bfloat16)
+    return pl.pallas_call(
+        edge_kernel,
+        grid=(1,),
+        in_specs=[
             whole((nv, nl, 8, nx)),
             pl.BlockSpec((nv, nl, 8, nx), lambda i: (0, 0, nz // 8 - 1, 0)),
-            whole(weight.shape),
-        ],
-        out_specs=[whole(out.shape) for out in outs],
-        out_shape=outs,
-        compiler_params=params(16),
-        name="pick",
-    )(counts, routes, index, flow, flow, flow, weight)
+        ],
+        out_specs=[whole(plane.shape), whole(plane.shape)],
+        out_shape=[plane, plane],
+        compiler_params=params(8),
+        name="edge",
+    )(flow, flow)
 
 
 def widen_kernel(weight_ref, out_ref):
@@ -168,7 +179,7 @@
             at = pl.multiple_of((CORES * j + core) * rows, rows)
             weight_ref[pl.ds(at, rows), :] = mine_ref[j]
             at = pl.multiple_of((CORES * j + 1 - core) * rows, rows)
-            weight_ref[pl.ds(at, rows), :] = other_ref[j]
+            weight_ref[pl.ds(at, rows), :] = other_ref[j, :rows]
 
     hidden = weight_ref.shape[0]
     rows_ref[...] = got_ref[...]
@@ -213,13 +224,13 @@
             pl.BlockSpec(memory_space=pltpu.SMEM),
             pl.BlockSpec((group, ROWS, lanes), lambda i: (i, skip, 0)),
             whole((chips, rows_dev, width)),
-            whole((chips, rows_dev, width)),
+            whole(other.shape),
             whole(win.shape),
             whole(wout.shape),
         ],
         out_specs=out_specs,
         out_shape=out_shape,
-        compiler_params=params(28),
+        compiler_params=params(20),
         name="forward",
     )(place, got, mine, other, win, wout)
 
@@ -292,14 +303,14 @@
         out_specs=[whole(blocks.shape), whole(blocks.shape)],
         out_shape=[blocks, blocks],
         scratch_shapes=[pltpu.VMEM((width, hidden), jnp.float32)],
-        compiler_params=params(16),
+        compiler_params=params(14),
         name="middle",
     )(place, rows, win, wout, second, pred, *first)
 
 
 def input_kernel(
     place_ref, rows_ref, win_ref, wout_ref, weight_ref, second_ref, pred_ref, all_ref, own_ref,
-    info_ref, stay_ref, send_ref, gin_ref, *, step, live, scale, devices,
+    info_ref, stay_ref, send_ref, gin_ref, *, step, live, scale,
 ):
     @pl.when(pl.program_id(0) == 0)
     def _():
@@ -311,11 +322,10 @@
         route = info_ref[1:2].astype(jnp.float32)
         side = iota((8, lanes), 0)
         both = jnp.where(side == 0, route, squares).T
-        across = round_up(devices, LANE)
-        match = both[:, 0:1] == iota((lanes, across), 1).astype(jnp.float32)
+        match = both[:, 0:1] == iota((lanes, LANE), 1).astype(jnp.float32)
         loss = jnp.sum(jnp.where(match, both[:, 1:2], 0.0), axis=0, keepdims=True)
         count = jnp.sum(jnp.where(match, 1.0, 0.0), axis=0, keepdims=True)
-        gin_ref[FEATURES:CHANNELS, :across] = jnp.concatenate([loss, count], axis=0)
+        gin_ref[FEATURES:CHANNELS, :LANE] = jnp.concatenate([loss, count], axis=0)
 
     hidden = win_ref.shape[1]
     across, features = features_of(rows_ref)
@@ -333,7 +343,11 @@
 
     @pl.when(pl.program_id(0) == pl.num_programs(0) - 1)
     def _():
-        low, high = gin_ref[:, : hidden // CORES], gin_ref[:, hidden // CORES :]
+        cuts = [gin_ref[:FEATURES, at : at + LANE] for at in range(0, hidden, LANE)]
+        cut = len(cuts) // CORES
+        tail = gin_ref[FEATURES : FEATURES + TAIL, :LANE]
+        low = jnp.concatenate(cuts[:cut] + [tail], axis=0)
+        high = jnp.concatenate(cuts[cut:] + [jnp.zeros_like(tail)], axis=0)
         first = place_ref[0] == 0
         stay_ref[...] = jnp.where(first, low, high)
         send_ref[...] = jnp.where(first, high, low)
@@ -345,11 +359,12 @@
     chips, _, lanes = rows.shape
     hidden, width = weight.shape
     tile = group * lanes
-    half = jax.ShapeDtypeStruct((ROWS, hidden // CORES), jnp.float32)
-    return pl.pallas_call(
-        functools.partial(
-            input_kernel, step=min(hidden, STEP), live=live, scale=scale, devices=devices
-        ),
+    assert hidden % (CORES * LANE) == 0 and devices <= LANE
+    half = jax.ShapeDtypeStruct(
+        (FEATURES * (hidden // CORES // LANE) + TAIL, LANE), jnp.float32
+    )
+    return pl.pallas_call(
+        functools.partial(input_kernel, step=min(hidden, STEP), live=live, scale=scale),
         grid=(chips // group,),
         in_specs=[
             pl.BlockSpec(memory_space=pltpu.SMEM),
@@ -366,7 +381,7 @@
         out_specs=[whole(half.shape), whole(half.shape)],
         out_shape=[half, half],
         scratch_shapes=[pltpu.VMEM((ROWS, hidden), jnp.float32)],
-        compiler_params=params(16),
+        compiler_params=params(14),
         name="input",
     )(place, rows, win, wout, weight, second, pred, pred, own, info)
 
@@ -375,17 +390,19 @@
     first = place_ref[0] == 0
     half, rest = half_ref[...], rest_ref[...]
     low, high = jnp.where(first, half, rest), jnp.where(first, rest, half)
-    across = low.shape[1]
-    gin_ref[:, :across] = low[:FEATURES]
-    gin_ref[:, across:] = high[:FEATURES]
-    mine = iota((1, across), 1) == place_ref[1] * CORES + place_ref[0]
-    loss = jnp.sum(jnp.where(mine, low[FEATURES : FEATURES + 1], 0.0), axis=1, keepdims=True)
-    count = jnp.sum(jnp.where(mine, low[FEATURES + 1 : CHANNELS], 0.0), axis=1, keepdims=True)
+    count = (low.shape[0] - TAIL) // FEATURES
+    for i, part in enumerate((low, high)):
+        for j in range(count):
+            at = (i * count + j) * LANE
+            gin_ref[:, at : at + LANE] = part[j * FEATURES : (j + 1) * FEATURES]
+    mine = iota((TAIL, LANE), 1) == place_ref[1] * CORES + place_ref[0]
+    sums = jnp.sum(jnp.where(mine, low[count * FEATURES :], 0.0), axis=1, keepdims=True)
+    loss, count = sums[0:1], sums[1:2]
     loss_ref[...] = loss / count
 
 
 def join_halves(place, half, rest):
-    across = half.shape[1] * CORES
+    across = (half.shape[0] - TAIL) // FEATURES * LANE * CORES
     return pl.pallas_call(
         join_kernel,
         grid=(1,),
@@ -419,38 +436,67 @@
     )(blocks)
 
 
-def slab_kernel(flow_ref, diff_ref, below_ref, above_ref, out_ref):
+def slab_kernel(flow_ref, diff_ref, out_ref):
     layers, nz, nx = flow_ref.shape[1:]
     at_z, at_x = iota((nz, nx), 0), iota((nz, nx), 1)
     first_z, last_z = at_z == 0, at_z == nz - 1
     first_x, last_x = at_x == 0, at_x == nx - 1
-    below_edge = below_ref[0].astype(jnp.float32)
-    above_edge = above_ref[0].astype(jnp.float32)
     for l in range(layers):
         mid = flow_ref[0, l]
         below_x = jnp.where(first_x, mid, pltpu.roll(mid, 1, 1))
         above_x = jnp.where(last_x, mid, pltpu.roll(mid, nx - 1, 1))
-        below_z = jnp.where(first_z, below_edge[l : l + 1], pltpu.roll(mid, 1, 0))
-        above_z = jnp.where(last_z, above_edge[l : l + 1], pltpu.roll(mid, nz - 1, 0))
+        below_z = jnp.where(first_z, 0.0, pltpu.roll(mid, 1, 0))
+        above_z = jnp.where(last_z, 0.0, pltpu.roll(mid, nz - 1, 0))
         below_y = flow_ref[0, max(l - 1, 0)]
         above_y = flow_ref[0, min(l + 1, layers - 1)]
         spread = below_x + above_x + below_y + above_y + below_z + above_z - 6.0 * mid
         out_ref[0, l] = mid + advect_number * (below_x - mid) + diff_ref[l] * spread
 
 
-def slab(flow, diff, below, above):
+def slab(flow, diff):
     vars_, layers, nz, nx = flow.shape
     block = pl.BlockSpec((1, layers, nz, nx), lambda v: (v, 0, 0, 0))
-    edge = pl.BlockSpec((1, layers, nx), lambda v: (v, 0, 0))
     return pl.pallas_call(
         slab_kernel,
         grid=(vars_,),
-        in_specs=[block, pl.BlockSpec((layers, nz, nx), lambda v: (0, 0, 0)), edge, edge],
+        in_specs=[block, pl.BlockSpec((layers, nz, nx), lambda v: (0, 0, 0))],
         out_specs=block,
         out_shape=jax.ShapeDtypeStruct(flow.shape, flow.dtype),
-        compiler_params=params(16),
+        compiler_params=params(8),
         name="slab",
-    )(flow, diff, below, above)
+    )(flow, diff)
+
+
+def rim_kernel(below_ref, above_ref, diff_ref, field_ref, out_ref):
+    low = pl.program_id(0) == 0
+    rows = field_ref.shape[2]
+    edge = jnp.where(low, below_ref[...], above_ref[...]).astype(jnp.float32)
+    row = jnp.where(low, 0, rows - 1)
+    hit = iota((rows, field_ref.shape[3]), 0) == row
+    diff = jnp.where(hit, diff_ref[...], 0.0)
+    out_ref[...] = field_ref[...] + diff[None] * edge[:, :, None, :]
+
+
+def rim(below, above, diff, field):
+    vars_, layers, nz, nx = field.shape
+    assert nz % 8 == 0 and nz >= 16
+    last = nz // 8 - 1
+    block = pl.BlockSpec((vars_, layers, 8, nx), lambda i: (0, 0, i * last, 0))
+    return pl.pallas_call(
+        rim_kernel,
+        grid=(2,),
+        in_specs=[
+            whole(below.shape),
+            whole(above.shape),
+            pl.BlockSpec((layers, 8, nx), lambda i: (0, i * last, 0)),
+            block,
+        ],
+        out_specs=block,
+        out_shape=jax.ShapeDtypeStruct(field.shape, field.dtype),
+        input_output_aliases={3: 0},
+        compiler_params=params(6),
+        name="rim",
+    )(below, above, diff, field)
 
 
 def wall_kernel(place_ref, info_ref, pred_ref, stress_ref, field_ref, stress_out, field_out):
@@ -506,9 +552,11 @@
     return lax.ppermute(block, CHIPS, [(i, i ^ mask) for i in range(chips)])
 
 
-def sum_chips(block, chips, most):
+def sum_chips(block, chips, fans):
     mask = 1
-    while mask < chips:
+    for most in fans + fans[-1:] * chips:
+        if mask == chips:
+            break
         fan = min(most, chips // mask)
         others = [flip(block, k * mask, chips) for k in range(1, fan)]
         if fan == 4:
@@ -553,7 +601,7 @@
     place = jnp.stack([core, chip]).astype(jnp.int32)
     joint = lanes == width and rows_dev % ROWS == 0
     far = lambda array: pltpu.with_memory_space_constraint(array, pltpu.HBM)
-    own, info, first_z, last_z, *blocks = pick_samples(
+    own, info, *blocks = pick_samples(
         far(batch_counts),
         far(batch_routes.reshape(1, tile_count)),
         far(wall_index.T),
@@ -562,6 +610,8 @@
         lanes,
         (chips, rows_dev + ROWS, width) if joint else None,
     )
+    blocks = [far(b) for b in blocks]
+    first_z, last_z = edge_planes(flow_state)
     below = lax.ppermute(last_z, EVERY, order)
     above = lax.ppermute(first_z, EVERY, back_order)
     if joint:
@@ -574,7 +624,7 @@
         got, skip = None, 0
     if not joint:
         got = exchange(jnp.broadcast_to(own, (chips, ROWS, lanes)))
-    other = swap_cores(mine)
+    other = pltpu.with_memory_space_constraint(swap_cores(mine), pltpu.VMEM)
 
     win = widen(input_weight)
     wout = lax.dynamic_slice_in_dim(output_weight, chip * width, width, axis=1)
@@ -582,7 +632,7 @@
     second, part, rows, weight, *first = forward(
         place, got, skip, mine, other, win, wout, rows_dev, group, keep
     )
-    pred = sum_chips(part, chips, 4)
+    pred = sum_chips(part, chips, (4,))
 
     stay, send = middle_gradient(
         place, rows, win, wout, second, pred, first, rows_dev, group, live_dev, scale
@@ -595,12 +645,13 @@
         place, rows, win, wout, weight, second, pred, own, info, group, live_dev, scale, devices
     )
     half = stay + swap_cores(send)
-    half = sum_chips(half, chips, 2)
+    half = sum_chips(half, chips, (4, 2))
     rest = swap_cores(half)
     grad_w_in, loss = join_halves(place, half, rest)
     batch_loss = loss.reshape(1)
 
-    field = slab(flow_state, diffusion, below, above)
+    field = slab(flow_state, diffusion)
+    field = rim(below, above, far(diffusion), field)
     new_stress, new_field = wall(place, info, pred, wall_stress, field)
     return (new_field, new_stress, batch_loss, grad_w_in, grad_w_mid)
 
@@ -626,4 +677,6 @@
         P(),
         P(EVERY, None),
     )
-    return jax.shard_map(step, mesh=inner, in_specs=in_specs, out_specs=out_specs, check_vma=False)
+    return jax.shard_map(
+        step, mesh=inner, in_specs=in_specs, out_specs=out_specs, check_vma=False
+    )

time: 99.6 us -> 99.6 us (level)
  the two profiles are of different devices: /device:TPU:27 before, /device:TPU:0 now
where the time goes in v3:
time: 99.6 us; the launch traced here: 99.1 us
  Pallas kernels  28 us (28%)
  starting transfers between devices  26.4 us (27%)
  waiting for transfers between devices  21.1 us (21%)
  blocking collectives  19.5 us (20%)
  local copies, waits for them, and re-layouts  2.31 us (2%)
  other arithmetic  1.01 us (1%)
    all_to_all x1, blocking collectives, exchange(): lax.all_to_all(blocks, CHIPS, split_axis=0, concat_axis=0, tiled=True)  19.5 us
    ppermute x11, waiting for transfers between devices, flip(): return lax.ppermute(block, CHIPS, [(i, i ^ mask) for i in range(chips)])  16.4 us
    ppermute x11, starting transfers between devices, flip(): return lax.ppermute(block, CHIPS, [(i, i ^ mask) for i in range(chips)])  15.5 us
    pallas_call x1, Pallas kernels, input_gradient(): pl.pallas_call(functools.partial(input_kernel, step=min(hidden, STEP), li...  6.92 us
    pallas_call x1, Pallas kernels, forward(): pl.pallas_call(functools.partial(forward_kernel, step=min(hidden, STEP)),...  6.4 us
    all_to_all x1, starting transfers between devices, exchange(): lax.all_to_all(blocks, CHIPS, split_axis=0, concat_axis=0, tiled=True)  5.37 us
    ppermute x1, starting transfers between devices, step(): above = lax.ppermute(first_z, EVERY, back_order)  4.86 us
    ppermute x4, waiting for transfers between devices, swap_cores(): return lax.ppermute(block, 'core', [(0, 1), (1, 0)])  4.63 us
  transfers between devices with their start and end apart: 18, of which 14 were waited for; matrix products, arithmetic and copies ran while one was open for 0% of the time, Pallas kernels for 17%

profile of v3, /device:TPU:0, one launch (start us, length us, event | category | flops | bytes accessed | tf_op | source)
XLA Modules:
  0.0 99.1 jit_solution(8376213192496830477)
XLA Ops:
  0.6 0.0 copy-start
  0.6 0.0 copy-start.8
  0.7 2.1 %pick.1 = (bf16[1,16,128]{2,1,0:T(8,128)(2,1)S(1)}, s32[8,128]{1,0:T(8,128)S(1)}, bf16[16,80,128]{2,1,0:T(8,128)(2,1)S(1)}) custom-call(s32[1,48]{1,0:T(1,128)} %counts_ref.1, s32[1,48]{1,0:T(1,128)} %bitcast.6, s32[4,48]{1,0:T(4,128)} %bitcast.5, f32[5,8,32,512]{3,2,1,0:T(8,128)} %flow_ref.3, bf16[64,2048]{1,0:T(8,128)(2,1)} %weight_ref.2), custom_call_target="tpu_custom_call" | custom-call | tf_op jit(solution)/shard_map/pick/pallas_call | solution.py:106
  2.8 19.5 %all_to_all.10.got_ref.mine_ref = bf16[16,80,128]{2,1,0:T(8,128)(2,1)S(1)} all-to-all(bf16[16,80,128]{2,1,0:T(8,128)(2,1)S(1)} %get-tuple-element.24), channel_id=1, replica_groups=mesh['sec'=2,'chip'=8,'core'=2] {'sec','chip'}, dimensions={0} | all-to-all | bytes 655360 | tf_op jit(solution)/shard_map/all_to_all | solution.py:571
  22.2 0.0 collective-permute-start
  22.2 0.0 copy-done.8
  22.3 0.0 copy-done
  22.3 0.1 pad_add_fusion.place_ref
  22.4 1.5 %collective-permute-done.other_ref = bf16[16,80,128]{2,1,0:T(8,128)(2,1)S(1)} collective-permute-done((bf16[16,80,128]{2,1,0:T(8,128)(2,1)S(1)}, bf16[16,80,128]{2,1,0:T(8,128)(2,1)S(1)}, u32[]{:S(2)}, u32[]{:S(2)}) %collective-permute-start) | collective-permute-done | bytes 327712 | tf_op jit(solution)/shard_map/ppermute | solution.py:548
  23.9 0.0 copy-done.9
  23.9 6.4 %forward.1 = (f32[128,2048]{1,0:T(8,128)S(1)}, f32[2,2048]{1,0:T(2,128)S(1)}, bf16[16,16,128]{2,1,0:T(8,128)(2,1)S(1)}, bf16[2048,128]{1,0:T(8,128)(2,1)S(1)}, bf16[2048,2048]{1,0:T(8,128)(2,1)S(1)}) custom-call(s32[2]{0:T(128)S(1)} %pad_add_fusion.place_ref, bf16[16,80,128]{2,1,0:T(8,128)(2,1)} %copy-done.9, bf16[16,80,128]{2,1,0:T(8,128)(2,1)} %copy-done.9, ...), custom_call_target="tpu_custom_call" | custom-call | tf_op jit(solution)/shard_map/forward/pallas_call | solution.py:220
  30.3 0.6 collective-permute-start.1
  30.9 0.8 collective-permute-start.2
  31.7 2.1 %collective-permute-start.3 = (f32[2,2048]{1,0:T(2,128)S(1)}, f32[2,2048]{1,0:T(2,128)S(1)}, u32[]{:S(2)}, u32[]{:S(2)}) collective-permute-start(f32[2,2048]{1,0:T(2,128)S(1)} %get-tuple-element.25), channel_id=1, source_target_pairs={{0,6},{2,4},{4,2},{6,0},{8,14},{10,12},{12,10},{14,8},{16,22},{18,... | collective-permute-start | bytes 49160 | tf_op jit(solution)/shard_map/ppermute | solution.py:552
  33.8 0.2 collective-permute-done.1
  34.1 0.6 collective-permute-done.2
  34.6 1.7 %collective-permute-done.3 = f32[2,2048]{1,0:T(2,128)S(1)} collective-permute-done((f32[2,2048]{1,0:T(2,128)S(1)}, f32[2,2048]{1,0:T(2,128)S(1)}, u32[]{:S(2)}, u32[]{:S(2)}) %collective-permute-start.3) | collective-permute-done | bytes 16416 | tf_op jit(solution)/shard_map/ppermute | solution.py:552
  36.3 1.7 %collective-permute-start.4 = (f32[2,2048]{1,0:T(2,128)S(1)}, f32[2,2048]{1,0:T(2,128)S(1)}, u32[]{:S(2)}, u32[]{:S(2)}) collective-permute-start(f32[2,2048]{1,0:T(2,128)S(1)} %add_add_fusion.2), channel_id=1, source_target_pairs={{0,8},{2,10},{4,12},{6,14},{8,0},{10,2},{12,4},{14,6},{16,24},{18,... | collective-permute-start | bytes 49160 | tf_op jit(solution)/shard_map/ppermute | solution.py:552
  38.1 0.3 collective-permute-start.5
  38.4 2.4 %collective-permute-start.6 = (f32[2,2048]{1,0:T(2,128)S(1)}, f32[2,2048]{1,0:T(2,128)S(1)}, u32[]{:S(2)}, u32[]{:S(2)}) collective-permute-start(f32[2,2048]{1,0:T(2,128)S(1)} %add_add_fusion.2), channel_id=1, source_target_pairs={{0,24},{2,26},{4,28},{6,30},{8,16},{10,18},{12,20},{14,22},{16,8},... | collective-permute-start | bytes 49160 | tf_op jit(solution)/shard_map/ppermute | solution.py:552
  40.8 0.5 collective-permute-done.4
  41.3 0.5 collective-permute-done.5
  41.8 2.1 %collective-permute-done.6 = f32[2,2048]{1,0:T(2,128)S(1)} collective-permute-done((f32[2,2048]{1,0:T(2,128)S(1)}, f32[2,2048]{1,0:T(2,128)S(1)}, u32[]{:S(2)}, u32[]{:S(2)}) %collective-permute-start.6) | collective-permute-done | bytes 16416 | tf_op jit(solution)/shard_map/ppermute | solution.py:552
  43.9 2.2 %middle.1 = (f32[16,64,128]{2,1,0:T(8,128)S(1)}, f32[16,64,128]{2,1,0:T(8,128)S(1)}) custom-call(s32[2]{0:T(128)S(1)} %pad_add_fusion.place_ref, bf16[16,16,128]{2,1,0:T(8,128)(2,1)S(1)} %get-tuple-element.30.rows_ref, bf16[16,2048]{1,0:T(8,128)(2,1)S(1)} %widen.1.win_ref, bf16[2,128]{1,0:T(2,128)(2,1)S(1)} %constant_dynamic-slice_fusion.wout_ref, ...), custom_call_target="tpu_custom_call" | custom-call | tf_op jit(solution)/shard_map/middle/pallas_call | solution.py:289
  46.1 0.0 copy-done.2
  46.1 0.0 copy-done.5
  46.1 0.0 copy-start.1
  46.1 0.1 collective-permute-start.16
  46.2 1.9 %collective-permute-done.16 = f32[16,64,128]{2,1,0:T(8,128)S(1)} collective-permute-done((f32[16,64,128]{2,1,0:T(8,128)S(1)}, f32[16,64,128]{2,1,0:T(8,128)S(1)}, u32[]{:S(2)}, u32[]{:S(2)}) %collective-permute-start.16) | collective-permute-done | bytes 524320 | tf_op jit(solution)/shard_map/ppermute | solution.py:548
  48.1 0.9 add.59
  49.0 5.4 %all-to-all-start.1 = ((f32[16,64,128]{2,1,0:T(8,128)}), f32[16,64,128]{2,1,0:T(8,128)S(1)}, u32[]{:S(2)}, u32[]{:S(2)}) async-start(f32[16,64,128]{2,1,0:T(8,128)} %add.59), calls=%async_computation.1 | async-start | bytes 1048576 | tf_op jit(solution)/shard_map/all_to_all | solution.py:571
  54.4 0.0 copy-start.3
  54.4 1.2 %copy-done.3 = f32[128,2048]{1,0:T(8,128)S(1)} copy-done((f32[128,2048]{1,0:T(8,128)S(1)}, f32[128,2048]{1,0:T(8,128)}, u32[]{:S(2)}) %copy-start.3) | copy-done | bytes 1048600
  55.6 1.0 %copy-done.6 = bf16[2048,128]{1,0:T(8,128)(2,1)S(1)} copy-done((bf16[2048,128]{1,0:T(8,128)(2,1)S(1)}, bf16[2048,128]{1,0:T(8,128)(2,1)}, u32[]{:S(2)}) %copy-start.6) | copy-done | bytes 524312
  56.6 6.9 %input.1 = (f32[100,128]{1,0:T(8,128)S(1)}, f32[100,128]{1,0:T(8,128)S(1)}) custom-call(s32[2]{0:T(128)S(1)} %pad_add_fusion.place_ref, bf16[16,16,128]{2,1,0:T(8,128)(2,1)S(1)} %get-tuple-element.30.rows_ref, bf16[16,2048]{1,0:T(8,128)(2,1)S(1)} %widen.1.win_ref, bf16[2,128]{1,0:T(2,128)(2,1)S(1)} %constant_dynamic-slice_fusion.wout_ref, ...), custom_call_target="tpu_custom_call" | custom-call | tf_op jit(solution)/shard_map/input/pallas_call | solution.py:366
  63.6 0.0 collective-permute-start.9
  63.6 1.2 %collective-permute-done.9 = f32[100,128]{1,0:T(8,128)S(1)} collective-permute-done((f32[100,128]{1,0:T(8,128)S(1)}, f32[100,128]{1,0:T(8,128)S(1)}, u32[]{:S(2)}, u32[]{:S(2)}) %collective-permute-start.9) | collective-permute-done | bytes 51232 | tf_op jit(solution)/shard_map/ppermute | solution.py:548
  64.8 2.0 %collective-permute-start.10 = (f32[100,128]{1,0:T(8,128)S(1)}, f32[100,128]{1,0:T(8,128)S(1)}, u32[]{:S(2)}, u32[]{:S(2)}) collective-permute-start(f32[100,128]{1,0:T(8,128)S(1)} %add.53), channel_id=1, source_target_pairs={{0,2},{2,0},{4,6},{6,4},{8,10},{10,8},{12,14},{14,12},{16,18},{18,... | collective-permute-start | bytes 153608 | tf_op jit(solution)/shard_map/ppermute | solution.py:552
  66.8 1.5 %collective-permute-start.11 = (f32[100,128]{1,0:T(8,128)S(1)}, f32[100,128]{1,0:T(8,128)S(1)}, u32[]{:S(2)}, u32[]{:S(2)}) collective-permute-start(f32[100,128]{1,0:T(8,128)S(1)} %add.53), channel_id=1, source_target_pairs={{0,4},{2,6},{4,0},{6,2},{8,12},{10,14},{12,8},{14,10},{16,20},{18,... | collective-permute-start | bytes 153608 | tf_op jit(solution)/shard_map/ppermute | solution.py:552
  68.3 0.1 collective-permute-start.12
  68.4 1.0 collective-permute-done.10
  69.3 2.1 %collective-permute-done.11 = f32[100,128]{1,0:T(8,128)S(1)} collective-permute-done((f32[100,128]{1,0:T(8,128)S(1)}, f32[100,128]{1,0:T(8,128)S(1)}, u32[]{:S(2)}, u32[]{:S(2)}) %collective-permute-start.11) | collective-permute-done | bytes 51232 | tf_op jit(solution)/shard_map/ppermute | solution.py:552
  71.4 1.8 %collective-permute-done.12 = f32[100,128]{1,0:T(8,128)S(1)} collective-permute-done((f32[100,128]{1,0:T(8,128)S(1)}, f32[100,128]{1,0:T(8,128)S(1)}, u32[]{:S(2)}, u32[]{:S(2)}) %collective-permute-start.12) | collective-permute-done | bytes 51232 | tf_op jit(solution)/shard_map/ppermute | solution.py:552
  73.3 2.4 %collective-permute-start.13 = (f32[100,128]{1,0:T(8,128)S(1)}, f32[100,128]{1,0:T(8,128)S(1)}, u32[]{:S(2)}, u32[]{:S(2)}) collective-permute-start(f32[100,128]{1,0:T(8,128)S(1)} %add_add_fusion), channel_id=1, source_target_pairs={{0,8},{2,10},{4,12},{6,14},{8,0},{10,2},{12,4},{14,6},{16,24},{18,... | collective-permute-start | bytes 153608 | tf_op jit(solution)/shard_map/ppermute | solution.py:552
  75.7 3.2 %collective-permute-done.13 = f32[100,128]{1,0:T(8,128)S(1)} collective-permute-done((f32[100,128]{1,0:T(8,128)S(1)}, f32[100,128]{1,0:T(8,128)S(1)}, u32[]{:S(2)}, u32[]{:S(2)}) %collective-permute-start.13) | collective-permute-done | bytes 51232 | tf_op jit(solution)/shard_map/ppermute | solution.py:552
  79.0 1.5 %collective-permute-start.14 = (f32[100,128]{1,0:T(8,128)S(1)}, f32[100,128]{1,0:T(8,128)S(1)}, u32[]{:S(2)}, u32[]{:S(2)}) collective-permute-start(f32[100,128]{1,0:T(8,128)S(1)} %add.57), channel_id=1, source_target_pairs={{0,16},{2,18},{4,20},{6,22},{8,24},{10,26},{12,28},{14,30},{16,0},... | collective-permute-start | bytes 153608 | tf_op jit(solution)/shard_map/ppermute | solution.py:552
  80.5 2.7 %collective-permute-done.14 = f32[100,128]{1,0:T(8,128)S(1)} collective-permute-done((f32[100,128]{1,0:T(8,128)S(1)}, f32[100,128]{1,0:T(8,128)S(1)}, u32[]{:S(2)}, u32[]{:S(2)}) %collective-permute-start.14) | collective-permute-done | bytes 51232 | tf_op jit(solution)/shard_map/ppermute | solution.py:552
  83.2 0.0 copy-start.4
  83.2 0.1 collective-permute-start.15
  83.3 0.0 copy-done.1
  83.3 0.3 edge.1
  83.6 0.5 collective-permute-start.7
  84.2 4.9 %collective-permute-start.8 = (bf16[5,8,512]{2,1,0:T(8,128)(2,1)S(1)}, bf16[5,8,512]{2,1,0:T(8,128)(2,1)S(1)}, u32[]{:S(2)}, u32[]{:S(2)}) collective-permute-start(bf16[5,8,512]{2,1,0:T(8,128)(2,1)S(1)} %get-tuple-element.27), channel_id=1, source_target_pairs={{1,0},{2,1},{3,2},{4,3},{5,4},{6,5},{7,6},{8,7},{9,8},{10,9},{11,1... | collective-permute-start | bytes 122888 | tf_op jit(solution)/shard_map/ppermute | solution.py:616
  89.0 0.0 copy-done.4
  89.0 3.7 %slab.1.field_ref = f32[5,8,32,512]{3,2,1,0:T(8,128)} custom-call(f32[5,8,32,512]{3,2,1,0:T(8,128)S(1)} %copy-done.1, f32[8,32,512]{2,1,0:T(8,128)S(1)} %copy-done.4), custom_call_target="tpu_custom_call" | custom-call | tf_op jit(solution)/shard_map/slab/pallas_call | solution.py:459
  92.7 0.0 collective-permute-done.7.below_ref
  92.7 0.0 collective-permute-done.8.above_ref
  92.7 2.4 %rim.1.field_ref = f32[5,8,32,512]{3,2,1,0:T(8,128)} custom-call(bf16[5,8,512]{2,1,0:T(8,128)(2,1)S(1)} %collective-permute-done.7.below_ref, bf16[5,8,512]{2,1,0:T(8,128)(2,1)S(1)} %collective-permute-done.8.above_ref, f32[8,32,512]{2,1,0:T(8,128)} %diff_ref.3, f32[5,8,32,512]{3,2,1,0:T(8,128)} %slab.1.field_ref), custom_call_target="tpu_custom_call", output_to_operand_aliasing={{}: (3, {})} | custom-call | tf_op jit(solution)/shard_map/rim/pallas_call | solution.py:485
  95.1 0.0 copy-done.7
  95.1 2.0 %wall.1 = (f32[2,32,512]{2,1,0:T(8,128)}, f32[5,8,32,512]{3,2,1,0:T(8,128)}) custom-call(s32[2]{0:T(128)S(1)} %pad_add_fusion.place_ref, s32[8,128]{1,0:T(8,128)S(1)} %get-tuple-element.23.info_ref, f32[2,2048]{1,0:T(2,128)S(1)} %add_add_fusion.1.pred_ref.all_ref, f32[2,32,512]{2,1,0:T(8,128)S(1)} %copy-done.7, ...), custom_call_target="tpu_custom_call", output_to_operand_aliasing={{1}: (4, {})} | custom-call | tf_op jit(solution)/shard_map/wall/pallas_call | solution.py:526
  97.1 0.0 collective-permute-done.15.rest_ref
  97.1 1.2 %join.1 = (f32[12,2048]{1,0:T(8,128)}, f32[1,1]{1,0:T(1,128)}) custom-call(s32[2]{0:T(128)S(1)} %pad_add_fusion.place_ref, f32[100,128]{1,0:T(8,128)S(1)} %add.58.half_ref, f32[100,128]{1,0:T(8,128)S(1)} %collective-permute-done.15.rest_ref), custom_call_target="tpu_custom_call" | custom-call | tf_op jit(solution)/shard_map/join/pallas_call | solution.py:406
  98.3 0.0 all-to-all-done.1.blocks_ref
  98.3 0.8 lay.1
  (13 shorter events, 0.1 us)
Async XLA Ops:
  0.6 21.6 %copy-start = (bf16[2,2048]{1,0:T(2,128)(2,1)S(1)}, bf16[2,2048]{1,0:T(2,128)(2,1)}, u32[]{:S(2)}) copy-start(bf16[2,2048]{1,0:T(2,128)(2,1)} %param.17) | copy-start | bytes 24580
  0.6 21.6 %copy-start.8 = (bf16[12,2048]{1,0:T(8,128)(2,1)S(1)}, bf16[12,2048]{1,0:T(8,128)(2,1)}, u32[]{:S(2)}) copy-start(bf16[12,2048]{1,0:T(8,128)(2,1)} %weight_ref.3) | copy-start | bytes 147460
  22.2 1.6 %copy-start.9 = (bf16[16,80,128]{2,1,0:T(8,128)(2,1)}, bf16[16,80,128]{2,1,0:T(8,128)(2,1)S(1)}, u32[]{:S(2)}) copy-start(bf16[16,80,128]{2,1,0:T(8,128)(2,1)S(1)} %all_to_all.10.got_ref.mine_ref) | copy-start | bytes 983044
  22.2 1.6 %collective-permute-start = (bf16[16,80,128]{2,1,0:T(8,128)(2,1)S(1)}, bf16[16,80,128]{2,1,0:T(8,128)(2,1)S(1)}, u32[]{:S(2)}, u32[]{:S(2)}) collective-permute-start(bf16[16,80,128]{2,1,0:T(8,128)(2,1)S(1)} %all_to_all.10.got_ref.mine_ref), channel_id=1, source_target_pairs={{0,1},{1,0},{2,3},{3,2},{4,5},{5,4},{6,7},{7,6},{8,9},{9,8},{10,11... | collective-permute-start | bytes 983048 | tf_op jit(solution)/shard_map/ppermute | solution.py:548
  30.3 15.8 %copy-start.2 = (f32[128,2048]{1,0:T(8,128)}, f32[128,2048]{1,0:T(8,128)S(1)}, u32[]{:S(2)}) copy-start(f32[128,2048]{1,0:T(8,128)S(1)} %get-tuple-element.32.second_ref) | copy-start | bytes 3145732
  30.3 15.9 %copy-start.5 = (bf16[2048,128]{1,0:T(8,128)(2,1)}, bf16[2048,128]{1,0:T(8,128)(2,1)S(1)}, u32[]{:S(2)}) copy-start(bf16[2048,128]{1,0:T(8,128)(2,1)S(1)} %get-tuple-element.31.weight_ref) | copy-start | bytes 1572868
  30.3 3.8 %collective-permute-start.1 = (f32[2,2048]{1,0:T(2,128)S(1)}, f32[2,2048]{1,0:T(2,128)S(1)}, u32[]{:S(2)}, u32[]{:S(2)}) collective-permute-start(f32[2,2048]{1,0:T(2,128)S(1)} %get-tuple-element.25), channel_id=1, source_target_pairs={{0,2},{2,0},{4,6},{6,4},{8,10},{10,8},{12,14},{14,12},{16,18},{18,... | collective-permute-start | bytes 49160 | tf_op jit(solution)/shard_map/ppermute | solution.py:552
  30.9 3.7 %collective-permute-start.2 = (f32[2,2048]{1,0:T(2,128)S(1)}, f32[2,2048]{1,0:T(2,128)S(1)}, u32[]{:S(2)}, u32[]{:S(2)}) collective-permute-start(f32[2,2048]{1,0:T(2,128)S(1)} %get-tuple-element.25), channel_id=1, source_target_pairs={{0,4},{2,6},{4,0},{6,2},{8,12},{10,14},{12,8},{14,10},{16,20},{18,... | collective-permute-start | bytes 49160 | tf_op jit(solution)/shard_map/ppermute | solution.py:552
  31.7 4.6 %collective-permute-start.3 = (f32[2,2048]{1,0:T(2,128)S(1)}, f32[2,2048]{1,0:T(2,128)S(1)}, u32[]{:S(2)}, u32[]{:S(2)}) collective-permute-start(f32[2,2048]{1,0:T(2,128)S(1)} %get-tuple-element.25), channel_id=1, source_target_pairs={{0,6},{2,4},{4,2},{6,0},{8,14},{10,12},{12,10},{14,8},{16,22},{18,... | collective-permute-start | bytes 49160 | tf_op jit(solution)/shard_map/ppermute | solution.py:552
  36.3 5.0 %collective-permute-start.4 = (f32[2,2048]{1,0:T(2,128)S(1)}, f32[2,2048]{1,0:T(2,128)S(1)}, u32[]{:S(2)}, u32[]{:S(2)}) collective-permute-start(f32[2,2048]{1,0:T(2,128)S(1)} %add_add_fusion.2), channel_id=1, source_target_pairs={{0,8},{2,10},{4,12},{6,14},{8,0},{10,2},{12,4},{14,6},{16,24},{18,... | collective-permute-start | bytes 49160 | tf_op jit(solution)/shard_map/ppermute | solution.py:552
  38.1 3.7 %collective-permute-start.5 = (f32[2,2048]{1,0:T(2,128)S(1)}, f32[2,2048]{1,0:T(2,128)S(1)}, u32[]{:S(2)}, u32[]{:S(2)}) collective-permute-start(f32[2,2048]{1,0:T(2,128)S(1)} %add_add_fusion.2), channel_id=1, source_target_pairs={{0,16},{2,18},{4,20},{6,22},{8,24},{10,26},{12,28},{14,30},{16,0},... | collective-permute-start | bytes 49160 | tf_op jit(solution)/shard_map/ppermute | solution.py:552
  38.4 5.5 %collective-permute-start.6 = (f32[2,2048]{1,0:T(2,128)S(1)}, f32[2,2048]{1,0:T(2,128)S(1)}, u32[]{:S(2)}, u32[]{:S(2)}) collective-permute-start(f32[2,2048]{1,0:T(2,128)S(1)} %add_add_fusion.2), channel_id=1, source_target_pairs={{0,24},{2,26},{4,28},{6,30},{8,16},{10,18},{12,20},{14,22},{16,8},... | collective-permute-start | bytes 49160 | tf_op jit(solution)/shard_map/ppermute | solution.py:552
  46.1 37.1 %copy-start.1 = (f32[5,8,32,512]{3,2,1,0:T(8,128)S(1)}, f32[5,8,32,512]{3,2,1,0:T(8,128)}, u32[]{:S(2)}) copy-start(f32[5,8,32,512]{3,2,1,0:T(8,128)} %flow_ref.3) | copy-start | bytes 7864324
  46.1 2.0 %collective-permute-start.16 = (f32[16,64,128]{2,1,0:T(8,128)S(1)}, f32[16,64,128]{2,1,0:T(8,128)S(1)}, u32[]{:S(2)}, u32[]{:S(2)}) collective-permute-start(f32[16,64,128]{2,1,0:T(8,128)S(1)} %get-tuple-element.40), channel_id=1, source_target_pairs={{0,1},{1,0},{2,3},{3,2},{4,5},{5,4},{6,7},{7,6},{8,9},{9,8},{10,11... | collective-permute-start | bytes 1572872 | tf_op jit(solution)/shard_map/ppermute | solution.py:548
  49.0 49.3 %all-to-all-start.1 = ((f32[16,64,128]{2,1,0:T(8,128)}), f32[16,64,128]{2,1,0:T(8,128)S(1)}, u32[]{:S(2)}, u32[]{:S(2)}) async-start(f32[16,64,128]{2,1,0:T(8,128)} %add.59), calls=%async_computation.1 | async-start | bytes 1048576 | tf_op jit(solution)/shard_map/all_to_all | solution.py:571
  54.4 1.2 %copy-start.3 = (f32[128,2048]{1,0:T(8,128)S(1)}, f32[128,2048]{1,0:T(8,128)}, u32[]{:S(2)}) copy-start(f32[128,2048]{1,0:T(8,128)} %copy-done.2) | copy-start | bytes 3145732
  55.6 1.0 %copy-start.6 = (bf16[2048,128]{1,0:T(8,128)(2,1)S(1)}, bf16[2048,128]{1,0:T(8,128)(2,1)}, u32[]{:S(2)}) copy-start(bf16[2048,128]{1,0:T(8,128)(2,1)} %copy-done.5) | copy-start | bytes 1572868
  63.6 1.2 %collective-permute-start.9 = (f32[100,128]{1,0:T(8,128)S(1)}, f32[100,128]{1,0:T(8,128)S(1)}, u32[]{:S(2)}, u32[]{:S(2)}) collective-permute-start(f32[100,128]{1,0:T(8,128)S(1)} %get-tuple-element.35), channel_id=1, source_target_pairs={{0,1},{1,0},{2,3},{3,2},{4,5},{5,4},{6,7},{7,6},{8,9},{9,8},{10,11... | collective-permute-start | bytes 153608 | tf_op jit(solution)/shard_map/ppermute | solution.py:548
  64.8 4.5 %collective-permute-start.10 = (f32[100,128]{1,0:T(8,128)S(1)}, f32[100,128]{1,0:T(8,128)S(1)}, u32[]{:S(2)}, u32[]{:S(2)}) collective-permute-start(f32[100,128]{1,0:T(8,128)S(1)} %add.53), channel_id=1, source_target_pairs={{0,2},{2,0},{4,6},{6,4},{8,10},{10,8},{12,14},{14,12},{16,18},{18,... | collective-permute-start | bytes 153608 | tf_op jit(solution)/shard_map/ppermute | solution.py:552
  66.8 4.7 %collective-permute-start.11 = (f32[100,128]{1,0:T(8,128)S(1)}, f32[100,128]{1,0:T(8,128)S(1)}, u32[]{:S(2)}, u32[]{:S(2)}) collective-permute-start(f32[100,128]{1,0:T(8,128)S(1)} %add.53), channel_id=1, source_target_pairs={{0,4},{2,6},{4,0},{6,2},{8,12},{10,14},{12,8},{14,10},{16,20},{18,... | collective-permute-start | bytes 153608 | tf_op jit(solution)/shard_map/ppermute | solution.py:552
  68.3 5.0 %collective-permute-start.12 = (f32[100,128]{1,0:T(8,128)S(1)}, f32[100,128]{1,0:T(8,128)S(1)}, u32[]{:S(2)}, u32[]{:S(2)}) collective-permute-start(f32[100,128]{1,0:T(8,128)S(1)} %add.53), channel_id=1, source_target_pairs={{0,6},{2,4},{4,2},{6,0},{8,14},{10,12},{12,10},{14,8},{16,22},{18,... | collective-permute-start | bytes 153608 | tf_op jit(solution)/shard_map/ppermute | solution.py:552
  73.3 5.7 %collective-permute-start.13 = (f32[100,128]{1,0:T(8,128)S(1)}, f32[100,128]{1,0:T(8,128)S(1)}, u32[]{:S(2)}, u32[]{:S(2)}) collective-permute-start(f32[100,128]{1,0:T(8,128)S(1)} %add_add_fusion), channel_id=1, source_target_pairs={{0,8},{2,10},{4,12},{6,14},{8,0},{10,2},{12,4},{14,6},{16,24},{18,... | collective-permute-start | bytes 153608 | tf_op jit(solution)/shard_map/ppermute | solution.py:552
  79.0 4.2 %collective-permute-start.14 = (f32[100,128]{1,0:T(8,128)S(1)}, f32[100,128]{1,0:T(8,128)S(1)}, u32[]{:S(2)}, u32[]{:S(2)}) collective-permute-start(f32[100,128]{1,0:T(8,128)S(1)} %add.57), channel_id=1, source_target_pairs={{0,16},{2,18},{4,20},{6,22},{8,24},{10,26},{12,28},{14,30},{16,0},... | collective-permute-start | bytes 153608 | tf_op jit(solution)/shard_map/ppermute | solution.py:552
  83.2 5.8 %copy-start.4 = (f32[8,32,512]{2,1,0:T(8,128)S(1)}, f32[8,32,512]{2,1,0:T(8,128)}, u32[]{:S(2)}) copy-start(f32[8,32,512]{2,1,0:T(8,128)} %diff_ref.3) | copy-start | bytes 1572868
  83.2 13.9 %collective-permute-start.15 = (f32[100,128]{1,0:T(8,128)S(1)}, f32[100,128]{1,0:T(8,128)S(1)}, u32[]{:S(2)}, u32[]{:S(2)}) collective-permute-start(f32[100,128]{1,0:T(8,128)S(1)} %add.58.half_ref), channel_id=1, source_target_pairs={{0,1},{1,0},{2,3},{3,2},{4,5},{5,4},{6,7},{7,6},{8,9},{9,8},{10,11... | collective-permute-start | bytes 153608 | tf_op jit(solution)/shard_map/ppermute | solution.py:548
  83.6 9.1 %collective-permute-start.7 = (bf16[5,8,512]{2,1,0:T(8,128)(2,1)S(1)}, bf16[5,8,512]{2,1,0:T(8,128)(2,1)S(1)}, u32[]{:S(2)}, u32[]{:S(2)}) collective-permute-start(bf16[5,8,512]{2,1,0:T(8,128)(2,1)S(1)} %get-tuple-element.26), channel_id=1, source_target_pairs={{0,1},{1,2},{2,3},{3,4},{4,5},{5,6},{6,7},{7,8},{8,9},{9,10},{10,1... | collective-permute-start | bytes 122888 | tf_op jit(solution)/shard_map/ppermute | solution.py:615
  84.2 8.6 %collective-permute-start.8 = (bf16[5,8,512]{2,1,0:T(8,128)(2,1)S(1)}, bf16[5,8,512]{2,1,0:T(8,128)(2,1)S(1)}, u32[]{:S(2)}, u32[]{:S(2)}) collective-permute-start(bf16[5,8,512]{2,1,0:T(8,128)(2,1)S(1)} %get-tuple-element.27), channel_id=1, source_target_pairs={{1,0},{2,1},{3,2},{4,3},{5,4},{6,5},{7,6},{8,7},{9,8},{10,9},{11,1... | collective-permute-start | bytes 122888 | tf_op jit(solution)/shard_map/ppermute | solution.py:616
  92.7 2.4 %copy-start.7 = (f32[2,32,512]{2,1,0:T(8,128)S(1)}, f32[2,32,512]{2,1,0:T(8,128)}, u32[]{:S(2)}) copy-start(f32[2,32,512]{2,1,0:T(8,128)} %stress_ref.1) | copy-start | bytes 393220

commit v4 on v3

--- a/solution.py
+++ b/solution.py
@@ -167,19 +167,96 @@
     return across, jnp.where(iota(across.shape, 0) < FEATURES, across, 0.0)
 
 
-def forward_kernel(
-    place_ref, got_ref, mine_ref, other_ref, win_ref, wout_ref,
-    second_ref, pred_ref, rows_ref, weight_ref, *first_ref, step,
+def assemble(place_ref, mine_ref, other_ref, weight_ref):
+    core = place_ref[0]
+    chips, rows, _ = mine_ref.shape
+    for j in range(chips):
+        at = pl.multiple_of((CORES * j + core) * rows, rows)
+        weight_ref[pl.ds(at, rows), :] = mine_ref[j]
+        at = pl.multiple_of((CORES * j + 1 - core) * rows, rows)
+        weight_ref[pl.ds(at, rows), :] = other_ref[j, :rows]
+
+
+def first_kernel(got_ref, win_ref, rows_ref, first_ref, *, step):
+    rows_ref[...] = got_ref[...]
+    _, features = features_of(got_ref)
+    tall = features.T.astype(jnp.bfloat16)
+    for at in range(0, first_ref.shape[1], step):
+        act = jnp.tanh(mm(tall, win_ref[:, at : at + step]))
+        first_ref[:, at : at + step] = act.astype(jnp.bfloat16)
+
+
+def first_layer(got, skip, win, group):
+    chips, _, lanes = got.shape
+    hidden = win.shape[1]
+    tile, samples = group * lanes, chips * lanes
+    return pl.pallas_call(
+        functools.partial(first_kernel, step=min(hidden, STEP)),
+        grid=(chips // group,),
+        in_specs=[
+            pl.BlockSpec((group, ROWS, lanes), lambda i: (i, skip, 0)),
+            whole(win.shape),
+        ],
+        out_specs=[
+            pl.BlockSpec((group, ROWS, lanes), lambda i: (i, 0, 0)),
+            pl.BlockSpec((tile, hidden), lambda i: (i, 0)),
+        ],
+        out_shape=[
+            jax.ShapeDtypeStruct((chips, ROWS, lanes), got.dtype),
+            jax.ShapeDtypeStruct((samples, hidden), jnp.bfloat16),
+        ],
+        compiler_params=params(28),
+        name="first",
+    )(got, win)
+
+
+def second_kernel(
+    place_ref, first_ref, mine_ref, other_ref, wout_ref, second_ref, pred_ref, weight_ref
 ):
     @pl.when(pl.program_id(0) == 0)
     def _():
-        core = place_ref[0]
-        chips, rows, _ = mine_ref.shape
-        for j in range(chips):
-            at = pl.multiple_of((CORES * j + core) * rows, rows)
-            weight_ref[pl.ds(at, rows), :] = mine_ref[j]
-            at = pl.multiple_of((CORES * j + 1 - core) * rows, rows)
-            weight_ref[pl.ds(at, rows), :] = other_ref[j, :rows]
+        assemble(place_ref, mine_ref, other_ref, weight_ref)
+
+    second = jnp.tanh(mm(first_ref[...], weight_ref[...])).T
+    second_ref[...] = second
+    pred_ref[...] = mm(wout_ref[...], second.astype(jnp.bfloat16))
+
+
+def second_layer(place, first, mine, other, wout, rows_dev, tile):
+    chips, _, width = mine.shape
+    samples, hidden = first.shape
+    return pl.pallas_call(
+        second_kernel,
+        grid=(samples // tile,),
+        in_specs=[
+            pl.BlockSpec(memory_space=pltpu.SMEM),
+            pl.BlockSpec((tile, hidden), lambda i: (i, 0)),
+            whole((chips, rows_dev, width)),
+            whole(other.shape),
+            whole(wout.shape),
+        ],
+        out_specs=[
+            pl.BlockSpec((width, tile), lambda i: (0, i)),
+            pl.BlockSpec((wout.shape[0], tile), lambda i: (0, i)),
+            whole((hidden, width)),
+        ],
+        out_shape=[
+            jax.ShapeDtypeStruct((width, samples), jnp.float32),
+            jax.ShapeDtypeStruct((wout.shape[0], samples), jnp.float32),
+            jax.ShapeDtypeStruct((hidden, width), jnp.bfloat16),
+        ],
+        compiler_params=params(28),
+        name="second",
+    )(place, first, mine, other, wout)
+
+
+def forward_kernel(
+    place_ref, got_ref, mine_ref, other_ref, win_ref, wout_ref,
+    second_ref, pred_ref, rows_ref, weight_ref, *, step,
+):
+    @pl.when(pl.program_id(0) == 0)
+    def _():
+        assemble(place_ref, mine_ref, other_ref, weight_ref)
 
     hidden = weight_ref.shape[0]
     rows_ref[...] = got_ref[...]
@@ -188,8 +265,6 @@
     total = None
     for at in range(0, hidden, step):
         first = jnp.tanh(mm(tall, win_ref[:, at : at + step])).astype(jnp.bfloat16)
-        if first_ref:
-            first_ref[0][:, at : at + step] = first
         term = mm(first, weight_ref[at : at + step, :])
         total = term if total is None else total + term
     second = jnp.tanh(total).T
@@ -197,7 +272,7 @@
     pred_ref[...] = mm(wout_ref[...], second.astype(jnp.bfloat16))
 
 
-def forward(place, got, skip, mine, other, win, wout, rows_dev, group, keep):
+def forward(place, got, skip, mine, other, win, wout, rows_dev, group):
     chips, _, width = mine.shape
     lanes = got.shape[2]
     hidden = win.shape[1]
@@ -214,9 +289,6 @@
         jax.ShapeDtypeStruct((chips, ROWS, lanes), got.dtype),
         jax.ShapeDtypeStruct((hidden, width), jnp.bfloat16),
     ]
-    if keep:
-        out_specs.append(pl.BlockSpec((tile, hidden), lambda i: (i, 0)))
-        out_shape.append(jax.ShapeDtypeStruct((samples, hidden), jnp.bfloat16))
     return pl.pallas_call(
         functools.partial(forward_kernel, step=min(hidden, STEP)),
         grid=(chips // group,),
@@ -610,7 +682,7 @@
         lanes,
         (chips, rows_dev + ROWS, width) if joint else None,
     )
-    blocks = [far(b) for b in blocks]
+    blocks = [pltpu.with_memory_space_constraint(b, pltpu.VMEM) for b in blocks]
     first_z, last_z = edge_planes(flow_state)
     below = lax.ppermute(last_z, EVERY, order)
     above = lax.ppermute(first_z, EVERY, back_order)
@@ -629,9 +701,16 @@
     win = widen(input_weight)
     wout = lax.dynamic_slice_in_dim(output_weight, chip * width, width, axis=1)
     keep = chips * lanes * hidden * 2 <= KEEP_BYTES
-    second, part, rows, weight, *first = forward(
-        place, got, skip, mine, other, win, wout, rows_dev, group, keep
-    )
+    if keep:
+        rows, *first = first_layer(got, skip, win, group)
+        second, part, weight = second_layer(
+            place, first[0], mine, other, wout, rows_dev, group * lanes
+        )
+    else:
+        first = []
+        second, part, rows, weight = forward(
+            place, got, skip, mine, other, win, wout, rows_dev, group
+        )
     pred = sum_chips(part, chips, (4,))
 
     stay, send = middle_gradient(
@@ -651,8 +730,8 @@
     batch_loss = loss.reshape(1)
 
     field = slab(flow_state, diffusion)
-    field = rim(below, above, far(diffusion), field)
-    new_stress, new_field = wall(place, info, pred, wall_stress, field)
+    new_stress, field = wall(place, info, pred, wall_stress, field)
+    new_field = rim(below, above, far(diffusion), field)
     return (new_field, new_stress, batch_loss, grad_w_in, grad_w_mid)
 
 

time: 99.6 us -> 97.4 us (0.978)
  waiting for transfers between devices: 21.1 us -> 19.6 us
    ppermute x4, waiting for transfers between devices: 4.63 us -> 3.14 us  [swap_cores(): return lax.ppermute(block, 'core', [(0, 1), (1, 0)])]
    pallas_call x1 -> x2, Pallas kernels: 6.4 us -> 5.7 us  [the longest x1 3.24 us: second_layer(): pl.pallas_call(second_kernel, grid=(samples // tile,), in_specs=[pl.Block...]
    unnamed x20 -> x18, local copies, waits for them, and re-layouts: 2.3 us -> 2.3 us
  transfers between devices with their start and end apart: 18 -> 18, of which waited for: 14 -> 13; matrix products, arithmetic and copies ran while one was open for 0% -> 0% of each run, Pallas kernels for 17% -> 20%
where the time goes in v4:
time: 97.4 us; the launch traced here: 96.9 us
  Pallas kernels  27.3 us (28%)
  starting transfers between devices  26.4 us (27%)
  waiting for transfers between devices  19.6 us (20%)
  blocking collectives  19.5 us (20%)
  local copies, waits for them, and re-layouts  2.31 us (2%)
  other arithmetic  1.01 us (1%)
    all_to_all x1, blocking collectives, exchange(): lax.all_to_all(blocks, CHIPS, split_axis=0, concat_axis=0, tiled=True)  19.5 us
    ppermute x11, waiting for transfers between devices, flip(): return lax.ppermute(block, CHIPS, [(i, i ^ mask) for i in range(chips)])  16.4 us
    ppermute x11, starting transfers between devices, flip(): return lax.ppermute(block, CHIPS, [(i, i ^ mask) for i in range(chips)])  15.5 us
    pallas_call x1, Pallas kernels, input_gradient(): pl.pallas_call(functools.partial(input_kernel, step=min(hidden, STEP), li...  6.91 us
    all_to_all x1, starting transfers between devices, exchange(): lax.all_to_all(blocks, CHIPS, split_axis=0, concat_axis=0, tiled=True)  5.4 us
    ppermute x1, starting transfers between devices, step(): above = lax.ppermute(first_z, EVERY, back_order)  4.86 us
    pallas_call x1, Pallas kernels, slab(): pl.pallas_call(slab_kernel, grid=(vars_,), in_specs=[block, pl.BlockSpec(...  3.75 us
    pallas_call x1, Pallas kernels, second_layer(): pl.pallas_call(second_kernel, grid=(samples // tile,), in_specs=[pl.Block...  3.24 us
  transfers between devices with their start and end apart: 18, of which 13 were waited for; matrix products, arithmetic and copies ran while one was open for 0% of the time, Pallas kernels for 20%

profile of v4, /device:TPU:0, one launch (start us, length us, event | category | flops | bytes accessed | tf_op | source)
XLA Modules:
  0.0 96.9 jit_solution(11830966708762511787)
XLA Ops:
  0.6 0.0 copy-start
  0.6 0.0 copy-start.8
  0.7 2.1 %pick.1 = (bf16[1,16,128]{2,1,0:T(8,128)(2,1)S(1)}, s32[8,128]{1,0:T(8,128)S(1)}, bf16[16,80,128]{2,1,0:T(8,128)(2,1)S(1)}) custom-call(s32[1,48]{1,0:T(1,128)} %counts_ref.1, s32[1,48]{1,0:T(1,128)} %bitcast.6, s32[4,48]{1,0:T(4,128)} %bitcast.5, f32[5,8,32,512]{3,2,1,0:T(8,128)} %flow_ref.3, bf16[64,2048]{1,0:T(8,128)(2,1)} %weight_ref.2), custom_call_target="tpu_custom_call" | custom-call | tf_op jit(solution)/shard_map/pick/pallas_call | solution.py:106
  2.8 19.5 %all_to_all.10.got_ref.mine_ref = bf16[16,80,128]{2,1,0:T(8,128)(2,1)S(1)} all-to-all(bf16[16,80,128]{2,1,0:T(8,128)(2,1)S(1)} %get-tuple-element.26), channel_id=1, replica_groups=mesh['sec'=2,'chip'=8,'core'=2] {'sec','chip'}, dimensions={0} | all-to-all | bytes 655360 | tf_op jit(solution)/shard_map/all_to_all | solution.py:643
  22.2 0.0 collective-permute-start.2
  22.2 0.0 copy-done.8
  22.2 0.0 copy-done
  22.3 0.1 pad_add_fusion.place_ref
  22.4 2.5 %first.1 = (bf16[16,16,128]{2,1,0:T(8,128)(2,1)S(1)}, bf16[2048,2048]{1,0:T(8,128)(2,1)S(1)}) custom-call(bf16[16,80,128]{2,1,0:T(8,128)(2,1)S(1)} %all_to_all.10.got_ref.mine_ref, bf16[16,2048]{1,0:T(8,128)(2,1)S(1)} %widen.1.win_ref), custom_call_target="tpu_custom_call" | custom-call | tf_op jit(solution)/shard_map/first/pallas_call | solution.py:193
  24.8 0.0 collective-permute-done.2.other_ref
  24.8 3.2 %second.1 = (f32[128,2048]{1,0:T(8,128)S(1)}, f32[2,2048]{1,0:T(2,128)S(1)}, bf16[2048,128]{1,0:T(8,128)(2,1)S(1)}) custom-call(s32[2]{0:T(128)S(1)} %pad_add_fusion.place_ref, bf16[2048,2048]{1,0:T(8,128)(2,1)S(1)} %get-tuple-element.27.first_ref.refs_0_, bf16[16,80,128]{2,1,0:T(8,128)(2,1)S(1)} %all_to_all.10.got_ref.mine_ref, ...), custom_call_target="tpu_custom_call" | custom-call | tf_op jit(solution)/shard_map/second/pallas_call | solution.py:228
  28.1 0.6 collective-permute-start.3
  28.7 0.8 collective-permute-start.4
  29.5 2.1 %collective-permute-start.5 = (f32[2,2048]{1,0:T(2,128)S(1)}, f32[2,2048]{1,0:T(2,128)S(1)}, u32[]{:S(2)}, u32[]{:S(2)}) collective-permute-start(f32[2,2048]{1,0:T(2,128)S(1)} %get-tuple-element.28), channel_id=1, source_target_pairs={{0,6},{2,4},{4,2},{6,0},{8,14},{10,12},{12,10},{14,8},{16,22},{18,... | collective-permute-start | bytes 49160 | tf_op jit(solution)/shard_map/ppermute | solution.py:624
  31.6 0.2 collective-permute-done.3
  31.9 0.6 collective-permute-done.4
  32.4 1.7 %collective-permute-done.5 = f32[2,2048]{1,0:T(2,128)S(1)} collective-permute-done((f32[2,2048]{1,0:T(2,128)S(1)}, f32[2,2048]{1,0:T(2,128)S(1)}, u32[]{:S(2)}, u32[]{:S(2)}) %collective-permute-start.5) | collective-permute-done | bytes 16416 | tf_op jit(solution)/shard_map/ppermute | solution.py:624
  34.1 1.7 %collective-permute-start.6 = (f32[2,2048]{1,0:T(2,128)S(1)}, f32[2,2048]{1,0:T(2,128)S(1)}, u32[]{:S(2)}, u32[]{:S(2)}) collective-permute-start(f32[2,2048]{1,0:T(2,128)S(1)} %add_add_fusion.2), channel_id=1, source_target_pairs={{0,8},{2,10},{4,12},{6,14},{8,0},{10,2},{12,4},{14,6},{16,24},{18,... | collective-permute-start | bytes 49160 | tf_op jit(solution)/shard_map/ppermute | solution.py:624
  35.9 0.3 collective-permute-start.7
  36.1 2.4 %collective-permute-start.8 = (f32[2,2048]{1,0:T(2,128)S(1)}, f32[2,2048]{1,0:T(2,128)S(1)}, u32[]{:S(2)}, u32[]{:S(2)}) collective-permute-start(f32[2,2048]{1,0:T(2,128)S(1)} %add_add_fusion.2), channel_id=1, source_target_pairs={{0,24},{2,26},{4,28},{6,30},{8,16},{10,18},{12,20},{14,22},{16,8},... | collective-permute-start | bytes 49160 | tf_op jit(solution)/shard_map/ppermute | solution.py:624
  38.6 0.2 collective-permute-done.6
  38.8 0.8 collective-permute-done.7
  39.6 2.1 %collective-permute-done.8 = f32[2,2048]{1,0:T(2,128)S(1)} collective-permute-done((f32[2,2048]{1,0:T(2,128)S(1)}, f32[2,2048]{1,0:T(2,128)S(1)}, u32[]{:S(2)}, u32[]{:S(2)}) %collective-permute-start.8) | collective-permute-done | bytes 16416 | tf_op jit(solution)/shard_map/ppermute | solution.py:624
  41.7 2.2 %middle.1 = (f32[16,64,128]{2,1,0:T(8,128)S(1)}, f32[16,64,128]{2,1,0:T(8,128)S(1)}) custom-call(s32[2]{0:T(128)S(1)} %pad_add_fusion.place_ref, bf16[16,16,128]{2,1,0:T(8,128)(2,1)S(1)} %get-tuple-element.31.rows_ref, bf16[16,2048]{1,0:T(8,128)(2,1)S(1)} %widen.1.win_ref, bf16[2,128]{1,0:T(2,128)(2,1)S(1)} %constant_dynamic-slice_fusion.wout_ref, ...), custom_call_target="tpu_custom_call" | custom-call | tf_op jit(solution)/shard_map/middle/pallas_call | solution.py:361
  43.9 0.0 copy-done.2
  43.9 0.0 copy-done.5
  43.9 0.0 copy-start.1
  43.9 0.1 collective-permute-start.16
  44.0 1.9 %collective-permute-done.16 = f32[16,64,128]{2,1,0:T(8,128)S(1)} collective-permute-done((f32[16,64,128]{2,1,0:T(8,128)S(1)}, f32[16,64,128]{2,1,0:T(8,128)S(1)}, u32[]{:S(2)}, u32[]{:S(2)}) %collective-permute-start.16) | collective-permute-done | bytes 524320 | tf_op jit(solution)/shard_map/ppermute | solution.py:620
  45.9 0.9 add.59
  46.7 5.4 %all-to-all-start.1 = ((f32[16,64,128]{2,1,0:T(8,128)}), f32[16,64,128]{2,1,0:T(8,128)S(1)}, u32[]{:S(2)}, u32[]{:S(2)}) async-start(f32[16,64,128]{2,1,0:T(8,128)} %add.59), calls=%async_computation.1 | async-start | bytes 1048576 | tf_op jit(solution)/shard_map/all_to_all | solution.py:643
  52.1 0.0 copy-start.3
  52.2 1.2 %copy-done.3 = f32[128,2048]{1,0:T(8,128)S(1)} copy-done((f32[128,2048]{1,0:T(8,128)S(1)}, f32[128,2048]{1,0:T(8,128)}, u32[]{:S(2)}) %copy-start.3) | copy-done | bytes 1048600
  53.4 1.0 %copy-done.6 = bf16[2048,128]{1,0:T(8,128)(2,1)S(1)} copy-done((bf16[2048,128]{1,0:T(8,128)(2,1)S(1)}, bf16[2048,128]{1,0:T(8,128)(2,1)}, u32[]{:S(2)}) %copy-start.6) | copy-done | bytes 524312
  54.4 6.9 %input.1 = (f32[100,128]{1,0:T(8,128)S(1)}, f32[100,128]{1,0:T(8,128)S(1)}) custom-call(s32[2]{0:T(128)S(1)} %pad_add_fusion.place_ref, bf16[16,16,128]{2,1,0:T(8,128)(2,1)S(1)} %get-tuple-element.31.rows_ref, bf16[16,2048]{1,0:T(8,128)(2,1)S(1)} %widen.1.win_ref, bf16[2,128]{1,0:T(2,128)(2,1)S(1)} %constant_dynamic-slice_fusion.wout_ref, ...), custom_call_target="tpu_custom_call" | custom-call | tf_op jit(solution)/shard_map/input/pallas_call | solution.py:438
  61.3 0.0 collective-permute-start.9
  61.3 1.2 %collective-permute-done.9 = f32[100,128]{1,0:T(8,128)S(1)} collective-permute-done((f32[100,128]{1,0:T(8,128)S(1)}, f32[100,128]{1,0:T(8,128)S(1)}, u32[]{:S(2)}, u32[]{:S(2)}) %collective-permute-start.9) | collective-permute-done | bytes 51232 | tf_op jit(solution)/shard_map/ppermute | solution.py:620
  62.6 2.0 %collective-permute-start.10 = (f32[100,128]{1,0:T(8,128)S(1)}, f32[100,128]{1,0:T(8,128)S(1)}, u32[]{:S(2)}, u32[]{:S(2)}) collective-permute-start(f32[100,128]{1,0:T(8,128)S(1)} %add.53), channel_id=1, source_target_pairs={{0,2},{2,0},{4,6},{6,4},{8,10},{10,8},{12,14},{14,12},{16,18},{18,... | collective-permute-start | bytes 153608 | tf_op jit(solution)/shard_map/ppermute | solution.py:624
  64.6 1.5 %collective-permute-start.11 = (f32[100,128]{1,0:T(8,128)S(1)}, f32[100,128]{1,0:T(8,128)S(1)}, u32[]{:S(2)}, u32[]{:S(2)}) collective-permute-start(f32[100,128]{1,0:T(8,128)S(1)} %add.53), channel_id=1, source_target_pairs={{0,4},{2,6},{4,0},{6,2},{8,12},{10,14},{12,8},{14,10},{16,20},{18,... | collective-permute-start | bytes 153608 | tf_op jit(solution)/shard_map/ppermute | solution.py:624
  66.0 0.1 collective-permute-start.12
  66.1 1.0 collective-permute-done.10
  67.1 2.1 %collective-permute-done.11 = f32[100,128]{1,0:T(8,128)S(1)} collective-permute-done((f32[100,128]{1,0:T(8,128)S(1)}, f32[100,128]{1,0:T(8,128)S(1)}, u32[]{:S(2)}, u32[]{:S(2)}) %collective-permute-start.11) | collective-permute-done | bytes 51232 | tf_op jit(solution)/shard_map/ppermute | solution.py:624
  69.2 1.8 %collective-permute-done.12 = f32[100,128]{1,0:T(8,128)S(1)} collective-permute-done((f32[100,128]{1,0:T(8,128)S(1)}, f32[100,128]{1,0:T(8,128)S(1)}, u32[]{:S(2)}, u32[]{:S(2)}) %collective-permute-start.12) | collective-permute-done | bytes 51232 | tf_op jit(solution)/shard_map/ppermute | solution.py:624
  71.1 2.4 %collective-permute-start.13 = (f32[100,128]{1,0:T(8,128)S(1)}, f32[100,128]{1,0:T(8,128)S(1)}, u32[]{:S(2)}, u32[]{:S(2)}) collective-permute-start(f32[100,128]{1,0:T(8,128)S(1)} %add_add_fusion), channel_id=1, source_target_pairs={{0,8},{2,10},{4,12},{6,14},{8,0},{10,2},{12,4},{14,6},{16,24},{18,... | collective-permute-start | bytes 153608 | tf_op jit(solution)/shard_map/ppermute | solution.py:624
  73.5 3.2 %collective-permute-done.13 = f32[100,128]{1,0:T(8,128)S(1)} collective-permute-done((f32[100,128]{1,0:T(8,128)S(1)}, f32[100,128]{1,0:T(8,128)S(1)}, u32[]{:S(2)}, u32[]{:S(2)}) %collective-permute-start.13) | collective-permute-done | bytes 51232 | tf_op jit(solution)/shard_map/ppermute | solution.py:624
  76.8 1.5 %collective-permute-start.14 = (f32[100,128]{1,0:T(8,128)S(1)}, f32[100,128]{1,0:T(8,128)S(1)}, u32[]{:S(2)}, u32[]{:S(2)}) collective-permute-start(f32[100,128]{1,0:T(8,128)S(1)} %add.57), channel_id=1, source_target_pairs={{0,16},{2,18},{4,20},{6,22},{8,24},{10,26},{12,28},{14,30},{16,0},... | collective-permute-start | bytes 153608 | tf_op jit(solution)/shard_map/ppermute | solution.py:624
  78.3 2.7 %collective-permute-done.14 = f32[100,128]{1,0:T(8,128)S(1)} collective-permute-done((f32[100,128]{1,0:T(8,128)S(1)}, f32[100,128]{1,0:T(8,128)S(1)}, u32[]{:S(2)}, u32[]{:S(2)}) %collective-permute-start.14) | collective-permute-done | bytes 51232 | tf_op jit(solution)/shard_map/ppermute | solution.py:624
  81.0 0.0 copy-start.4
  81.0 0.1 collective-permute-start.15
  81.1 0.0 copy-done.1
  81.1 0.3 edge.1
  81.4 0.5 collective-permute-start
  82.0 4.9 %collective-permute-start.1 = (bf16[5,8,512]{2,1,0:T(8,128)(2,1)S(1)}, bf16[5,8,512]{2,1,0:T(8,128)(2,1)S(1)}, u32[]{:S(2)}, u32[]{:S(2)}) collective-permute-start(bf16[5,8,512]{2,1,0:T(8,128)(2,1)S(1)} %get-tuple-element.24), channel_id=1, source_target_pairs={{1,0},{2,1},{3,2},{4,3},{5,4},{6,5},{7,6},{8,7},{9,8},{10,9},{11,1... | collective-permute-start | bytes 122888 | tf_op jit(solution)/shard_map/ppermute | solution.py:688
  86.8 0.0 copy-done.4
  86.8 3.7 %slab.1.field_ref = f32[5,8,32,512]{3,2,1,0:T(8,128)} custom-call(f32[5,8,32,512]{3,2,1,0:T(8,128)S(1)} %copy-done.1, f32[8,32,512]{2,1,0:T(8,128)S(1)} %copy-done.4), custom_call_target="tpu_custom_call" | custom-call | tf_op jit(solution)/shard_map/slab/pallas_call | solution.py:531
  90.6 0.0 copy-done.7
  90.6 2.0 %wall.1 = (f32[2,32,512]{2,1,0:T(8,128)}, f32[5,8,32,512]{3,2,1,0:T(8,128)}) custom-call(s32[2]{0:T(128)S(1)} %pad_add_fusion.place_ref, s32[8,128]{1,0:T(8,128)S(1)} %get-tuple-element.25.info_ref, f32[2,2048]{1,0:T(2,128)S(1)} %add_add_fusion.1.pred_ref.all_ref, f32[2,32,512]{2,1,0:T(8,128)S(1)} %copy-done.7, ...), custom_call_target="tpu_custom_call", output_to_operand_aliasing={{1}: (4, {})} | custom-call | tf_op jit(solution)/shard_map/wall/pallas_call | solution.py:598
  92.5 0.0 collective-permute-done.below_ref
  92.5 0.0 collective-permute-done.1.above_ref
  92.5 2.4 %rim.1 = f32[5,8,32,512]{3,2,1,0:T(8,128)} custom-call(bf16[5,8,512]{2,1,0:T(8,128)(2,1)S(1)} %collective-permute-done.below_ref, bf16[5,8,512]{2,1,0:T(8,128)(2,1)S(1)} %collective-permute-done.1.above_ref, f32[8,32,512]{2,1,0:T(8,128)} %diff_ref.3, f32[5,8,32,512]{3,2,1,0:T(8,128)} %get-tuple-element.29.field_ref), custom_call_target="tpu_custom_call", output_to_operand_aliasing={{}: (3, {})} | custom-call | tf_op jit(solution)/shard_map/rim/pallas_call | solution.py:557
  94.9 0.0 collective-permute-done.15.rest_ref
  94.9 1.2 %join.1 = (f32[12,2048]{1,0:T(8,128)}, f32[1,1]{1,0:T(1,128)}) custom-call(s32[2]{0:T(128)S(1)} %pad_add_fusion.place_ref, f32[100,128]{1,0:T(8,128)S(1)} %add.58.half_ref, f32[100,128]{1,0:T(8,128)S(1)} %collective-permute-done.15.rest_ref), custom_call_target="tpu_custom_call" | custom-call | tf_op jit(solution)/shard_map/join/pallas_call | solution.py:478
  96.1 0.0 all-to-all-done.1.blocks_ref
  96.1 0.8 lay.1
  (12 shorter events, 0.1 us)
Async XLA Ops:
  0.6 21.6 %copy-start = (bf16[2,2048]{1,0:T(2,128)(2,1)S(1)}, bf16[2,2048]{1,0:T(2,128)(2,1)}, u32[]{:S(2)}) copy-start(bf16[2,2048]{1,0:T(2,128)(2,1)} %param.17) | copy-start | bytes 24580
  0.6 21.6 %copy-start.8 = (bf16[12,2048]{1,0:T(8,128)(2,1)S(1)}, bf16[12,2048]{1,0:T(8,128)(2,1)}, u32[]{:S(2)}) copy-start(bf16[12,2048]{1,0:T(8,128)(2,1)} %weight_ref.3) | copy-start | bytes 147460
  22.2 2.6 %collective-permute-start.2 = (bf16[16,80,128]{2,1,0:T(8,128)(2,1)S(1)}, bf16[16,80,128]{2,1,0:T(8,128)(2,1)S(1)}, u32[]{:S(2)}, u32[]{:S(2)}) collective-permute-start(bf16[16,80,128]{2,1,0:T(8,128)(2,1)S(1)} %all_to_all.10.got_ref.mine_ref), channel_id=1, source_target_pairs={{0,1},{1,0},{2,3},{3,2},{4,5},{5,4},{6,7},{7,6},{8,9},{9,8},{10,11... | collective-permute-start | bytes 983048 | tf_op jit(solution)/shard_map/ppermute | solution.py:620
  28.1 15.8 %copy-start.2 = (f32[128,2048]{1,0:T(8,128)}, f32[128,2048]{1,0:T(8,128)S(1)}, u32[]{:S(2)}) copy-start(f32[128,2048]{1,0:T(8,128)S(1)} %get-tuple-element.33.second_ref) | copy-start | bytes 3145732
  28.1 15.8 %copy-start.5 = (bf16[2048,128]{1,0:T(8,128)(2,1)}, bf16[2048,128]{1,0:T(8,128)(2,1)S(1)}, u32[]{:S(2)}) copy-start(bf16[2048,128]{1,0:T(8,128)(2,1)S(1)} %get-tuple-element.32.weight_ref) | copy-start | bytes 1572868
  28.1 3.8 %collective-permute-start.3 = (f32[2,2048]{1,0:T(2,128)S(1)}, f32[2,2048]{1,0:T(2,128)S(1)}, u32[]{:S(2)}, u32[]{:S(2)}) collective-permute-start(f32[2,2048]{1,0:T(2,128)S(1)} %get-tuple-element.28), channel_id=1, source_target_pairs={{0,2},{2,0},{4,6},{6,4},{8,10},{10,8},{12,14},{14,12},{16,18},{18,... | collective-permute-start | bytes 49160 | tf_op jit(solution)/shard_map/ppermute | solution.py:624
  28.7 3.7 %collective-permute-start.4 = (f32[2,2048]{1,0:T(2,128)S(1)}, f32[2,2048]{1,0:T(2,128)S(1)}, u32[]{:S(2)}, u32[]{:S(2)}) collective-permute-start(f32[2,2048]{1,0:T(2,128)S(1)} %get-tuple-element.28), channel_id=1, source_target_pairs={{0,4},{2,6},{4,0},{6,2},{8,12},{10,14},{12,8},{14,10},{16,20},{18,... | collective-permute-start | bytes 49160 | tf_op jit(solution)/shard_map/ppermute | solution.py:624
  29.5 4.6 %collective-permute-start.5 = (f32[2,2048]{1,0:T(2,128)S(1)}, f32[2,2048]{1,0:T(2,128)S(1)}, u32[]{:S(2)}, u32[]{:S(2)}) collective-permute-start(f32[2,2048]{1,0:T(2,128)S(1)} %get-tuple-element.28), channel_id=1, source_target_pairs={{0,6},{2,4},{4,2},{6,0},{8,14},{10,12},{12,10},{14,8},{16,22},{18,... | collective-permute-start | bytes 49160 | tf_op jit(solution)/shard_map/ppermute | solution.py:624
  34.1 4.7 %collective-permute-start.6 = (f32[2,2048]{1,0:T(2,128)S(1)}, f32[2,2048]{1,0:T(2,128)S(1)}, u32[]{:S(2)}, u32[]{:S(2)}) collective-permute-start(f32[2,2048]{1,0:T(2,128)S(1)} %add_add_fusion.2), channel_id=1, source_target_pairs={{0,8},{2,10},{4,12},{6,14},{8,0},{10,2},{12,4},{14,6},{16,24},{18,... | collective-permute-start | bytes 49160 | tf_op jit(solution)/shard_map/ppermute | solution.py:624
  35.9 3.7 %collective-permute-start.7 = (f32[2,2048]{1,0:T(2,128)S(1)}, f32[2,2048]{1,0:T(2,128)S(1)}, u32[]{:S(2)}, u32[]{:S(2)}) collective-permute-start(f32[2,2048]{1,0:T(2,128)S(1)} %add_add_fusion.2), channel_id=1, source_target_pairs={{0,16},{2,18},{4,20},{6,22},{8,24},{10,26},{12,28},{14,30},{16,0},... | collective-permute-start | bytes 49160 | tf_op jit(solution)/shard_map/ppermute | solution.py:624
  36.1 5.5 %collective-permute-start.8 = (f32[2,2048]{1,0:T(2,128)S(1)}, f32[2,2048]{1,0:T(2,128)S(1)}, u32[]{:S(2)}, u32[]{:S(2)}) collective-permute-start(f32[2,2048]{1,0:T(2,128)S(1)} %add_add_fusion.2), channel_id=1, source_target_pairs={{0,24},{2,26},{4,28},{6,30},{8,16},{10,18},{12,20},{14,22},{16,8},... | collective-permute-start | bytes 49160 | tf_op jit(solution)/shard_map/ppermute | solution.py:624
  43.9 37.2 %copy-start.1 = (f32[5,8,32,512]{3,2,1,0:T(8,128)S(1)}, f32[5,8,32,512]{3,2,1,0:T(8,128)}, u32[]{:S(2)}) copy-start(f32[5,8,32,512]{3,2,1,0:T(8,128)} %flow_ref.3) | copy-start | bytes 7864324
  43.9 2.0 %collective-permute-start.16 = (f32[16,64,128]{2,1,0:T(8,128)S(1)}, f32[16,64,128]{2,1,0:T(8,128)S(1)}, u32[]{:S(2)}, u32[]{:S(2)}) collective-permute-start(f32[16,64,128]{2,1,0:T(8,128)S(1)} %get-tuple-element.40), channel_id=1, source_target_pairs={{0,1},{1,0},{2,3},{3,2},{4,5},{5,4},{6,7},{7,6},{8,9},{9,8},{10,11... | collective-permute-start | bytes 1572872 | tf_op jit(solution)/shard_map/ppermute | solution.py:620
  46.7 49.4 %all-to-all-start.1 = ((f32[16,64,128]{2,1,0:T(8,128)}), f32[16,64,128]{2,1,0:T(8,128)S(1)}, u32[]{:S(2)}, u32[]{:S(2)}) async-start(f32[16,64,128]{2,1,0:T(8,128)} %add.59), calls=%async_computation.1 | async-start | bytes 1048576 | tf_op jit(solution)/shard_map/all_to_all | solution.py:643
  52.1 1.2 %copy-start.3 = (f32[128,2048]{1,0:T(8,128)S(1)}, f32[128,2048]{1,0:T(8,128)}, u32[]{:S(2)}) copy-start(f32[128,2048]{1,0:T(8,128)} %copy-done.2) | copy-start | bytes 3145732
  53.4 1.0 %copy-start.6 = (bf16[2048,128]{1,0:T(8,128)(2,1)S(1)}, bf16[2048,128]{1,0:T(8,128)(2,1)}, u32[]{:S(2)}) copy-start(bf16[2048,128]{1,0:T(8,128)(2,1)} %copy-done.5) | copy-start | bytes 1572868
  61.3 1.2 %collective-permute-start.9 = (f32[100,128]{1,0:T(8,128)S(1)}, f32[100,128]{1,0:T(8,128)S(1)}, u32[]{:S(2)}, u32[]{:S(2)}) collective-permute-start(f32[100,128]{1,0:T(8,128)S(1)} %get-tuple-element.36), channel_id=1, source_target_pairs={{0,1},{1,0},{2,3},{3,2},{4,5},{5,4},{6,7},{7,6},{8,9},{9,8},{10,11... | collective-permute-start | bytes 153608 | tf_op jit(solution)/shard_map/ppermute | solution.py:620
  62.6 4.5 %collective-permute-start.10 = (f32[100,128]{1,0:T(8,128)S(1)}, f32[100,128]{1,0:T(8,128)S(1)}, u32[]{:S(2)}, u32[]{:S(2)}) collective-permute-start(f32[100,128]{1,0:T(8,128)S(1)} %add.53), channel_id=1, source_target_pairs={{0,2},{2,0},{4,6},{6,4},{8,10},{10,8},{12,14},{14,12},{16,18},{18,... | collective-permute-start | bytes 153608 | tf_op jit(solution)/shard_map/ppermute | solution.py:624
  64.6 4.7 %collective-permute-start.11 = (f32[100,128]{1,0:T(8,128)S(1)}, f32[100,128]{1,0:T(8,128)S(1)}, u32[]{:S(2)}, u32[]{:S(2)}) collective-permute-start(f32[100,128]{1,0:T(8,128)S(1)} %add.53), channel_id=1, source_target_pairs={{0,4},{2,6},{4,0},{6,2},{8,12},{10,14},{12,8},{14,10},{16,20},{18,... | collective-permute-start | bytes 153608 | tf_op jit(solution)/shard_map/ppermute | solution.py:624
  66.0 5.0 %collective-permute-start.12 = (f32[100,128]{1,0:T(8,128)S(1)}, f32[100,128]{1,0:T(8,128)S(1)}, u32[]{:S(2)}, u32[]{:S(2)}) collective-permute-start(f32[100,128]{1,0:T(8,128)S(1)} %add.53), channel_id=1, source_target_pairs={{0,6},{2,4},{4,2},{6,0},{8,14},{10,12},{12,10},{14,8},{16,22},{18,... | collective-permute-start | bytes 153608 | tf_op jit(solution)/shard_map/ppermute | solution.py:624
  71.1 5.7 %collective-permute-start.13 = (f32[100,128]{1,0:T(8,128)S(1)}, f32[100,128]{1,0:T(8,128)S(1)}, u32[]{:S(2)}, u32[]{:S(2)}) collective-permute-start(f32[100,128]{1,0:T(8,128)S(1)} %add_add_fusion), channel_id=1, source_target_pairs={{0,8},{2,10},{4,12},{6,14},{8,0},{10,2},{12,4},{14,6},{16,24},{18,... | collective-permute-start | bytes 153608 | tf_op jit(solution)/shard_map/ppermute | solution.py:624
  76.8 4.2 %collective-permute-start.14 = (f32[100,128]{1,0:T(8,128)S(1)}, f32[100,128]{1,0:T(8,128)S(1)}, u32[]{:S(2)}, u32[]{:S(2)}) collective-permute-start(f32[100,128]{1,0:T(8,128)S(1)} %add.57), channel_id=1, source_target_pairs={{0,16},{2,18},{4,20},{6,22},{8,24},{10,26},{12,28},{14,30},{16,0},... | collective-permute-start | bytes 153608 | tf_op jit(solution)/shard_map/ppermute | solution.py:624
  81.0 5.8 %copy-start.4 = (f32[8,32,512]{2,1,0:T(8,128)S(1)}, f32[8,32,512]{2,1,0:T(8,128)}, u32[]{:S(2)}) copy-start(f32[8,32,512]{2,1,0:T(8,128)} %diff_ref.3) | copy-start | bytes 1572868
  81.0 13.9 %collective-permute-start.15 = (f32[100,128]{1,0:T(8,128)S(1)}, f32[100,128]{1,0:T(8,128)S(1)}, u32[]{:S(2)}, u32[]{:S(2)}) collective-permute-start(f32[100,128]{1,0:T(8,128)S(1)} %add.58.half_ref), channel_id=1, source_target_pairs={{0,1},{1,0},{2,3},{3,2},{4,5},{5,4},{6,7},{7,6},{8,9},{9,8},{10,11... | collective-permute-start | bytes 153608 | tf_op jit(solution)/shard_map/ppermute | solution.py:620
  81.4 11.1 %collective-permute-start = (bf16[5,8,512]{2,1,0:T(8,128)(2,1)S(1)}, bf16[5,8,512]{2,1,0:T(8,128)(2,1)S(1)}, u32[]{:S(2)}, u32[]{:S(2)}) collective-permute-start(bf16[5,8,512]{2,1,0:T(8,128)(2,1)S(1)} %get-tuple-element.23), channel_id=1, source_target_pairs={{0,1},{1,2},{2,3},{3,4},{4,5},{5,6},{6,7},{7,8},{8,9},{9,10},{10,1... | collective-permute-start | bytes 122888 | tf_op jit(solution)/shard_map/ppermute | solution.py:687
  82.0 8.6 %copy-start.7 = (f32[2,32,512]{2,1,0:T(8,128)S(1)}, f32[2,32,512]{2,1,0:T(8,128)}, u32[]{:S(2)}) copy-start(f32[2,32,512]{2,1,0:T(8,128)} %stress_ref.1) | copy-start | bytes 393220
  82.0 10.6 %collective-permute-start.1 = (bf16[5,8,512]{2,1,0:T(8,128)(2,1)S(1)}, bf16[5,8,512]{2,1,0:T(8,128)(2,1)S(1)}, u32[]{:S(2)}, u32[]{:S(2)}) collective-permute-start(bf16[5,8,512]{2,1,0:T(8,128)(2,1)S(1)} %get-tuple-element.24), channel_id=1, source_target_pairs={{1,0},{2,1},{3,2},{4,3},{5,4},{6,5},{7,6},{8,7},{9,8},{10,9},{11,1... | collective-permute-start | bytes 122888 | tf_op jit(solution)/shard_map/ppermute | solution.py:688
